TPU v7x, 32 devices: a whole 2x2x4 slice. The times are simulated.
32 devices in a mesh: groups: 2 (over y), gx: 16 (over z, x, core).
Axes of the slice: x: 2, y: 2, z: 4, core: 2. Of those that a mesh axis runs over, the one named last changes fastest.
Arguments:
- volume: bfloat16 [64, 16, 16, 512], P(None, 'gx', 'groups'), parts along dimension 2, may hold values from -6 to 6
- weights: bfloat16 [4, 4, 4, 64, 32], replicated, may hold values from -0.25 to 0.25
- cotangent: bfloat16 [32, 32, 32, 1024], P(None, 'gx', 'groups'), parts along dimension 2, may hold values from -6 to 6
Outputs:
- upsampled: bfloat16 [32, 32, 32, 1024], P(None, 'gx', 'groups'), parts along dimension 2
- volume_grad: bfloat16 [64, 16, 16, 512], P(None, 'gx', 'groups'), parts along dimension 2
- weight_grad: float32 [8, 4, 4, 64, 32], P('groups'), parts along dimension 0
There are 2 independent parts, one for each index of `groups`. A program takes and returns all parts, laid end to end along the dimension named above; an argument that names none is the same for every part. Nothing has to cross between parts.
All inputs are finite; a program needn't handle non-finite values.
Results may differ from a plain program's by a relative error of at most 0.001.
Values may be sent and summed in bfloat16 or wider, within the bound.
No kernel may reach another device: no remote copies, remote signals or barrier semaphores. Data moves between devices by JAX's collectives and lax.ppermute only.
A program may use at most 128 MiB of HBM per device.

v0:
```python
import functools
import math

import jax
import jax.numpy as jnp
from jax import lax
from jax.experimental import pallas as pl
from jax.experimental.pallas import tpu as pltpu
from jax.sharding import PartitionSpec as P

F32 = jnp.float32
BF16 = jnp.bfloat16
NT = (((1,), (1,)), ((), ()))


def roles(core):
    inner = (1 - core, 2 - core, 3 * core)
    outer = (core, 1 + core, 3 - 3 * core)
    return inner, outer


def dot(a, b):
    return jnp.dot(a, b, preferred_element_type=F32)


def split_table():
    row = lax.broadcasted_iota(jnp.int32, (256, 256), 0)
    col = lax.broadcasted_iota(jnp.int32, (256, 256), 1)
    return (row == jnp.where(col < 128, 2 * col, 2 * col - 255)).astype(BF16)


def join_table():
    row = lax.broadcasted_iota(jnp.int32, (256, 256), 0)
    col = lax.broadcasted_iota(jnp.int32, (256, 256), 1)
    return (col == jnp.where(row < 128, 2 * row, 2 * row - 255)).astype(BF16)


def load_rows(ref, start, count, stride):
    return jnp.concatenate([ref[b, pl.ds(start, count, stride=stride), :] for b in range(ref.shape[0])], 1)


def store_rows(ref, start, stride, value):
    for b in range(ref.shape[0]):
        ref[b, pl.ds(start, value.shape[0], stride=stride), :] = value[:, 128 * b : 128 * b + 128]


def rows_by_y(source_ref, wide_ref, target_ref, ny):
    chans = source_ref.shape[0] // ny
    for b in range(wide_ref.shape[0]):
        wide_ref[b] = source_ref[:, 128 * b : 128 * b + 128].astype(F32)
    for y in range(ny):
        target_ref[y * chans : (y + 1) * chans, :] = load_rows(wide_ref, y, chans, ny).astype(BF16)


def tap_rows(cot_ref, side, table, even_ref, odd_ref, taps_ref):
    dout, _, ny2, nz2 = cot_ref.shape
    nz = nz2 // 2
    for b in range(nz2 // 256):
        block = cot_ref[:, side, :, 256 * b : 256 * b + 256].reshape(dout * ny2, 256)
        halves = dot(block, table)
        even_ref[b] = halves[:, :128]
        odd_ref[b] = halves[:, 128:]

    def row(y, carry):
        even = load_rows(even_ref, y, dout, ny2)
        odd = load_rows(odd_ref, y, dout, ny2)
        base = pl.multiple_of((y + 1) * 4 * dout, 4 * dout)
        pieces = (pltpu.roll(odd, 1, 1), even, odd, pltpu.roll(even, nz - 1, 1))
        for k, piece in enumerate(pieces):
            taps_ref[pl.ds(base + k * dout, dout), :] = piece.astype(BF16)
        return carry

    lax.fori_loop(0, ny2, row, 0, unroll=2)
    group = 4 * dout
    taps_ref[:group, :] = taps_ref[ny2 * group : (ny2 + 1) * group, :]
    taps_ref[(ny2 + 1) * group :, :] = taps_ref[group : 2 * group, :]


def first_kernel(
    core_ref, own_ref, inner_ref, cot_ref, w_ref,
    taps_out_ref, own_t_ref, inner_t_ref, wg_ref, vg_ref, to_inner_ref, to_outer_ref,
    wide_ref, even_ref, odd_ref, taps_in_ref,
):
    dout, _, ny2, _ = cot_ref.shape
    ny = ny2 // 2
    chans = w_ref.shape[2]
    group = 4 * dout
    (side_i, own_i, nbr_i), (side_o, own_o, nbr_o) = roles(core_ref[0])
    table = split_table()

    def grad_weights(own, nbr):
        both = jnp.concatenate([w_ref[own].astype(F32), w_ref[nbr].astype(F32)], 1)
        return both.T.astype(BF16)

    tap_rows(cot_ref, side_o, table, even_ref, odd_ref, taps_out_ref)
    weights_o = grad_weights(own_o, nbr_o)

    def outer_row(y, carry):
        taps = taps_out_ref[pl.ds(pl.multiple_of(y * 2 * group, 2 * group), 4 * group), :]
        sums = dot(weights_o, taps)
        store_rows(vg_ref, y, ny, sums[:chans])
        store_rows(to_outer_ref, y, ny, sums[chans:])
        return carry

    lax.fori_loop(0, ny, outer_row, 0)
    rows_by_y(own_ref, wide_ref, own_t_ref, ny)
    rows_by_y(inner_ref, wide_ref, inner_t_ref, ny)
    tap_rows(cot_ref, side_i, table, even_ref, odd_ref, taps_in_ref)
    weights_i = grad_weights(own_i, nbr_i)
    wg_ref[...] = jnp.zeros_like(wg_ref)

    def inner_row(y, carry):
        taps = taps_in_ref[pl.ds(pl.multiple_of(y * 2 * group, 2 * group), 4 * group), :]
        sums = dot(weights_i, taps)
        store_rows(vg_ref, y, ny, load_rows(vg_ref, y, chans, ny) + sums[:chans])
        store_rows(to_inner_ref, y, ny, sums[chans:])
        at = pl.ds(pl.multiple_of(y * chans, chans), chans)
        cells = jnp.concatenate([own_t_ref[at, :], inner_t_ref[at, :]], 0)
        wg_ref[...] += lax.dot_general(taps, cells, NT, preferred_element_type=F32)
        return carry

    lax.fori_loop(0, ny, inner_row, 0)


def second_kernel(taps_ref, own_t_ref, outer_ref, arrived_ref, sum_ref, outer_t_ref, wide_ref):
    chans = arrived_ref.shape[1] // 2
    ny = outer_ref.shape[0] // chans
    rows = sum_ref.shape[0]
    rows_by_y(outer_ref, wide_ref, outer_t_ref, ny)
    sum_ref[...] = arrived_ref[...]

    def row(y, carry):
        taps = taps_ref[pl.ds(pl.multiple_of(y * rows // 2, rows // 2), rows), :]
        at = pl.ds(pl.multiple_of(y * chans, chans), chans)
        cells = jnp.concatenate([own_t_ref[at, :], outer_t_ref[at, :]], 0)
        sum_ref[...] += lax.dot_general(taps, cells, NT, preferred_element_type=F32)
        return carry

    lax.fori_loop(0, ny, row, 0)


def fine_kernel(core_ref, own_t_ref, inner_t_ref, outer_t_ref, w_ref, out_ref, even_ref, odd_ref):
    dout, _, ny2, nz2 = out_ref.shape
    ny, nz = ny2 // 2, nz2 // 2
    chans = w_ref.shape[2]
    group = 4 * dout
    table = join_table()
    for (side, own, nbr), nbr_t_ref in zip(roles(core_ref[0]), (inner_t_ref, outer_t_ref)):
        weights = []
        for near, far in ((1, 3), (2, 0)):
            slabs = [w_ref[x, y * group : (y + 1) * group, :] for x in (own, nbr) for y in (near, far)]
            weights.append(jnp.concatenate(slabs, 1))

        def row(y, carry):
            for phase, step in ((0, ny - 1), (1, 1)):
                near = pl.ds(pl.multiple_of(y * chans, chans), chans)
                far = pl.ds(pl.multiple_of(lax.rem(y + step, ny) * chans, chans), chans)
                cells = jnp.concatenate(
                    [own_t_ref[near, :], own_t_ref[far, :], nbr_t_ref[near, :], nbr_t_ref[far, :]], 0
                )
                sums = dot(weights[phase], cells)
                even = sums[dout : 2 * dout] + pltpu.roll(sums[3 * dout :], 1, 1)
                odd = sums[2 * dout : 3 * dout] + pltpu.roll(sums[:dout], nz - 1, 1)
                store_rows(even_ref, 2 * y + phase, ny2, even)
                store_rows(odd_ref, 2 * y + phase, ny2, odd)
            return carry

        lax.fori_loop(0, ny, row, 0)
        for b in range(nz // 128):
            halves = jnp.concatenate([even_ref[b].astype(BF16), odd_ref[b].astype(BF16)], 1)
            fine = dot(halves, table).astype(BF16)
            out_ref[:, side, :, 256 * b : 256 * b + 256] = fine.reshape(dout, ny2, 256)


def last_kernel(a_ref, b_ref, c_ref, out_ref):
    for b in range(a_ref.shape[0]):
        out_ref[:, 128 * b : 128 * b + 128] = (a_ref[b] + b_ref[b] + c_ref[b]).astype(BF16)


def call(kernel, outs, scratch, in_smem, flops, moved):
    vmem = pl.BlockSpec(memory_space=pltpu.VMEM)
    smem = pl.BlockSpec(memory_space=pltpu.SMEM)
    return pl.pallas_call(
        kernel,
        out_shape=outs,
        in_specs=[smem if s else vmem for s in in_smem],
        out_specs=[vmem] * len(outs),
        scratch_shapes=scratch,
        compiler_params=pltpu.CompilerParams(vmem_limit_bytes=40 << 20),
        cost_estimate=pl.CostEstimate(flops=flops, bytes_accessed=moved, transcendentals=0),
    )


def on_device(volume, weights, cotangent):
    chans, planes, ny, nz = volume.shape
    dout = cotangent.shape[0]
    peers = lax.axis_size("gx")
    me = lax.axis_index("gx")
    core = lax.rem(me, 2)
    core_arg = core.astype(jnp.int32).reshape(1)
    inner_pairs = [(i, i ^ 1) for i in range(peers)]
    outer_pairs = [(i, (i + (1 if i % 2 else -1)) % peers) for i in range(peers)]

    own = volume.reshape(chans * ny, nz)
    outer = lax.ppermute(own, "gx", outer_pairs)
    inner = lax.ppermute(own, "gx", inner_pairs)
    kernels = jnp.transpose(weights, (0, 1, 2, 4, 3)).reshape(4, 16 * dout, chans)

    rows, wide = chans * ny, 16 * dout
    group = 4 * dout
    struct = jax.ShapeDtypeStruct
    blocks_c, blocks_d = (nz // 128, rows, 128), (nz // 128, dout * 2 * ny, 128)
    taps_o, own_t, inner_t, wg_i, vg, to_inner, to_outer = call(
        first_kernel,
        [struct(((2 * ny + 2) * group, nz), BF16), struct((rows, nz), BF16), struct((rows, nz), BF16),
         struct((wide, 2 * chans), F32), struct(blocks_c, F32), struct(blocks_c, F32), struct(blocks_c, F32)],
        [pltpu.VMEM(blocks_c, F32), pltpu.VMEM(blocks_d, F32), pltpu.VMEM(blocks_d, F32),
         pltpu.VMEM(((2 * ny + 2) * group, nz), BF16)],
        (1, 0, 0, 0, 0), 6_000_000_000, 12_000_000,
    )(core_arg, own, inner, cotangent, kernels)

    from_outer = lax.ppermute(to_outer, "gx", outer_pairs)
    from_inner = lax.ppermute(to_inner, "gx", inner_pairs)
    wg_arrived = lax.ppermute(wg_i, "gx", inner_pairs)

    total, outer_t = call(
        second_kernel,
        [struct((wide, 2 * chans), F32), struct((rows, nz), BF16)],
        [pltpu.VMEM(blocks_c, F32)],
        (0, 0, 0, 0), 1_000_000_000, 4_000_000,
    )(taps_o, own_t, outer, wg_arrived)

    (upsampled,) = call(
        fine_kernel,
        [struct(cotangent.shape, BF16)],
        [pltpu.VMEM(blocks_d, F32), pltpu.VMEM(blocks_d, F32)],
        (1, 0, 0, 0, 0), 4_000_000_000, 4_000_000,
    )(core_arg, own_t, inner_t, outer_t, kernels)

    total = sum_over_chips(total, me, peers)
    other = lax.ppermute(total, "gx", inner_pairs)
    scale = 1.0 / math.sqrt(peers * planes * ny * nz)
    mine_own, mine_nbr = total[:, :chans], total[:, chans:]
    other_own, other_nbr = other[:, :chans], other[:, chans:]
    first = core == 0
    blocks = jnp.stack(
        [
            jnp.where(first, other_nbr, mine_nbr),
            jnp.where(first, mine_own, other_own),
            jnp.where(first, other_own, mine_own),
            jnp.where(first, mine_nbr, other_nbr),
        ]
    )
    weight_grad = jnp.transpose((blocks * scale).reshape(4, 4, 4, dout, chans), (0, 1, 2, 4, 3))
    (volume_grad,) = call(last_kernel, [struct((rows, nz), BF16)], [], (0, 0, 0), 600_000, 4_000_000)(
        vg, from_inner, from_outer
    )
    volume_grad = volume_grad.reshape(volume.shape)
    return (upsampled, volume_grad, weight_grad)


def sum_over_chips(total, me, peers):
    if peers & (peers - 1) or peers < 4:
        groups = [[i for i in range(peers) if i % 2 == c] for c in range(2)]
        return lax.psum(total, "gx", axis_index_groups=groups)
    half = total.shape[0] // 2
    bit = lax.rem(me // 2, 2)
    pairs = lambda k: [(i, i ^ k) for i in range(peers)]
    mine = lax.dynamic_slice_in_dim(total, bit * half, half, 0)
    away = lax.dynamic_slice_in_dim(total, (1 - bit) * half, half, 0)
    mine = mine + lax.ppermute(away, "gx", pairs(2))
    step = 4
    while step < peers:
        mine = mine + lax.ppermute(mine, "gx", pairs(step))
        step *= 2
    away = lax.ppermute(mine, "gx", pairs(2))
    return jnp.where(bit == 0, jnp.concatenate([mine, away]), jnp.concatenate([away, mine]))


def solution(mesh):
    placed = (P(None, "gx", "groups", None), P(), P(None, "gx", "groups", None))
    return jax.shard_map(
        on_device,
        mesh=mesh,
        in_specs=placed,
        out_specs=(
            P(None, "gx", "groups", None),
            P(None, "gx", "groups", None),
            P("groups", None, None, None, None),
        ),
        check_vma=False,
    )
```

profile of v0, /device:TPU:0, one launch (start us, length us, event | category | flops | bytes accessed | tf_op | source)
XLA Modules:
  0.0 86.6 jit_solution(11195739189606200636)
XLA Ops:
  1.1 5.6 %collective-permute-start.1 = (bf16[512,512]{1,0:T(8,128)(2,1)}, bf16[512,512]{1,0:T(8,128)(2,1)S(1)}, u32[]{:S(2)}, u32[]{:S(2)}) collective-permute-start(bf16[512,512]{1,0:T(8,128)(2,1)} %bitcast.15), channel_id=1, source_target_pairs={{0,15},{1,2},{2,1},{3,4},{4,3},{5,6},{6,5},{7,8},{8,7},{9,10},{10,... | collective-permute-start | bytes 1572872 | tf_op jit(solution)/shard_map/ppermute | solution.py:205
  6.8 1.6 %copy-done = bf16[32,2,16,1024]{3,2,1,0:T(8,128)(2,1)S(1)} copy-done((bf16[32,2,16,1024]{3,2,1,0:T(8,128)(2,1)S(1)}, bf16[32,2,16,1024]{3,2,1,0:T(8,128)(2,1)}, u32[]{:S(2)}) %copy-start) | copy-done | bytes 2097176
  8.4 1.0 %copy-done.2 = bf16[64,1,8,512]{3,2,1,0:T(8,128)(2,1)S(1)} copy-done((bf16[64,1,8,512]{3,2,1,0:T(8,128)(2,1)S(1)}, bf16[64,1,8,512]{3,2,1,0:T(8,128)(2,1)}, u32[]{:S(2)}) %copy-start.2) | copy-done | bytes 524312
  9.4 1.0 %copy-done.3 = bf16[4,4,4,64,32]{3,4,2,1,0:T(8,128)(2,1)S(1)} copy-done((bf16[4,4,4,64,32]{3,4,2,1,0:T(8,128)(2,1)S(1)}, bf16[4,4,4,64,32]{3,4,2,1,0:T(8,128)(2,1)}, u32[]{:S(2)}) %copy-start.3) | copy-done | bytes 262168
  10.5 11.2 %shard_map.58 = (bf16[2304,512]{1,0:T(8,128)(2,1)S(1)}, bf16[512,512]{1,0:T(8,128)(2,1)S(1)}, bf16[512,512]{1,0:T(8,128)(2,1)S(1)}, f32[512,128]{1,0:T(8,128)S(1...) custom-call(s32[1]{0:T(128)} %bitcast.core_ref, bf16[512,512]{1,0:T(8,128)(2,1)S(1)} %bitcast.16, ...), custom_call_target="tpu_custom_call" | custom-call | flops 6000000000 | bytes 12000000 | tf_op jit(solution)/shard_map/pallas_call | solution.py:213
  21.7 1.0 %copy-done.1 = f32[4,512,128]{2,1,0:T(8,128)} copy-done((f32[4,512,128]{2,1,0:T(8,128)}, f32[4,512,128]{2,1,0:T(8,128)S(1)}, u32[]{:S(2)}) %copy-start.1) | copy-done | bytes 1048600
  22.7 1.4 %copy-done.5 = bf16[2304,512]{1,0:T(8,128)(2,1)} copy-done((bf16[2304,512]{1,0:T(8,128)(2,1)}, bf16[2304,512]{1,0:T(8,128)(2,1)S(1)}, u32[]{:S(2)}) %copy-start.5) | copy-done | bytes 2359320
  24.1 0.8 copy-done.11
  24.9 1.5 %collective-permute-done.2.arrived_ref = f32[512,128]{1,0:T(8,128)S(1)} collective-permute-done((f32[512,128]{1,0:T(8,128)S(1)}, f32[512,128]{1,0:T(8,128)S(1)}, u32[]{:S(2)}, u32[]{:S(2)}) %collective-permute-start.2) | collective-permute-done | bytes 262176 | tf_op jit(solution)/shard_map/ppermute | solution.py:224
  26.4 1.7 %copy-done.6 = bf16[2304,512]{1,0:T(8,128)(2,1)S(1)} copy-done((bf16[2304,512]{1,0:T(8,128)(2,1)S(1)}, bf16[2304,512]{1,0:T(8,128)(2,1)}, u32[]{:S(2)}) %copy-start.6) | copy-done | bytes 2359320
  28.1 2.6 %shard_map.59 = (f32[512,128]{1,0:T(8,128)S(1)}, bf16[512,512]{1,0:T(8,128)(2,1)S(1)}) custom-call(bf16[2304,512]{1,0:T(8,128)(2,1)S(1)} %copy-done.6, bf16[512,512]{1,0:T(8,128)(2,1)S(1)} %get-tuple-element.12.own_t_ref, bf16[512,512]{1,0:T(8,128)(2,1)S(1)} %collective-permute-done.1.outer_ref, f32[512,128]{1,0:T(8,128)S(1)} %collective-permute-done.2.arrived_ref), custom_call_target="tpu_custom_call" | custom-call | flops 1000000000 | bytes 4000000 | tf_op jit(solution)/shard_map/pallas_call | solution.py:226
  31.6 5.5 %collective-permute-done.5 = f32[256,128]{1,0:T(8,128)S(1)} collective-permute-done((f32[256,128]{1,0:T(8,128)S(1)}, f32[256,128]{1,0:T(8,128)S(1)}, u32[]{:S(2)}, u32[]{:S(2)}) %collective-permute-start.5) | collective-permute-done | bytes 131104 | tf_op jit(solution)/shard_map/ppermute | solution.py:271
  37.3 5.0 %collective-permute-done.6 = f32[256,128]{1,0:T(8,128)S(1)} collective-permute-done((f32[256,128]{1,0:T(8,128)S(1)}, f32[256,128]{1,0:T(8,128)S(1)}, u32[]{:S(2)}, u32[]{:S(2)}) %collective-permute-start.6) | collective-permute-done | bytes 131104 | tf_op jit(solution)/shard_map/ppermute | solution.py:274
  42.4 2.5 %collective-permute-start.4 = (f32[4,512,128]{2,1,0:T(8,128)}, f32[4,512,128]{2,1,0:T(8,128)S(1)}, u32[]{:S(2)}, u32[]{:S(2)}) collective-permute-start(f32[4,512,128]{2,1,0:T(8,128)} %copy-done.1), channel_id=1, source_target_pairs={{0,15},{1,2},{2,1},{3,4},{4,3},{5,6},{6,5},{7,8},{8,7},{9,10},{10,... | collective-permute-start | bytes 3145736 | tf_op jit(solution)/shard_map/ppermute | solution.py:222
  44.9 4.5 %collective-permute-done.7 = f32[256,128]{1,0:T(8,128)S(1)} collective-permute-done((f32[256,128]{1,0:T(8,128)S(1)}, f32[256,128]{1,0:T(8,128)S(1)}, u32[]{:S(2)}, u32[]{:S(2)}) %collective-permute-start.7) | collective-permute-done | bytes 131104 | tf_op jit(solution)/shard_map/ppermute | solution.py:274
  49.4 12.1 %collective-permute-start.8 = (f32[256,128]{1,0:T(8,128)S(1)}, f32[256,128]{1,0:T(8,128)S(1)}, u32[]{:S(2)}, u32[]{:S(2)}) collective-permute-start(f32[256,128]{1,0:T(8,128)S(1)} %add.20), channel_id=1, source_target_pairs={{0,2},{1,3},{2,0},{3,1},{4,6},{5,7},{6,4},{7,5},{8,10},{9,11},{10,... | collective-permute-start | bytes 393224 | tf_op jit(solution)/shard_map/ppermute | solution.py:276
  61.6 10.0 %collective-permute-done.8 = f32[256,128]{1,0:T(8,128)S(1)} collective-permute-done((f32[256,128]{1,0:T(8,128)S(1)}, f32[256,128]{1,0:T(8,128)S(1)}, u32[]{:S(2)}, u32[]{:S(2)}) %collective-permute-start.8) | collective-permute-done | bytes 131104 | tf_op jit(solution)/shard_map/ppermute | solution.py:276
  71.7 1.0 %copy-done.4 = bf16[4,4,4,64,32]{3,4,2,1,0:T(8,128)(2,1)S(1)} copy-done((bf16[4,4,4,64,32]{3,4,2,1,0:T(8,128)(2,1)S(1)}, bf16[4,4,4,64,32]{3,4,2,1,0:T(8,128)(2,1)}, u32[]{:S(2)}) %copy-start.4) | copy-done | bytes 262168
  72.7 1.0 %copy-done.8 = bf16[512,512]{1,0:T(8,128)(2,1)S(1)} copy-done((bf16[512,512]{1,0:T(8,128)(2,1)S(1)}, bf16[512,512]{1,0:T(8,128)(2,1)}, u32[]{:S(2)}) %copy-start.8) | copy-done | bytes 524312
  73.8 1.0 %copy-done.10 = bf16[512,512]{1,0:T(8,128)(2,1)S(1)} copy-done((bf16[512,512]{1,0:T(8,128)(2,1)S(1)}, bf16[512,512]{1,0:T(8,128)(2,1)}, u32[]{:S(2)}) %copy-start.10) | copy-done | bytes 524312
  74.8 1.0 %copy-done.12 = bf16[512,512]{1,0:T(8,128)(2,1)S(1)} copy-done((bf16[512,512]{1,0:T(8,128)(2,1)S(1)}, bf16[512,512]{1,0:T(8,128)(2,1)}, u32[]{:S(2)}) %copy-start.12) | copy-done | bytes 524312
  75.8 8.5 %shard_map.60 = bf16[32,2,16,1024]{3,2,1,0:T(8,128)(2,1)} custom-call(s32[1]{0:T(128)} %bitcast.core_ref, bf16[512,512]{1,0:T(8,128)(2,1)S(1)} %copy-done.8, bf16[512,512]{1,0:T(8,128)(2,1)S(1)} %copy-done.12, bf16[512,512]{1,0:T(8,128)(2,1)S(1)} %copy-done.10, bf16[4,512,64]{2,1,0:T(8,128)(2,1)S(1)} %bitcast.18), custom_call_target="tpu_custom_call" | custom-call | flops 4000000000 | bytes 4000000 | tf_op jit(solution)/shard_map/pallas_call | solution.py:233
  84.6 1.1 %fusion = f32[4,4,4,64,32]{3,4,2,1,0:T(8,128)} fusion(f32[1,4,4,32,64]{4,3,2,1,0:T(8,128)S(1)} %bitcast.20, f32[1,4,4,32,64]{4,3,2,1,0:T(8,128)S(1)} %bitcast.21, f32[1,4,4,32,64]{4,3,2,1,0:T(8,128)S(1)} %bitcast.22, f32[1,4,4,32,64]{4,3,2,1,0:T(8,128)S(1)} %bitcast.19), kind=kLoop, calls=%fused_computation.1 | loop fusion | flops 524288 | bytes 1048576 | tf_op jit(solution)/shard_map/transpose | solution.py:254
  85.7 0.9 %shard_map.61 = bf16[512,512]{1,0:T(8,128)(2,1)} custom-call(f32[4,512,128]{2,1,0:T(8,128)S(1)} %get-tuple-element.17.a_ref, f32[4,512,128]{2,1,0:T(8,128)S(1)} %collective-permute-done.3.b_ref, f32[4,512,128]{2,1,0:T(8,128)S(1)} %collective-permute-done.4.c_ref), custom_call_target="tpu_custom_call" | custom-call | flops 600000 | bytes 4000000 | tf_op jit(solution)/shard_map/pallas_call | solution.py:255
  (33 shorter events, 2.0 us)
Async XLA Ops:
  0.6 6.2 %collective-permute-start = (bf16[512,512]{1,0:T(8,128)(2,1)}, bf16[512,512]{1,0:T(8,128)(2,1)S(1)}, u32[]{:S(2)}, u32[]{:S(2)}) collective-permute-start(bf16[512,512]{1,0:T(8,128)(2,1)} %bitcast.14), channel_id=1, source_target_pairs={{0,1},{1,0},{2,3},{3,2},{4,5},{5,4},{6,7},{7,6},{8,9},{9,8},{10,11... | collective-permute-start | bytes 1572872 | tf_op jit(solution)/shard_map/ppermute | solution.py:206
  1.1 23.8 %collective-permute-start.1 = (bf16[512,512]{1,0:T(8,128)(2,1)}, bf16[512,512]{1,0:T(8,128)(2,1)S(1)}, u32[]{:S(2)}, u32[]{:S(2)}) collective-permute-start(bf16[512,512]{1,0:T(8,128)(2,1)} %bitcast.15), channel_id=1, source_target_pairs={{0,15},{1,2},{2,1},{3,4},{4,3},{5,6},{6,5},{7,8},{8,7},{9,10},{10,... | collective-permute-start | bytes 1572872 | tf_op jit(solution)/shard_map/ppermute | solution.py:205
  6.8 1.6 %copy-start = (bf16[32,2,16,1024]{3,2,1,0:T(8,128)(2,1)S(1)}, bf16[32,2,16,1024]{3,2,1,0:T(8,128)(2,1)}, u32[]{:S(2)}) copy-start(bf16[32,2,16,1024]{3,2,1,0:T(8,128)(2,1)} %cot_ref.1) | copy-start | bytes 6291460
  8.4 1.0 %copy-start.2 = (bf16[64,1,8,512]{3,2,1,0:T(8,128)(2,1)S(1)}, bf16[64,1,8,512]{3,2,1,0:T(8,128)(2,1)}, u32[]{:S(2)}) copy-start(bf16[64,1,8,512]{3,2,1,0:T(8,128)(2,1)} %param.3) | copy-start | bytes 1572868
  9.4 1.0 %copy-start.3 = (bf16[4,4,4,64,32]{3,4,2,1,0:T(8,128)(2,1)S(1)}, bf16[4,4,4,64,32]{3,4,2,1,0:T(8,128)(2,1)}, u32[]{:S(2)}) copy-start(bf16[4,4,4,64,32]{3,4,2,1,0:T(8,128)(2,1)} %param.4) | copy-start | bytes 786436
  21.7 1.0 %copy-start.1 = (f32[4,512,128]{2,1,0:T(8,128)}, f32[4,512,128]{2,1,0:T(8,128)S(1)}, u32[]{:S(2)}) copy-start(f32[4,512,128]{2,1,0:T(8,128)S(1)} %get-tuple-element.19) | copy-start | bytes 3145732
  22.7 1.4 %copy-start.5 = (bf16[2304,512]{1,0:T(8,128)(2,1)}, bf16[2304,512]{1,0:T(8,128)(2,1)S(1)}, u32[]{:S(2)}) copy-start(bf16[2304,512]{1,0:T(8,128)(2,1)S(1)} %get-tuple-element.14.taps_ref) | copy-start | bytes 7077892
  24.1 0.8 copy-start.11
  24.9 12.3 %copy-start.7 = (bf16[512,512]{1,0:T(8,128)(2,1)}, bf16[512,512]{1,0:T(8,128)(2,1)S(1)}, u32[]{:S(2)}) copy-start(bf16[512,512]{1,0:T(8,128)(2,1)S(1)} %get-tuple-element.12.own_t_ref) | copy-start | bytes 1572868
  24.9 1.5 %collective-permute-start.2 = (f32[512,128]{1,0:T(8,128)S(1)}, f32[512,128]{1,0:T(8,128)S(1)}, u32[]{:S(2)}, u32[]{:S(2)}) collective-permute-start(f32[512,128]{1,0:T(8,128)S(1)} %get-tuple-element.15), channel_id=1, source_target_pairs={{0,1},{1,0},{2,3},{3,2},{4,5},{5,4},{6,7},{7,6},{8,9},{9,8},{10,11... | collective-permute-start | bytes 786440 | tf_op jit(solution)/shard_map/ppermute | solution.py:224
  26.4 1.7 %copy-start.6 = (bf16[2304,512]{1,0:T(8,128)(2,1)S(1)}, bf16[2304,512]{1,0:T(8,128)(2,1)}, u32[]{:S(2)}) copy-start(bf16[2304,512]{1,0:T(8,128)(2,1)} %copy-done.5) | copy-start | bytes 7077892
  30.7 0.8 copy-start.9
  31.6 5.6 %collective-permute-start.5 = (f32[256,128]{1,0:T(8,128)S(1)}, f32[256,128]{1,0:T(8,128)S(1)}, u32[]{:S(2)}, u32[]{:S(2)}) collective-permute-start(f32[256,128]{1,0:T(8,128)S(1)} %constant_dynamic-slice_fusion), channel_id=1, source_target_pairs={{0,2},{1,3},{2,0},{3,1},{4,6},{5,7},{6,4},{7,5},{8,10},{9,11},{10,... | collective-permute-start | bytes 393224 | tf_op jit(solution)/shard_map/ppermute | solution.py:271
  37.2 5.0 %collective-permute-start.6 = (f32[256,128]{1,0:T(8,128)S(1)}, f32[256,128]{1,0:T(8,128)S(1)}, u32[]{:S(2)}, u32[]{:S(2)}) collective-permute-start(f32[256,128]{1,0:T(8,128)S(1)} %dynamic-slice_add_fusion), channel_id=1, source_target_pairs={{0,4},{1,5},{2,6},{3,7},{4,0},{5,1},{6,2},{7,3},{8,12},{9,13},{10,... | collective-permute-start | bytes 393224 | tf_op jit(solution)/shard_map/ppermute | solution.py:274
  42.2 7.2 %collective-permute-start.7 = (f32[256,128]{1,0:T(8,128)S(1)}, f32[256,128]{1,0:T(8,128)S(1)}, u32[]{:S(2)}, u32[]{:S(2)}) collective-permute-start(f32[256,128]{1,0:T(8,128)S(1)} %add.19), channel_id=1, source_target_pairs={{0,8},{1,9},{2,10},{3,11},{4,12},{5,13},{6,14},{7,15},{8,0},{9,1},... | collective-permute-start | bytes 393224 | tf_op jit(solution)/shard_map/ppermute | solution.py:274
  42.4 43.3 %collective-permute-start.3 = (f32[4,512,128]{2,1,0:T(8,128)}, f32[4,512,128]{2,1,0:T(8,128)S(1)}, u32[]{:S(2)}, u32[]{:S(2)}) collective-permute-start(f32[4,512,128]{2,1,0:T(8,128)} %get-tuple-element.18), channel_id=1, source_target_pairs={{0,1},{1,0},{2,3},{3,2},{4,5},{5,4},{6,7},{7,6},{8,9},{9,8},{10,11... | collective-permute-start | bytes 3145736 | tf_op jit(solution)/shard_map/ppermute | solution.py:223
  42.4 43.3 %collective-permute-start.4 = (f32[4,512,128]{2,1,0:T(8,128)}, f32[4,512,128]{2,1,0:T(8,128)S(1)}, u32[]{:S(2)}, u32[]{:S(2)}) collective-permute-start(f32[4,512,128]{2,1,0:T(8,128)} %copy-done.1), channel_id=1, source_target_pairs={{0,15},{1,2},{2,1},{3,4},{4,3},{5,6},{6,5},{7,8},{8,7},{9,10},{10,... | collective-permute-start | bytes 3145736 | tf_op jit(solution)/shard_map/ppermute | solution.py:222
  49.4 22.1 %collective-permute-start.8 = (f32[256,128]{1,0:T(8,128)S(1)}, f32[256,128]{1,0:T(8,128)S(1)}, u32[]{:S(2)}, u32[]{:S(2)}) collective-permute-start(f32[256,128]{1,0:T(8,128)S(1)} %add.20), channel_id=1, source_target_pairs={{0,2},{1,3},{2,0},{3,1},{4,6},{5,7},{6,4},{7,5},{8,10},{9,11},{10,... | collective-permute-start | bytes 393224 | tf_op jit(solution)/shard_map/ppermute | solution.py:276
  71.6 12.8 %collective-permute-start.9 = (f32[512,128]{1,0:T(8,128)S(1)}, f32[512,128]{1,0:T(8,128)S(1)}, u32[]{:S(2)}, u32[]{:S(2)}) collective-permute-start(f32[512,128]{1,0:T(8,128)S(1)} %maximum_select_fusion), channel_id=1, source_target_pairs={{0,1},{1,0},{2,3},{3,2},{4,5},{5,4},{6,7},{7,6},{8,9},{9,8},{10,11... | collective-permute-start | bytes 786440 | tf_op jit(solution)/shard_map/ppermute | solution.py:241
  71.7 1.0 %copy-start.4 = (bf16[4,4,4,64,32]{3,4,2,1,0:T(8,128)(2,1)S(1)}, bf16[4,4,4,64,32]{3,4,2,1,0:T(8,128)(2,1)}, u32[]{:S(2)}) copy-start(bf16[4,4,4,64,32]{3,4,2,1,0:T(8,128)(2,1)} %param.4) | copy-start | bytes 786436
  72.7 1.0 %copy-start.8 = (bf16[512,512]{1,0:T(8,128)(2,1)S(1)}, bf16[512,512]{1,0:T(8,128)(2,1)}, u32[]{:S(2)}) copy-start(bf16[512,512]{1,0:T(8,128)(2,1)} %copy-done.7) | copy-start | bytes 1572868
  73.8 1.0 %copy-start.10 = (bf16[512,512]{1,0:T(8,128)(2,1)S(1)}, bf16[512,512]{1,0:T(8,128)(2,1)}, u32[]{:S(2)}) copy-start(bf16[512,512]{1,0:T(8,128)(2,1)} %copy-done.9) | copy-start | bytes 1572868
  74.8 1.0 %copy-start.12 = (bf16[512,512]{1,0:T(8,128)(2,1)S(1)}, bf16[512,512]{1,0:T(8,128)(2,1)}, u32[]{:S(2)}) copy-start(bf16[512,512]{1,0:T(8,128)(2,1)} %copy-done.11) | copy-start | bytes 1572868
where the time goes:
time: 87.1 us; the launch traced here: 86.6 us
  waiting for transfers between devices  26.6 us (31%)
  Pallas kernels  23.3 us (27%)
  starting transfers between devices  21.1 us (24%)
  local copies, waits for them, and re-layouts  13.5 us (15%)
  other arithmetic  1.37 us (2%)
    unnamed x26, local copies, waits for them, and re-layouts  13.5 us
    ppermute x1, starting transfers between devices, sum_over_chips(): away = lax.ppermute(mine, 'gx', pairs(2))  12.1 us
    pallas_call x1, Pallas kernels, on_device(): call(first_kernel, [struct(((2 * ny + 2) * group, nz), BF16), struct((row...  11.2 us
    ppermute x1, waiting for transfers between devices, sum_over_chips(): away = lax.ppermute(mine, 'gx', pairs(2))  10 us
    ppermute x2, waiting for transfers between devices, sum_over_chips(): mine = mine + lax.ppermute(mine, 'gx', pairs(step))  9.5 us
    pallas_call x1, Pallas kernels, on_device(): call(fine_kernel, [struct(cotangent.shape, BF16)], [pltpu.VMEM(blocks_d,...  8.54 us
    ppermute x1, starting transfers between devices, on_device(): outer = lax.ppermute(own, 'gx', outer_pairs)  5.64 us
    ppermute x1, waiting for transfers between devices, sum_over_chips(): mine = mine + lax.ppermute(away, 'gx', pairs(2))  5.53 us
  transfers between devices with their start and end apart: 10, of which 5 were waited for; matrix products, arithmetic and copies ran while one was open for 2% of the time, Pallas kernels for 23%

commit v1 on v0

v1 whole, which is shorter than its diff:
```python
import functools
import math

import jax
import jax.numpy as jnp
from jax import lax
from jax.experimental import pallas as pl
from jax.experimental.pallas import tpu as pltpu
from jax.sharding import PartitionSpec as P

F32 = jnp.float32
BF16 = jnp.bfloat16
NT = (((1,), (1,)), ((), ()))
TOP = 14.0
FLOPS_A = 500_000_000
FLOPS_B = 500_000_000


def roles(core):
    inner = (1 - core, 2 - core, 3 * core)
    outer = (core, 1 + core, 3 - 3 * core)
    return inner, outer


def dot(a, b):
    return jnp.dot(a, b, preferred_element_type=F32)


def split_table():
    row = lax.broadcasted_iota(jnp.int32, (256, 256), 0)
    col = lax.broadcasted_iota(jnp.int32, (256, 256), 1)
    return (row == jnp.where(col < 128, 2 * col, 2 * col - 255)).astype(BF16)


def join_table():
    row = lax.broadcasted_iota(jnp.int32, (256, 256), 0)
    col = lax.broadcasted_iota(jnp.int32, (256, 256), 1)
    return (col == jnp.where(row < 128, 2 * row, 2 * row - 255)).astype(BF16)


def load_rows(ref, start, count, stride):
    return jnp.concatenate([ref[b, pl.ds(start, count, stride=stride), :] for b in range(ref.shape[0])], 1)


def store_rows(ref, start, stride, value):
    for b in range(ref.shape[0]):
        ref[b, pl.ds(start, value.shape[0], stride=stride), :] = value[:, 128 * b : 128 * b + 128]


def rows_by_y(source_ref, wide_ref, target_ref, ny):
    chans = source_ref.shape[0] // ny
    for b in range(wide_ref.shape[0]):
        wide_ref[b] = source_ref[:, 128 * b : 128 * b + 128].astype(F32)
    for y in range(ny):
        target_ref[y * chans : (y + 1) * chans, :] = load_rows(wide_ref, y, chans, ny).astype(BF16)


def fetches(cot_ref, side, plane_ref, sems):
    chunk = plane_ref.shape[0] // sems.shape[0]
    return [
        pltpu.make_async_copy(
            cot_ref.at[pl.ds(chunk * i, chunk), side], plane_ref.at[pl.ds(chunk * i, chunk)], sems.at[i]
        )
        for i in range(sems.shape[0])
    ]


def tap_rows(copies, plane_ref, even_ref, odd_ref, taps_ref):
    dout, ny2, nz2 = plane_ref.shape
    nz = nz2 // 2
    table = split_table()
    chunk = dout // len(copies)
    for i, copy in enumerate(copies):
        copy.wait()
        at = pl.ds(chunk * i * ny2, chunk * ny2)
        for b in range(nz2 // 256):
            block = plane_ref[chunk * i : chunk * i + chunk, :, 256 * b : 256 * b + 256]
            halves = dot(block.reshape(chunk * ny2, 256), table)
            even_ref[b, at, :] = halves[:, :128]
            odd_ref[b, at, :] = halves[:, 128:]

    def row(y, carry):
        even = load_rows(even_ref, y, dout, ny2)
        odd = load_rows(odd_ref, y, dout, ny2)
        base = pl.multiple_of((y + 1) * 4 * dout, 4 * dout)
        pieces = (pltpu.roll(odd, 1, 1), even, odd, pltpu.roll(even, nz - 1, 1))
        for k, piece in enumerate(pieces):
            taps_ref[pl.ds(base + k * dout, dout), :] = piece.astype(BF16)
        return carry

    lax.fori_loop(0, ny2, row, 0, unroll=4)
    group = 4 * dout
    taps_ref[:group, :] = taps_ref[ny2 * group : (ny2 + 1) * group, :]
    taps_ref[(ny2 + 1) * group :, :] = taps_ref[group : 2 * group, :]


def grad_weights(w_ref, own, nbr):
    both = jnp.concatenate([w_ref[own].astype(F32), w_ref[nbr].astype(F32)], 1)
    return both.T.astype(BF16)


def flatten(blocks_ref, out_ref):
    for b in range(blocks_ref.shape[0]):
        out_ref[:, 128 * b : 128 * b + 128] = blocks_ref[b]


def outer_kernel(
    core_ref, cot_ref, w_ref, taps_ref, vg_ref, partial_ref,
    plane_ref, even_ref, odd_ref, vg_blocks, partial_blocks, sems,
):
    dout, ny2, _ = plane_ref.shape
    ny, group, chans = ny2 // 2, 4 * dout, w_ref.shape[2]
    side, own, nbr = roles(core_ref[0])[1]
    copies = fetches(cot_ref, side, plane_ref, sems)
    for copy in copies:
        copy.start()
    weights = grad_weights(w_ref, own, nbr)
    tap_rows(copies, plane_ref, even_ref, odd_ref, taps_ref)
    most = jnp.zeros((chans, vg_ref.shape[1]), F32)
    for y in range(ny):
        sums = dot(weights, taps_ref[y * 2 * group : (y * 2 + 4) * group, :])
        store_rows(vg_blocks, y, ny, sums[:chans])
        store_rows(partial_blocks, y, ny, sums[chans:])
        most = jnp.maximum(most, jnp.abs(sums[chans:]))
    flatten(vg_blocks, vg_ref)
    rows = chans * ny
    most = jnp.max(jnp.max(most, axis=0, keepdims=True), axis=1, keepdims=True)
    level = jnp.ceil(jnp.log2(jnp.maximum(most, 1e-30)))
    shrink = jnp.exp2(TOP - level)
    for b in range(partial_blocks.shape[0]):
        partial_ref[:rows, 128 * b : 128 * b + 128] = partial_blocks[b] * shrink
    partial_ref[rows:, :] = jnp.broadcast_to(level, (partial_ref.shape[0] - rows, partial_ref.shape[1]))


def inner_kernel(
    core_ref, cot_ref, w_ref, own_ref, inner_ref, vg_part_ref,
    own_t_ref, inner_t_ref, wg_ref, vg_ref, partial_ref,
    plane_ref, even_ref, odd_ref, vg_blocks, partial_blocks, taps_ref, sems,
):
    dout, ny2, _ = plane_ref.shape
    ny, group, chans = ny2 // 2, 4 * dout, w_ref.shape[2]
    side, own, nbr = roles(core_ref[0])[0]
    copies = fetches(cot_ref, side, plane_ref, sems)
    for copy in copies:
        copy.start()
    rows_by_y(own_ref, vg_blocks, own_t_ref, ny)
    rows_by_y(inner_ref, partial_blocks, inner_t_ref, ny)
    weights = grad_weights(w_ref, own, nbr)
    tap_rows(copies, plane_ref, even_ref, odd_ref, taps_ref)
    for y in range(ny):
        taps = taps_ref[y * 2 * group : (y * 2 + 4) * group, :]
        sums = dot(weights, taps)
        store_rows(vg_blocks, y, ny, sums[:chans])
        store_rows(partial_blocks, y, ny, sums[chans:])
        cells = jnp.concatenate([r[y * chans : (y + 1) * chans, :] for r in (own_t_ref, inner_t_ref)], 0)
        grads = lax.dot_general(taps, cells, NT, preferred_element_type=F32)
        wg_ref[...] = grads if y == 0 else wg_ref[...] + grads
    for b in range(vg_blocks.shape[0]):
        at = slice(128 * b, 128 * b + 128)
        vg_ref[:, at] = vg_part_ref[:, at] + vg_blocks[b]
    flatten(partial_blocks, partial_ref)


def split(bit, whole_ref, keep_ref, send_ref):
    half = keep_ref.shape[0]
    keep_ref[...] = whole_ref[pl.ds(pl.multiple_of(bit * half, half), half), :]
    send_ref[...] = whole_ref[pl.ds(pl.multiple_of((1 - bit) * half, half), half), :]


def second_kernel(bits_ref, taps_ref, own_t_ref, outer_ref, arrived_ref, keep_ref, send_ref, outer_t_ref, wide_ref, sum_ref):
    chans = arrived_ref.shape[1] // 2
    ny = outer_ref.shape[0] // chans
    rows = sum_ref.shape[0]
    rows_by_y(outer_ref, wide_ref, outer_t_ref, ny)
    for y in range(ny):
        taps = taps_ref[y * rows // 2 : y * rows // 2 + rows, :]
        cells = jnp.concatenate([r[y * chans : (y + 1) * chans, :] for r in (own_t_ref, outer_t_ref)], 0)
        grads = lax.dot_general(taps, cells, NT, preferred_element_type=F32)
        sum_ref[...] = (arrived_ref if y == 0 else sum_ref)[...] + grads
    split(bits_ref[1], sum_ref, keep_ref, send_ref)


def add_split_kernel(which, bits_ref, a_ref, b_ref, keep_ref, send_ref, sum_ref):
    sum_ref[...] = a_ref[...] + b_ref[...]
    split(bits_ref[which], sum_ref, keep_ref, send_ref)


def add_kernel(a_ref, b_ref, out_ref):
    out_ref[...] = a_ref[...] + b_ref[...]


def join_kernel(which, bits_ref, mine_ref, there_ref, out_ref):
    bit, half = bits_ref[which], mine_ref.shape[0]
    out_ref[pl.ds(pl.multiple_of(bit * half, half), half), :] = mine_ref[...]
    out_ref[pl.ds(pl.multiple_of((1 - bit) * half, half), half), :] = there_ref[...]


def taps_kernel(scale, bits_ref, mine_ref, other_ref, out_ref):
    chans = out_ref.shape[2]
    core = bits_ref[0]
    for ref, side in ((mine_ref, core), (other_ref, 1 - core)):
        _, own, nbr = roles(side)[1]
        both = ref[...] * scale
        out_ref[own] = both[:, :chans]
        out_ref[nbr] = both[:, chans:]


def cells_kernel(vg_ref, inner_ref, outer_ref, out_ref):
    rows = vg_ref.shape[0]
    grow = jnp.exp2(outer_ref[rows : rows + 1, :] - TOP)
    out_ref[...] = (vg_ref[...] + inner_ref[...] + outer_ref[:rows, :] * grow).astype(BF16)


def fine_kernel(which, core_ref, own_t_ref, nbr_t_ref, w_ref, *refs):
    out_ref, plane_ref, even_ref, odd_ref, sem = refs[-5:]
    dout, ny2, nz2 = plane_ref.shape
    ny, nz = ny2 // 2, nz2 // 2
    chans = w_ref.shape[2]
    group = 4 * dout
    side, own, nbr = roles(core_ref[0])[which]
    for phase, step, taps in ((0, ny - 1, (1, 3)), (1, 1, (2, 0))):
        slabs = [w_ref[x, y * group : (y + 1) * group, :] for x in (own, nbr) for y in taps]
        weights = jnp.concatenate(slabs, 1)
        for y in range(ny):
            near = slice(y * chans, (y + 1) * chans)
            far = slice((y + step) % ny * chans, ((y + step) % ny + 1) * chans)
            cells = jnp.concatenate([r[at, :] for r in (own_t_ref, nbr_t_ref) for at in (near, far)], 0)
            sums = dot(weights, cells)
            even = sums[dout : 2 * dout] + pltpu.roll(sums[3 * dout :], 1, 1)
            odd = sums[2 * dout : 3 * dout] + pltpu.roll(sums[:dout], nz - 1, 1)
            store_rows(even_ref, 2 * y + phase, ny2, even)
            store_rows(odd_ref, 2 * y + phase, ny2, odd)
    table = join_table()
    for b in range(nz // 128):
        halves = jnp.concatenate([even_ref[b].astype(BF16), odd_ref[b].astype(BF16)], 1)
        fine = dot(halves, table).astype(BF16)
        plane_ref[:, :, 256 * b : 256 * b + 256] = fine.reshape(dout, ny2, 256)
    copy = pltpu.make_async_copy(plane_ref, out_ref.at[:, side], sem)
    copy.start()
    copy.wait()


VMEM = pl.BlockSpec(memory_space=pltpu.VMEM)
SMEM = pl.BlockSpec(memory_space=pltpu.SMEM)
HBM = pl.BlockSpec(memory_space=pltpu.HBM)


def call(kernel, in_specs, out_specs, outs, scratch, grant, flops=1_000, **more):
    return pl.pallas_call(
        kernel,
        out_shape=outs,
        in_specs=in_specs,
        out_specs=out_specs,
        scratch_shapes=scratch,
        compiler_params=pltpu.CompilerParams(vmem_limit_bytes=grant << 20),
        cost_estimate=pl.CostEstimate(flops=flops, bytes_accessed=1_000, transcendentals=0),
        **more,
    )


def together(*values):
    return lax.optimization_barrier(values)


def on_device(volume, weights, cotangent):
    chans, planes, ny, nz = volume.shape
    dout = cotangent.shape[0]
    peers = lax.axis_size("gx")
    me = lax.axis_index("gx")
    bits = jnp.stack([me & 1, (me >> 2) & 1, (me >> 1) & 1]).astype(jnp.int32)
    rows, wide, group = chans * ny, 16 * dout, 4 * dout
    struct = jax.ShapeDtypeStruct
    blocks_c, blocks_d = (nz // 128, rows, 128), (nz // 128, dout * 2 * ny, 128)
    taps_shape, plane_shape = ((2 * ny + 2) * group, nz), (dout, 2 * ny, 2 * nz)
    cells, wide_cells = struct((rows, nz), BF16), struct((rows, nz), F32)
    work = [pltpu.VMEM(plane_shape, BF16), pltpu.VMEM(blocks_d, F32), pltpu.VMEM(blocks_d, F32)]
    chunks = pltpu.SemaphoreType.DMA((4,))

    def swap(value, k):
        return lax.ppermute(value, "gx", [(i, i ^ k) for i in range(peers)])

    def beyond(value):
        return lax.ppermute(value, "gx", [(i, (i + (1 if i % 2 else -1)) % peers) for i in range(peers)])

    cotangent = pltpu.with_memory_space_constraint(cotangent, pltpu.HBM)
    own = volume.reshape(rows, nz)
    outer = beyond(own)
    inner = swap(own, 1)
    kernels = jnp.transpose(weights, (0, 1, 2, 4, 3)).reshape(4, wide, chans)

    taps_o, vg_o, to_outer = call(
        outer_kernel,
        [SMEM, HBM, VMEM],
        [VMEM] * 3,
        [struct(taps_shape, BF16), wide_cells, struct((rows + 16, nz), F32)],
        work + [pltpu.VMEM(blocks_c, F32), pltpu.VMEM(blocks_c, F32), chunks],
        8,
    )(bits, cotangent, kernels)
    to_outer, vg_o = together(to_outer.astype(jnp.float16), vg_o)
    from_outer = beyond(to_outer)

    own_t, inner_t, wg_i, vg, to_inner = call(
        inner_kernel,
        [SMEM, HBM] + [VMEM] * 4,
        [VMEM] * 5,
        [cells, cells, struct((wide, 2 * chans), F32), wide_cells, wide_cells],
        work + [pltpu.VMEM(blocks_c, F32), pltpu.VMEM(blocks_c, F32), pltpu.VMEM(taps_shape, BF16), chunks],
        12,
    )(bits, cotangent, kernels, own, inner, vg_o)
    wg_arrived = swap(wg_i, 1)

    def piece(n):
        return struct((wide // n, 2 * chans), F32)

    keep, send, outer_t = call(
        second_kernel,
        [SMEM] + [VMEM] * 4,
        [VMEM] * 3,
        [piece(2), piece(2), cells],
        [pltpu.VMEM(blocks_c, F32), pltpu.VMEM((wide, 2 * chans), F32)],
        6,
        flops=FLOPS_A,
    )(bits, taps_o, own_t, outer, wg_arrived)

    def fine(which, nbr_t, so_far):
        more = {} if so_far is None else {"input_output_aliases": {4: 0}}
        return call(
            functools.partial(fine_kernel, which),
            [SMEM, VMEM, VMEM, VMEM] + [HBM] * (so_far is not None),
            [HBM],
            [struct(cotangent.shape, BF16)],
            work + [pltpu.SemaphoreType.DMA],
            8,
            flops=FLOPS_B,
            **more,
        )(bits, own_t, nbr_t, kernels, *([] if so_far is None else [so_far]))[0]

    def add(a, b):
        return call(add_kernel, [VMEM] * 2, [VMEM], [struct(a.shape, F32)], [], 2)(a, b)[0]

    def add_split(which, a, b):
        half = struct((a.shape[0] // 2, a.shape[1]), F32)
        return call(
            functools.partial(add_split_kernel, which),
            [SMEM, VMEM, VMEM], [VMEM] * 2, [half, half], [pltpu.VMEM(a.shape, F32)], 2,
        )(bits, a, b)

    def join(which, a, b):
        whole = struct((2 * a.shape[0], a.shape[1]), F32)
        return call(functools.partial(join_kernel, which), [SMEM, VMEM, VMEM], [VMEM], [whole], [], 2)(bits, a, b)[0]

    inner_t, keep = together(inner_t, keep)
    upsampled = fine(0, inner_t, None)
    send, to_inner, upsampled, from_outer = together(send, to_inner, upsampled, from_outer)
    from_inner = swap(to_inner, 1)
    if peers & (peers - 1) or peers < 8:
        groups = [[i for i in range(peers) if i % 2 == c] for c in range(2)]
        total = lax.psum(join(1, keep, send), "gx", axis_index_groups=groups)
        upsampled = fine(1, outer_t, upsampled)
        (volume_grad,) = call(cells_kernel, [VMEM] * 3, [VMEM], [cells], [], 4)(vg, from_inner, from_outer.astype(F32))
    else:
        keep, send = add_split(2, keep, swap(send, 4))
        (volume_grad,) = call(cells_kernel, [VMEM] * 3, [VMEM], [cells], [], 4)(vg, from_inner, from_outer.astype(F32))
        send, volume_grad = together(send, volume_grad)
        mine = add(keep, swap(send, 2))
        mine, outer_t = together(mine, outer_t)
        upsampled = fine(1, outer_t, upsampled)
        for k in range(3, peers.bit_length() - 1):
            mine = add(mine, swap(mine, 1 << k))
        mine, upsampled = together(mine, upsampled)
        mine = join(2, mine, swap(mine, 2))
        total = join(1, mine, swap(mine, 4))
    scale = 1.0 / math.sqrt(peers * planes * ny * nz)
    (weight_grad,) = call(
        functools.partial(taps_kernel, scale), [SMEM, VMEM, VMEM], [VMEM], [struct((4, wide, chans), F32)], [], 4
    )(bits, total, swap(total, 1))
    weight_grad = jnp.transpose(weight_grad.reshape(4, 4, 4, dout, chans), (0, 1, 2, 4, 3))
    return (upsampled, volume_grad.reshape(volume.shape), weight_grad)


def solution(mesh):
    placed = (P(None, "gx", "groups", None), P(), P(None, "gx", "groups", None))
    return jax.shard_map(
        on_device,
        mesh=mesh,
        in_specs=placed,
        out_specs=(
            P(None, "gx", "groups", None),
            P(None, "gx", "groups", None),
            P("groups", None, None, None, None),
        ),
        check_vma=False,
    )
```

time: 87.1 us -> 60 us (0.69)
  local copies, waits for them, and re-layouts: 13.5 us -> 1.05 us
  waiting for transfers between devices: 26.6 us -> 15.2 us
  starting transfers between devices: 21.1 us -> 18.6 us
  other arithmetic: 1.37 us -> 0.31 us
    unnamed x26 -> x6, local copies, waits for them, and re-layouts: 13.5 us -> 1.05 us
    ppermute x10 -> x11, waiting for transfers between devices: 26.6 us -> 15.2 us  [the longest x9 15.2 us: swap(): return lax.ppermute(value, 'gx', [(i, i ^ k) for i in range(peers)])]
    ppermute x10 -> x11, starting transfers between devices: 21.1 us -> 18.6 us  [the longest x9 12.9 us: swap(): return lax.ppermute(value, 'gx', [(i, i ^ k) for i in range(peers)])]
    transpose x1 -> x0, other arithmetic: 1.1 us -> none  [on_device(): jnp.transpose((blocks * scale).reshape(4, 4, 4, dout, chans), (0, 1, 2, 4...]
    pallas_call x4 -> x12, Pallas kernels: 23.3 us -> 23.9 us  [the longest x2 6.75 us: fine(): call(functools.partial(fine_kernel, which), [SMEM, VMEM, VMEM, VMEM] + [H...]
  transfers between devices with their start and end apart: 10 -> 11, of which waited for: 5 -> 6; matrix products, arithmetic and copies ran while one was open for 2% -> 1% of each run, Pallas kernels for 23% -> 34%
where the time goes in v1:
time: 60 us; the launch traced here: 59.8 us
  Pallas kernels  23.9 us (40%)
  starting transfers between devices  18.6 us (31%)
  waiting for transfers between devices  15.2 us (25%)
  local copies, waits for them, and re-layouts  1.05 us (2%)
  between operations  0.81 us (1%)
    ppermute x9, waiting for transfers between devices, swap(): return lax.ppermute(value, 'gx', [(i, i ^ k) for i in range(peers)])  15.2 us
    ppermute x9, starting transfers between devices, swap(): return lax.ppermute(value, 'gx', [(i, i ^ k) for i in range(peers)])  12.9 us
    pallas_call x2, Pallas kernels, fine(): call(functools.partial(fine_kernel, which), [SMEM, VMEM, VMEM, VMEM] + [H...  6.75 us
    pallas_call x1, Pallas kernels, on_device(): call(inner_kernel, [SMEM, HBM] + [VMEM] * 4, [VMEM] * 5, [cells, cells, s...  5.85 us
    ppermute x2, starting transfers between devices, beyond(): lax.ppermute(value, 'gx', [(i, (i + (1 if i % 2 else -1)) % peers) for i...  5.71 us
    pallas_call x1, Pallas kernels, on_device(): call(outer_kernel, [SMEM, HBM, VMEM], [VMEM] * 3, [struct(taps_shape, BF1...  5.04 us
    pallas_call x1, Pallas kernels, on_device(): call(second_kernel, [SMEM] + [VMEM] * 4, [VMEM] * 3, [piece(2), piece(2),...  1.84 us
    pallas_call x1, Pallas kernels, on_device(): call(functools.partial(taps_kernel, scale), [SMEM, VMEM, VMEM], [VMEM], [...  1.73 us
  transfers between devices with their start and end apart: 11, of which 6 were waited for; matrix products, arithmetic and copies ran while one was open for 1% of the time, Pallas kernels for 34%

profile of v1, /device:TPU:0, one launch (start us, length us, event | category | flops | bytes accessed | tf_op | source)
XLA Modules:
  0.0 59.8 jit_solution(18264722403575979356)
XLA Ops:
  1.1 5.6 %collective-permute-start.1 = (bf16[512,512]{1,0:T(8,128)(2,1)}, bf16[512,512]{1,0:T(8,128)(2,1)S(1)}, u32[]{:S(2)}, u32[]{:S(2)}) collective-permute-start(bf16[512,512]{1,0:T(8,128)(2,1)} %bitcast.18), channel_id=1, source_target_pairs={{0,15},{1,2},{2,1},{3,4},{4,3},{5,6},{6,5},{7,8},{8,7},{9,10},{10,... | collective-permute-start | bytes 1572872 | tf_op jit(solution)/shard_map/ppermute | solution.py:283
  6.9 1.0 %copy-done = bf16[4,4,4,64,32]{3,4,2,1,0:T(8,128)(2,1)S(1)} copy-done((bf16[4,4,4,64,32]{3,4,2,1,0:T(8,128)(2,1)S(1)}, bf16[4,4,4,64,32]{3,4,2,1,0:T(8,128)(2,1)}, u32[]{:S(2)}) %copy-start) | copy-done | bytes 262168
  7.9 5.0 %shard_map.58 = (bf16[2304,512]{1,0:T(8,128)(2,1)S(1)}, f32[512,512]{1,0:T(8,128)S(1)}, f32[528,512]{1,0:T(8,128)S(1)}) custom-call(s32[3]{0:T(128)S(1)} %pad_add_fusion.core_ref.bits_ref, bf16[32,2,16,1024]{3,2,1,0:T(8,128)(2,1)} %cot_ref.3, bf16[4,512,64]{2,1,0:T(8,128)(2,1)S(1)} %bitcast.13), custom_call_target="tpu_custom_call" | custom-call | flops 1000 | bytes 1000 | tf_op jit(solution)/shard_map/pallas_call | solution.py:291
  13.2 5.9 %shard_map.59 = (bf16[512,512]{1,0:T(8,128)(2,1)S(1)}, bf16[512,512]{1,0:T(8,128)(2,1)S(1)}, f32[512,128]{1,0:T(8,128)S(1)}, f32[512,512]{1,0:T(8,128)S(1)}, f32[512,512]{1,0:T(8,128)S(1)}) custom-call(s32[3]{0:T(128)S(1)} %pad_add_fusion.core_ref.bits_ref, bf16[32,2,16,1024]{3,2,1,0:T(8,128)(2,1)} %cot_ref.3, bf16[4,512,64]{2,1,0:T(8,128)(2,1)S(1)} %bitcast.14, ...), custom_call_target="tpu_custom_call" | custom-call | flops 1000 | bytes 1000 | tf_op jit(solution)/shard_map/pallas_call | solution.py:302
  19.1 1.5 %collective-permute-done.2.arrived_ref = f32[512,128]{1,0:T(8,128)S(1)} collective-permute-done((f32[512,128]{1,0:T(8,128)S(1)}, f32[512,128]{1,0:T(8,128)S(1)}, u32[]{:S(2)}, u32[]{:S(2)}) %collective-permute-start.2) | collective-permute-done | bytes 262176 | tf_op jit(solution)/shard_map/ppermute | solution.py:280
  20.6 1.8 %shard_map.60 = (f32[256,128]{1,0:T(8,128)S(1)}, f32[256,128]{1,0:T(8,128)S(1)}, bf16[512,512]{1,0:T(8,128)(2,1)S(1)}) custom-call(s32[3]{0:T(128)S(1)} %pad_add_fusion.core_ref.bits_ref, bf16[2304,512]{1,0:T(8,128)(2,1)S(1)} %get-tuple-element.34.taps_ref, bf16[512,512]{1,0:T(8,128)(2,1)S(1)} %get-tuple-element.35.own_t_ref, ...), custom_call_target="tpu_custom_call" | custom-call | flops 500000000 | bytes 1000 | tf_op jit(solution)/shard_map/pallas_call | solution.py:315
  22.5 3.4 %shard_map.61.refs_0_ = bf16[32,2,16,1024]{3,2,1,0:T(8,128)(2,1)} custom-call(s32[3]{0:T(128)S(1)} %pad_add_fusion.core_ref.bits_ref, bf16[512,512]{1,0:T(8,128)(2,1)S(1)} %get-tuple-element.35.own_t_ref, bf16[512,512]{1,0:T(8,128)(2,1)S(1)} %get-tuple-element.41.nbr_t_ref, bf16[4,512,64]{2,1,0:T(8,128)(2,1)S(1)} %bitcast.15), custom_call_target="tpu_custom_call" | custom-call | flops 500000000 | bytes 1000 | tf_op jit(solution)/shard_map/pallas_call | solution.py:327
  25.9 2.2 %collective-permute-start.5 = (f32[512,512]{1,0:T(8,128)S(1)}, f32[512,512]{1,0:T(8,128)S(1)}, u32[]{:S(2)}, u32[]{:S(2)}) collective-permute-start(f32[512,512]{1,0:T(8,128)S(1)} %get-tuple-element.47), channel_id=1, source_target_pairs={{0,1},{1,0},{2,3},{3,2},{4,5},{5,4},{6,7},{7,6},{8,9},{9,8},{10,11... | collective-permute-start | bytes 3145736 | tf_op jit(solution)/shard_map/ppermute | solution.py:280
  28.1 2.1 %collective-permute-start.4 = (f32[256,128]{1,0:T(8,128)S(1)}, f32[256,128]{1,0:T(8,128)S(1)}, u32[]{:S(2)}, u32[]{:S(2)}) collective-permute-start(f32[256,128]{1,0:T(8,128)S(1)} %get-tuple-element.43), channel_id=1, source_target_pairs={{0,4},{1,5},{2,6},{3,7},{4,0},{5,1},{6,2},{7,3},{8,12},{9,13},{10,... | collective-permute-start | bytes 393224 | tf_op jit(solution)/shard_map/ppermute | solution.py:280
  30.4 3.5 %collective-permute-done.4.b_ref = f32[256,128]{1,0:T(8,128)S(1)} collective-permute-done((f32[256,128]{1,0:T(8,128)S(1)}, f32[256,128]{1,0:T(8,128)S(1)}, u32[]{:S(2)}, u32[]{:S(2)}) %collective-permute-start.4) | collective-permute-done | bytes 131104 | tf_op jit(solution)/shard_map/ppermute | solution.py:280
  33.9 0.6 shard_map.62
  34.5 0.9 %shard_map.63 = bf16[512,512]{1,0:T(8,128)(2,1)} custom-call(f32[512,512]{1,0:T(8,128)S(1)} %get-tuple-element.46.vg_ref, f32[512,512]{1,0:T(8,128)S(1)} %collective-permute-done.5.inner_ref, f32[528,512]{1,0:T(8,128)S(1)} %convert_element_type.7.outer_ref), custom_call_target="tpu_custom_call" | custom-call | flops 1000 | bytes 1000 | tf_op jit(solution)/shard_map/pallas_call | solution.py:363
  35.4 1.7 %collective-permute-start.6 = (f32[128,128]{1,0:T(8,128)S(1)}, f32[128,128]{1,0:T(8,128)S(1)}, u32[]{:S(2)}, u32[]{:S(2)}) collective-permute-start(f32[128,128]{1,0:T(8,128)S(1)} %get-tuple-element.49), channel_id=1, source_target_pairs={{0,2},{1,3},{2,0},{3,1},{4,6},{5,7},{6,4},{7,5},{8,10},{9,11},{10,... | collective-permute-start | bytes 196616 | tf_op jit(solution)/shard_map/ppermute | solution.py:280
  37.2 2.5 %collective-permute-done.6.b_ref = f32[128,128]{1,0:T(8,128)S(1)} collective-permute-done((f32[128,128]{1,0:T(8,128)S(1)}, f32[128,128]{1,0:T(8,128)S(1)}, u32[]{:S(2)}, u32[]{:S(2)}) %collective-permute-start.6) | collective-permute-done | bytes 65568 | tf_op jit(solution)/shard_map/ppermute | solution.py:280
  39.7 2.8 %collective-permute-start.7 = (f32[128,128]{1,0:T(8,128)S(1)}, f32[128,128]{1,0:T(8,128)S(1)}, u32[]{:S(2)}, u32[]{:S(2)}) collective-permute-start(f32[128,128]{1,0:T(8,128)S(1)} %shard_map.64.a_ref), channel_id=1, source_target_pairs={{0,8},{1,9},{2,10},{3,11},{4,12},{5,13},{6,14},{7,15},{8,0},{9,1},... | collective-permute-start | bytes 196616 | tf_op jit(solution)/shard_map/ppermute | solution.py:280
  42.5 3.4 %shard_map.66 = bf16[32,2,16,1024]{3,2,1,0:T(8,128)(2,1)} custom-call(s32[3]{0:T(128)S(1)} %pad_add_fusion.core_ref.bits_ref, bf16[512,512]{1,0:T(8,128)(2,1)S(1)} %get-tuple-element.35.own_t_ref, bf16[512,512]{1,0:T(8,128)(2,1)S(1)} %get-tuple-element.52.nbr_t_ref, bf16[4,512,64]{2,1,0:T(8,128)(2,1)S(1)} %bitcast.16, ...), custom_call_target="tpu_custom_call", output_to_operand_aliasing={{}: (4, {})} | custom-call | flops 500000000 | bytes 1000 | tf_op jit(solution)/shard_map/pallas_call | solution.py:327
  45.9 1.6 %collective-permute-start.8 = (f32[128,128]{1,0:T(8,128)S(1)}, f32[128,128]{1,0:T(8,128)S(1)}, u32[]{:S(2)}, u32[]{:S(2)}) collective-permute-start(f32[128,128]{1,0:T(8,128)S(1)} %shard_map.65.mine_ref), channel_id=1, source_target_pairs={{0,2},{1,3},{2,0},{3,1},{4,6},{5,7},{6,4},{7,5},{8,10},{9,11},{10,... | collective-permute-start | bytes 196616 | tf_op jit(solution)/shard_map/ppermute | solution.py:280
  47.6 2.7 %collective-permute-done.8.there_ref = f32[128,128]{1,0:T(8,128)S(1)} collective-permute-done((f32[128,128]{1,0:T(8,128)S(1)}, f32[128,128]{1,0:T(8,128)S(1)}, u32[]{:S(2)}, u32[]{:S(2)}) %collective-permute-start.8) | collective-permute-done | bytes 65568 | tf_op jit(solution)/shard_map/ppermute | solution.py:280
  50.3 0.6 shard_map.67.mine_ref
  50.8 1.6 %collective-permute-start.9 = (f32[256,128]{1,0:T(8,128)S(1)}, f32[256,128]{1,0:T(8,128)S(1)}, u32[]{:S(2)}, u32[]{:S(2)}) collective-permute-start(f32[256,128]{1,0:T(8,128)S(1)} %shard_map.67.mine_ref), channel_id=1, source_target_pairs={{0,4},{1,5},{2,6},{3,7},{4,0},{5,1},{6,2},{7,3},{8,12},{9,13},{10,... | collective-permute-start | bytes 393224 | tf_op jit(solution)/shard_map/ppermute | solution.py:280
  52.5 3.4 %collective-permute-done.9.there_ref = f32[256,128]{1,0:T(8,128)S(1)} collective-permute-done((f32[256,128]{1,0:T(8,128)S(1)}, f32[256,128]{1,0:T(8,128)S(1)}, u32[]{:S(2)}, u32[]{:S(2)}) %collective-permute-start.9) | collective-permute-done | bytes 131104 | tf_op jit(solution)/shard_map/ppermute | solution.py:280
  55.9 0.6 shard_map.68.mine_ref
  56.5 1.5 %collective-permute-done.10.other_ref = f32[512,128]{1,0:T(8,128)S(1)} collective-permute-done((f32[512,128]{1,0:T(8,128)S(1)}, f32[512,128]{1,0:T(8,128)S(1)}, u32[]{:S(2)}, u32[]{:S(2)}) %collective-permute-start.10) | collective-permute-done | bytes 262176 | tf_op jit(solution)/shard_map/ppermute | solution.py:280
  58.0 1.7 %shard_map.69 = f32[4,512,64]{2,1,0:T(8,128)} custom-call(s32[3]{0:T(128)S(1)} %pad_add_fusion.core_ref.bits_ref, f32[512,128]{1,0:T(8,128)S(1)} %shard_map.68.mine_ref, f32[512,128]{1,0:T(8,128)S(1)} %collective-permute-done.10.other_ref), custom_call_target="tpu_custom_call" | custom-call | flops 1000 | bytes 1000 | tf_op jit(solution)/shard_map/pallas_call | solution.py:374
  (19 shorter events, 1.1 us)
Async XLA Ops:
  0.6 12.5 %collective-permute-start = (bf16[512,512]{1,0:T(8,128)(2,1)}, bf16[512,512]{1,0:T(8,128)(2,1)S(1)}, u32[]{:S(2)}, u32[]{:S(2)}) collective-permute-start(bf16[512,512]{1,0:T(8,128)(2,1)} %bitcast.17), channel_id=1, source_target_pairs={{0,1},{1,0},{2,3},{3,2},{4,5},{5,4},{6,7},{7,6},{8,9},{9,8},{10,11... | collective-permute-start | bytes 1572872 | tf_op jit(solution)/shard_map/ppermute | solution.py:280
  1.1 18.0 %collective-permute-start.1 = (bf16[512,512]{1,0:T(8,128)(2,1)}, bf16[512,512]{1,0:T(8,128)(2,1)S(1)}, u32[]{:S(2)}, u32[]{:S(2)}) collective-permute-start(bf16[512,512]{1,0:T(8,128)(2,1)} %bitcast.18), channel_id=1, source_target_pairs={{0,15},{1,2},{2,1},{3,4},{4,3},{5,6},{6,5},{7,8},{8,7},{9,10},{10,... | collective-permute-start | bytes 1572872 | tf_op jit(solution)/shard_map/ppermute | solution.py:283
  6.9 1.0 %copy-start = (bf16[4,4,4,64,32]{3,4,2,1,0:T(8,128)(2,1)S(1)}, bf16[4,4,4,64,32]{3,4,2,1,0:T(8,128)(2,1)}, u32[]{:S(2)}) copy-start(bf16[4,4,4,64,32]{3,4,2,1,0:T(8,128)(2,1)} %param.4) | copy-start | bytes 786436
  7.9 5.3 %copy-start.1 = (bf16[4,4,4,64,32]{3,4,2,1,0:T(8,128)(2,1)S(1)}, bf16[4,4,4,64,32]{3,4,2,1,0:T(8,128)(2,1)}, u32[]{:S(2)}) copy-start(bf16[4,4,4,64,32]{3,4,2,1,0:T(8,128)(2,1)} %param.4) | copy-start | bytes 786436
  7.9 5.3 %copy-start.2 = (bf16[64,1,8,512]{3,2,1,0:T(8,128)(2,1)S(1)}, bf16[64,1,8,512]{3,2,1,0:T(8,128)(2,1)}, u32[]{:S(2)}) copy-start(bf16[64,1,8,512]{3,2,1,0:T(8,128)(2,1)} %param.3) | copy-start | bytes 1572868
  13.1 12.8 %collective-permute-start.3 = (f16[528,512]{1,0:T(8,128)(2,1)S(1)}, f16[528,512]{1,0:T(8,128)(2,1)S(1)}, u32[]{:S(2)}, u32[]{:S(2)}) collective-permute-start(f16[528,512]{1,0:T(8,128)(2,1)S(1)} %convert_element_type.6), channel_id=1, source_target_pairs={{0,15},{1,2},{2,1},{3,4},{4,3},{5,6},{6,5},{7,8},{8,7},{9,10},{10,... | collective-permute-start | bytes 1622024 | tf_op jit(solution)/shard_map/ppermute | solution.py:283
  19.0 1.6 %collective-permute-start.2 = (f32[512,128]{1,0:T(8,128)S(1)}, f32[512,128]{1,0:T(8,128)S(1)}, u32[]{:S(2)}, u32[]{:S(2)}) collective-permute-start(f32[512,128]{1,0:T(8,128)S(1)} %get-tuple-element.36), channel_id=1, source_target_pairs={{0,1},{1,0},{2,3},{3,2},{4,5},{5,4},{6,7},{7,6},{8,9},{9,8},{10,11... | collective-permute-start | bytes 786440 | tf_op jit(solution)/shard_map/ppermute | solution.py:280
  25.9 8.6 %collective-permute-start.5 = (f32[512,512]{1,0:T(8,128)S(1)}, f32[512,512]{1,0:T(8,128)S(1)}, u32[]{:S(2)}, u32[]{:S(2)}) collective-permute-start(f32[512,512]{1,0:T(8,128)S(1)} %get-tuple-element.47), channel_id=1, source_target_pairs={{0,1},{1,0},{2,3},{3,2},{4,5},{5,4},{6,7},{7,6},{8,9},{9,8},{10,11... | collective-permute-start | bytes 3145736 | tf_op jit(solution)/shard_map/ppermute | solution.py:280
  28.1 5.8 %collective-permute-start.4 = (f32[256,128]{1,0:T(8,128)S(1)}, f32[256,128]{1,0:T(8,128)S(1)}, u32[]{:S(2)}, u32[]{:S(2)}) collective-permute-start(f32[256,128]{1,0:T(8,128)S(1)} %get-tuple-element.43), channel_id=1, source_target_pairs={{0,4},{1,5},{2,6},{3,7},{4,0},{5,1},{6,2},{7,3},{8,12},{9,13},{10,... | collective-permute-start | bytes 393224 | tf_op jit(solution)/shard_map/ppermute | solution.py:280
  35.4 4.3 %collective-permute-start.6 = (f32[128,128]{1,0:T(8,128)S(1)}, f32[128,128]{1,0:T(8,128)S(1)}, u32[]{:S(2)}, u32[]{:S(2)}) collective-permute-start(f32[128,128]{1,0:T(8,128)S(1)} %get-tuple-element.49), channel_id=1, source_target_pairs={{0,2},{1,3},{2,0},{3,1},{4,6},{5,7},{6,4},{7,5},{8,10},{9,11},{10,... | collective-permute-start | bytes 196616 | tf_op jit(solution)/shard_map/ppermute | solution.py:280
  39.7 6.2 %collective-permute-start.7 = (f32[128,128]{1,0:T(8,128)S(1)}, f32[128,128]{1,0:T(8,128)S(1)}, u32[]{:S(2)}, u32[]{:S(2)}) collective-permute-start(f32[128,128]{1,0:T(8,128)S(1)} %shard_map.64.a_ref), channel_id=1, source_target_pairs={{0,8},{1,9},{2,10},{3,11},{4,12},{5,13},{6,14},{7,15},{8,0},{9,1},... | collective-permute-start | bytes 196616 | tf_op jit(solution)/shard_map/ppermute | solution.py:280
  45.9 4.3 %collective-permute-start.8 = (f32[128,128]{1,0:T(8,128)S(1)}, f32[128,128]{1,0:T(8,128)S(1)}, u32[]{:S(2)}, u32[]{:S(2)}) collective-permute-start(f32[128,128]{1,0:T(8,128)S(1)} %shard_map.65.mine_ref), channel_id=1, source_target_pairs={{0,2},{1,3},{2,0},{3,1},{4,6},{5,7},{6,4},{7,5},{8,10},{9,11},{10,... | collective-permute-start | bytes 196616 | tf_op jit(solution)/shard_map/ppermute | solution.py:280
  50.8 5.0 %collective-permute-start.9 = (f32[256,128]{1,0:T(8,128)S(1)}, f32[256,128]{1,0:T(8,128)S(1)}, u32[]{:S(2)}, u32[]{:S(2)}) collective-permute-start(f32[256,128]{1,0:T(8,128)S(1)} %shard_map.67.mine_ref), channel_id=1, source_target_pairs={{0,4},{1,5},{2,6},{3,7},{4,0},{5,1},{6,2},{7,3},{8,12},{9,13},{10,... | collective-permute-start | bytes 393224 | tf_op jit(solution)/shard_map/ppermute | solution.py:280
  56.4 1.6 %collective-permute-start.10 = (f32[512,128]{1,0:T(8,128)S(1)}, f32[512,128]{1,0:T(8,128)S(1)}, u32[]{:S(2)}, u32[]{:S(2)}) collective-permute-start(f32[512,128]{1,0:T(8,128)S(1)} %shard_map.68.mine_ref), channel_id=1, source_target_pairs={{0,1},{1,0},{2,3},{3,2},{4,5},{5,4},{6,7},{7,6},{8,9},{9,8},{10,11... | collective-permute-start | bytes 786440 | tf_op jit(solution)/shard_map/ppermute | solution.py:280

commit v2 on v1

--- a/solution.py
+++ b/solution.py
@@ -12,8 +12,7 @@
 BF16 = jnp.bfloat16
 NT = (((1,), (1,)), ((), ()))
 TOP = 14.0
-FLOPS_A = 500_000_000
-FLOPS_B = 500_000_000
+COSTS = (1_000, 1_000, 1_000, 500_000_000, 500_000_000)
 
 
 def roles(core):
@@ -133,9 +132,8 @@
 
 
 def inner_kernel(
-    core_ref, cot_ref, w_ref, own_ref, inner_ref, vg_part_ref,
-    own_t_ref, inner_t_ref, wg_ref, vg_ref, partial_ref,
-    plane_ref, even_ref, odd_ref, vg_blocks, partial_blocks, taps_ref, sems,
+    core_ref, cot_ref, w_ref, vg_part_ref, taps_ref, vg_ref, partial_ref,
+    plane_ref, even_ref, odd_ref, vg_blocks, partial_blocks, sems,
 ):
     dout, ny2, _ = plane_ref.shape
     ny, group, chans = ny2 // 2, 4 * dout, w_ref.shape[2]
@@ -143,40 +141,47 @@
     copies = fetches(cot_ref, side, plane_ref, sems)
     for copy in copies:
         copy.start()
-    rows_by_y(own_ref, vg_blocks, own_t_ref, ny)
-    rows_by_y(inner_ref, partial_blocks, inner_t_ref, ny)
     weights = grad_weights(w_ref, own, nbr)
     tap_rows(copies, plane_ref, even_ref, odd_ref, taps_ref)
     for y in range(ny):
-        taps = taps_ref[y * 2 * group : (y * 2 + 4) * group, :]
-        sums = dot(weights, taps)
+        sums = dot(weights, taps_ref[y * 2 * group : (y * 2 + 4) * group, :])
         store_rows(vg_blocks, y, ny, sums[:chans])
         store_rows(partial_blocks, y, ny, sums[chans:])
-        cells = jnp.concatenate([r[y * chans : (y + 1) * chans, :] for r in (own_t_ref, inner_t_ref)], 0)
-        grads = lax.dot_general(taps, cells, NT, preferred_element_type=F32)
-        wg_ref[...] = grads if y == 0 else wg_ref[...] + grads
     for b in range(vg_blocks.shape[0]):
         at = slice(128 * b, 128 * b + 128)
         vg_ref[:, at] = vg_part_ref[:, at] + vg_blocks[b]
     flatten(partial_blocks, partial_ref)
 
 
+def tap_sums(taps_ref, own_t_ref, nbr_t_ref, sum_ref, before_ref):
+    rows, chans = sum_ref.shape[0], sum_ref.shape[1] // 2
+    for y in range(own_t_ref.shape[0] // chans):
+        taps = taps_ref[y * rows // 2 : y * rows // 2 + rows, :]
+        cells = jnp.concatenate([r[y * chans : (y + 1) * chans, :] for r in (own_t_ref, nbr_t_ref)], 0)
+        grads = lax.dot_general(taps, cells, NT, preferred_element_type=F32)
+        before = before_ref if y == 0 else sum_ref
+        sum_ref[...] = grads if before is None else before[...] + grads
+
+
+def inner_sums_kernel(taps_ref, own_ref, inner_ref, own_t_ref, inner_t_ref, wg_ref, wide_ref):
+    ny = own_ref.shape[0] * 2 // wg_ref.shape[1]
+    rows_by_y(own_ref, wide_ref, own_t_ref, ny)
+    rows_by_y(inner_ref, wide_ref, inner_t_ref, ny)
+    tap_sums(taps_ref, own_t_ref, inner_t_ref, wg_ref, None)
+
+
 def split(bit, whole_ref, keep_ref, send_ref):
     half = keep_ref.shape[0]
     keep_ref[...] = whole_ref[pl.ds(pl.multiple_of(bit * half, half), half), :]
     send_ref[...] = whole_ref[pl.ds(pl.multiple_of((1 - bit) * half, half), half), :]
 
 
-def second_kernel(bits_ref, taps_ref, own_t_ref, outer_ref, arrived_ref, keep_ref, send_ref, outer_t_ref, wide_ref, sum_ref):
-    chans = arrived_ref.shape[1] // 2
-    ny = outer_ref.shape[0] // chans
-    rows = sum_ref.shape[0]
+def outer_sums_kernel(
+    bits_ref, taps_ref, own_t_ref, outer_ref, arrived_ref, keep_ref, send_ref, outer_t_ref, wide_ref, sum_ref
+):
+    ny = outer_ref.shape[0] * 2 // arrived_ref.shape[1]
     rows_by_y(outer_ref, wide_ref, outer_t_ref, ny)
-    for y in range(ny):
-        taps = taps_ref[y * rows // 2 : y * rows // 2 + rows, :]
-        cells = jnp.concatenate([r[y * chans : (y + 1) * chans, :] for r in (own_t_ref, outer_t_ref)], 0)
-        grads = lax.dot_general(taps, cells, NT, preferred_element_type=F32)
-        sum_ref[...] = (arrived_ref if y == 0 else sum_ref)[...] + grads
+    tap_sums(taps_ref, own_t_ref, outer_t_ref, sum_ref, arrived_ref)
     split(bits_ref[1], sum_ref, keep_ref, send_ref)
 
 
@@ -295,31 +300,43 @@
         [struct(taps_shape, BF16), wide_cells, struct((rows + 16, nz), F32)],
         work + [pltpu.VMEM(blocks_c, F32), pltpu.VMEM(blocks_c, F32), chunks],
         8,
+        flops=COSTS[0],
     )(bits, cotangent, kernels)
-    to_outer, vg_o = together(to_outer.astype(jnp.float16), vg_o)
+    to_outer = to_outer.astype(jnp.float16)
+
+    taps_i, vg, to_inner = call(
+        inner_kernel,
+        [SMEM, HBM, VMEM, VMEM],
+        [VMEM] * 3,
+        [struct(taps_shape, BF16), wide_cells, wide_cells],
+        work + [pltpu.VMEM(blocks_c, F32), pltpu.VMEM(blocks_c, F32), chunks],
+        8,
+        flops=COSTS[1],
+    )(bits, cotangent, kernels, vg_o)
+    to_outer, taps_i = together(to_outer, taps_i)
     from_outer = beyond(to_outer)
-
-    own_t, inner_t, wg_i, vg, to_inner = call(
-        inner_kernel,
-        [SMEM, HBM] + [VMEM] * 4,
-        [VMEM] * 5,
-        [cells, cells, struct((wide, 2 * chans), F32), wide_cells, wide_cells],
-        work + [pltpu.VMEM(blocks_c, F32), pltpu.VMEM(blocks_c, F32), pltpu.VMEM(taps_shape, BF16), chunks],
-        12,
-    )(bits, cotangent, kernels, own, inner, vg_o)
+    own_t, inner_t, wg_i = call(
+        inner_sums_kernel,
+        [VMEM] * 3,
+        [VMEM] * 3,
+        [cells, cells, struct((wide, 2 * chans), F32)],
+        [pltpu.VMEM(blocks_c, F32)],
+        4,
+        flops=COSTS[2],
+    )(taps_i, own, inner)
     wg_arrived = swap(wg_i, 1)
 
     def piece(n):
         return struct((wide // n, 2 * chans), F32)
 
     keep, send, outer_t = call(
-        second_kernel,
+        outer_sums_kernel,
         [SMEM] + [VMEM] * 4,
         [VMEM] * 3,
         [piece(2), piece(2), cells],
         [pltpu.VMEM(blocks_c, F32), pltpu.VMEM((wide, 2 * chans), F32)],
         6,
-        flops=FLOPS_A,
+        flops=COSTS[3],
     )(bits, taps_o, own_t, outer, wg_arrived)
 
     def fine(which, nbr_t, so_far):
@@ -331,7 +348,7 @@
             [struct(cotangent.shape, BF16)],
             work + [pltpu.SemaphoreType.DMA],
             8,
-            flops=FLOPS_B,
+            flops=COSTS[4],
             **more,
         )(bits, own_t, nbr_t, kernels, *([] if so_far is None else [so_far]))[0]
 
@@ -349,26 +366,29 @@
         whole = struct((2 * a.shape[0], a.shape[1]), F32)
         return call(functools.partial(join_kernel, which), [SMEM, VMEM, VMEM], [VMEM], [whole], [], 2)(bits, a, b)[0]
 
-    inner_t, keep = together(inner_t, keep)
+    def cell_grads(from_inner, from_outer):
+        return call(cells_kernel, [VMEM] * 3, [VMEM], [cells], [], 4)(vg, from_inner, from_outer)[0]
+
+    send, inner_t = together(send, inner_t)
     upsampled = fine(0, inner_t, None)
-    send, to_inner, upsampled, from_outer = together(send, to_inner, upsampled, from_outer)
-    from_inner = swap(to_inner, 1)
     if peers & (peers - 1) or peers < 8:
         groups = [[i for i in range(peers) if i % 2 == c] for c in range(2)]
         total = lax.psum(join(1, keep, send), "gx", axis_index_groups=groups)
         upsampled = fine(1, outer_t, upsampled)
-        (volume_grad,) = call(cells_kernel, [VMEM] * 3, [VMEM], [cells], [], 4)(vg, from_inner, from_outer.astype(F32))
+        volume_grad = cell_grads(swap(to_inner, 1), from_outer.astype(F32))
     else:
         keep, send = add_split(2, keep, swap(send, 4))
-        (volume_grad,) = call(cells_kernel, [VMEM] * 3, [VMEM], [cells], [], 4)(vg, from_inner, from_outer.astype(F32))
-        send, volume_grad = together(send, volume_grad)
+        send, upsampled, from_outer = together(send, upsampled, from_outer)
         mine = add(keep, swap(send, 2))
-        mine, outer_t = together(mine, outer_t)
+        mine, outer_t, to_inner, from_outer = together(mine, outer_t, to_inner, from_outer)
         upsampled = fine(1, outer_t, upsampled)
+        from_inner, from_outer = swap(to_inner, 1), from_outer.astype(F32)
         for k in range(3, peers.bit_length() - 1):
             mine = add(mine, swap(mine, 1 << k))
-        mine, upsampled = together(mine, upsampled)
+        mine, upsampled, from_inner, from_outer = together(mine, upsampled, from_inner, from_outer)
+        volume_grad = cell_grads(from_inner, from_outer)
         mine = join(2, mine, swap(mine, 2))
+        mine, volume_grad = together(mine, volume_grad)
         total = join(1, mine, swap(mine, 4))
     scale = 1.0 / math.sqrt(peers * planes * ny * nz)
     (weight_grad,) = call(

time: 60 us -> 55.9 us (0.932)
  starting transfers between devices: 18.6 us -> 12.8 us
  waiting for transfers between devices: 15.2 us -> 16.2 us
  Pallas kernels: 23.9 us -> 24.5 us
    ppermute x9, starting transfers between devices: 12.9 us -> 7.06 us  [swap(): return lax.ppermute(value, 'gx', [(i, i ^ k) for i in range(peers)])]
    pallas_call x3 -> x4, Pallas kernels: 8.63 us -> 9.32 us  [the longest x1 4.95 us: on_device(): call(inner_kernel, [SMEM, HBM, VMEM, VMEM], [VMEM] * 3, [struct(taps_shap...]
  transfers between devices with their start and end apart: 11 -> 11, of which waited for: 6 -> 8; matrix products, arithmetic and copies ran while one was open for 1% -> 1% of each run, Pallas kernels for 34% -> 39%
where the time goes in v2:
time: 55.9 us; the launch traced here: 55.7 us
  Pallas kernels  24.5 us (44%)
  waiting for transfers between devices  16.2 us (29%)
  starting transfers between devices  12.8 us (23%)
  local copies, waits for them, and re-layouts  1.06 us (2%)
  between operations  0.83 us (1%)
    ppermute x9, waiting for transfers between devices, swap(): return lax.ppermute(value, 'gx', [(i, i ^ k) for i in range(peers)])  15.7 us
    ppermute x9, starting transfers between devices, swap(): return lax.ppermute(value, 'gx', [(i, i ^ k) for i in range(peers)])  7.06 us
    pallas_call x2, Pallas kernels, fine(): call(functools.partial(fine_kernel, which), [SMEM, VMEM, VMEM, VMEM] + [H...  6.74 us
    ppermute x2, starting transfers between devices, beyond(): lax.ppermute(value, 'gx', [(i, (i + (1 if i % 2 else -1)) % peers) for i...  5.71 us
    pallas_call x1, Pallas kernels, on_device(): call(outer_kernel, [SMEM, HBM, VMEM], [VMEM] * 3, [struct(taps_shape, BF1...  5.03 us
    pallas_call x1, Pallas kernels, on_device(): call(inner_kernel, [SMEM, HBM, VMEM, VMEM], [VMEM] * 3, [struct(taps_shap...  4.95 us
    pallas_call x1, Pallas kernels, on_device(): call(outer_sums_kernel, [SMEM] + [VMEM] * 4, [VMEM] * 3, [piece(2), piece...  1.84 us
    pallas_call x1, Pallas kernels, on_device(): call(functools.partial(taps_kernel, scale), [SMEM, VMEM, VMEM], [VMEM], [...  1.73 us
  transfers between devices with their start and end apart: 11, of which 8 were waited for; matrix products, arithmetic and copies ran while one was open for 1% of the time, Pallas kernels for 39%

profile of v2, /device:TPU:0, one launch (start us, length us, event | category | flops | bytes accessed | tf_op | source)
XLA Modules:
  0.0 55.7 jit_solution(17834136452406035414)
XLA Ops:
  0.6 0.5 collective-permute-start
  1.1 5.6 %collective-permute-start.1 = (bf16[512,512]{1,0:T(8,128)(2,1)}, bf16[512,512]{1,0:T(8,128)(2,1)S(1)}, u32[]{:S(2)}, u32[]{:S(2)}) collective-permute-start(bf16[512,512]{1,0:T(8,128)(2,1)} %bitcast.18), channel_id=1, source_target_pairs={{0,15},{1,2},{2,1},{3,4},{4,3},{5,6},{6,5},{7,8},{8,7},{9,10},{10,... | collective-permute-start | bytes 1572872 | tf_op jit(solution)/shard_map/ppermute | solution.py:288
  6.9 1.0 %copy-done = bf16[4,4,4,64,32]{3,4,2,1,0:T(8,128)(2,1)S(1)} copy-done((bf16[4,4,4,64,32]{3,4,2,1,0:T(8,128)(2,1)S(1)}, bf16[4,4,4,64,32]{3,4,2,1,0:T(8,128)(2,1)}, u32[]{:S(2)}) %copy-start) | copy-done | bytes 262168
  7.9 5.0 %shard_map.58 = (bf16[2304,512]{1,0:T(8,128)(2,1)S(1)}, f32[512,512]{1,0:T(8,128)S(1)}, f32[528,512]{1,0:T(8,128)S(1)}) custom-call(s32[3]{0:T(128)S(1)} %pad_add_fusion.core_ref.bits_ref, bf16[32,2,16,1024]{3,2,1,0:T(8,128)(2,1)} %cot_ref.3, bf16[4,512,64]{2,1,0:T(8,128)(2,1)S(1)} %bitcast.13), custom_call_target="tpu_custom_call" | custom-call | flops 1000 | bytes 1000 | tf_op jit(solution)/shard_map/pallas_call | solution.py:296
  13.0 4.9 %shard_map.59 = (bf16[2304,512]{1,0:T(8,128)(2,1)S(1)}, f32[512,512]{1,0:T(8,128)S(1)}, f32[512,512]{1,0:T(8,128)S(1)}) custom-call(s32[3]{0:T(128)S(1)} %pad_add_fusion.core_ref.bits_ref, bf16[32,2,16,1024]{3,2,1,0:T(8,128)(2,1)} %cot_ref.3, bf16[4,512,64]{2,1,0:T(8,128)(2,1)S(1)} %bitcast.14, f32[512,512]{1,0:T(8,128)S(1)} %get-tuple-element.36.vg_part_ref), custom_call_target="tpu_custom_call" | custom-call | flops 1000 | bytes 1000 | tf_op jit(solution)/shard_map/pallas_call | solution.py:307
  18.1 1.6 %shard_map.60 = (bf16[512,512]{1,0:T(8,128)(2,1)S(1)}, bf16[512,512]{1,0:T(8,128)(2,1)S(1)}, f32[512,128]{1,0:T(8,128)S(1)}) custom-call(bf16[2304,512]{1,0:T(8,128)(2,1)S(1)} %get-tuple-element.38.taps_ref, bf16[512,512]{1,0:T(8,128)(2,1)S(1)} %bitcast.19, bf16[512,512]{1,0:T(8,128)(2,1)S(1)} %collective-permute-done.inner_ref), custom_call_target="tpu_custom_call" | custom-call | flops 1000 | bytes 1000 | tf_op jit(solution)/shard_map/pallas_call | solution.py:318
  19.8 1.5 %collective-permute-done.2.arrived_ref = f32[512,128]{1,0:T(8,128)S(1)} collective-permute-done((f32[512,128]{1,0:T(8,128)S(1)}, f32[512,128]{1,0:T(8,128)S(1)}, u32[]{:S(2)}, u32[]{:S(2)}) %collective-permute-start.2) | collective-permute-done | bytes 262176 | tf_op jit(solution)/shard_map/ppermute | solution.py:285
  21.3 1.8 %shard_map.61 = (f32[256,128]{1,0:T(8,128)S(1)}, f32[256,128]{1,0:T(8,128)S(1)}, bf16[512,512]{1,0:T(8,128)(2,1)S(1)}) custom-call(s32[3]{0:T(128)S(1)} %pad_add_fusion.core_ref.bits_ref, bf16[2304,512]{1,0:T(8,128)(2,1)S(1)} %get-tuple-element.34.taps_ref, bf16[512,512]{1,0:T(8,128)(2,1)S(1)} %get-tuple-element.39.own_t_ref, ...), custom_call_target="tpu_custom_call" | custom-call | flops 500000000 | bytes 1000 | tf_op jit(solution)/shard_map/pallas_call | solution.py:332
  23.3 3.4 %shard_map.63.refs_0_ = bf16[32,2,16,1024]{3,2,1,0:T(8,128)(2,1)} custom-call(s32[3]{0:T(128)S(1)} %pad_add_fusion.core_ref.bits_ref, bf16[512,512]{1,0:T(8,128)(2,1)S(1)} %get-tuple-element.39.own_t_ref, bf16[512,512]{1,0:T(8,128)(2,1)S(1)} %get-tuple-element.47.nbr_t_ref, bf16[4,512,64]{2,1,0:T(8,128)(2,1)S(1)} %bitcast.15), custom_call_target="tpu_custom_call" | custom-call | flops 500000000 | bytes 1000 | tf_op jit(solution)/shard_map/pallas_call | solution.py:344
  26.6 2.1 %collective-permute-done.3.b_ref = f32[256,128]{1,0:T(8,128)S(1)} collective-permute-done((f32[256,128]{1,0:T(8,128)S(1)}, f32[256,128]{1,0:T(8,128)S(1)}, u32[]{:S(2)}, u32[]{:S(2)}) %collective-permute-start.3) | collective-permute-done | bytes 131104 | tf_op jit(solution)/shard_map/ppermute | solution.py:285
  28.8 0.6 %shard_map.62 = (f32[128,128]{1,0:T(8,128)S(1)}, f32[128,128]{1,0:T(8,128)S(1)}) custom-call(s32[3]{0:T(128)S(1)} %pad_add_fusion.core_ref.bits_ref, f32[256,128]{1,0:T(8,128)S(1)} %get-tuple-element.41.a_ref, f32[256,128]{1,0:T(8,128)S(1)} %collective-permute-done.3.b_ref), custom_call_target="tpu_custom_call" | custom-call | flops 1000 | bytes 1000 | tf_op jit(solution)/shard_map/pallas_call | solution.py:360
  29.4 0.5 collective-permute-done.4
  29.9 3.7 %collective-permute-start.5 = (f32[128,128]{1,0:T(8,128)S(1)}, f32[128,128]{1,0:T(8,128)S(1)}, u32[]{:S(2)}, u32[]{:S(2)}) collective-permute-start(f32[128,128]{1,0:T(8,128)S(1)} %get-tuple-element.49), channel_id=1, source_target_pairs={{0,2},{1,3},{2,0},{3,1},{4,6},{5,7},{6,4},{7,5},{8,10},{9,11},{10,... | collective-permute-start | bytes 196616 | tf_op jit(solution)/shard_map/ppermute | solution.py:285
  33.6 2.3 %collective-permute-done.5.b_ref = f32[128,128]{1,0:T(8,128)S(1)} collective-permute-done((f32[128,128]{1,0:T(8,128)S(1)}, f32[128,128]{1,0:T(8,128)S(1)}, u32[]{:S(2)}, u32[]{:S(2)}) %collective-permute-start.5) | collective-permute-done | bytes 65568 | tf_op jit(solution)/shard_map/ppermute | solution.py:285
  36.6 3.4 %shard_map.66 = bf16[32,2,16,1024]{3,2,1,0:T(8,128)(2,1)} custom-call(s32[3]{0:T(128)S(1)} %pad_add_fusion.core_ref.bits_ref, bf16[512,512]{1,0:T(8,128)(2,1)S(1)} %get-tuple-element.39.own_t_ref, bf16[512,512]{1,0:T(8,128)(2,1)S(1)} %get-tuple-element.54.nbr_t_ref, bf16[4,512,64]{2,1,0:T(8,128)(2,1)S(1)} %bitcast.16, ...), custom_call_target="tpu_custom_call", output_to_operand_aliasing={{}: (4, {})} | custom-call | flops 500000000 | bytes 1000 | tf_op jit(solution)/shard_map/pallas_call | solution.py:344
  40.0 1.9 %collective-permute-done.6.b_ref = f32[128,128]{1,0:T(8,128)S(1)} collective-permute-done((f32[128,128]{1,0:T(8,128)S(1)}, f32[128,128]{1,0:T(8,128)S(1)}, u32[]{:S(2)}, u32[]{:S(2)}) %collective-permute-start.6) | collective-permute-done | bytes 65568 | tf_op jit(solution)/shard_map/ppermute | solution.py:285
  41.9 2.0 %collective-permute-start.8 = (f32[128,128]{1,0:T(8,128)S(1)}, f32[128,128]{1,0:T(8,128)S(1)}, u32[]{:S(2)}, u32[]{:S(2)}) collective-permute-start(f32[128,128]{1,0:T(8,128)S(1)} %shard_map.65.mine_ref), channel_id=1, source_target_pairs={{0,2},{1,3},{2,0},{3,1},{4,6},{5,7},{6,4},{7,5},{8,10},{9,11},{10,... | collective-permute-start | bytes 196616 | tf_op jit(solution)/shard_map/ppermute | solution.py:285
  43.9 0.9 %shard_map.68 = bf16[512,512]{1,0:T(8,128)(2,1)} custom-call(f32[512,512]{1,0:T(8,128)S(1)} %get-tuple-element.60.vg_ref, f32[512,512]{1,0:T(8,128)S(1)} %collective-permute-done.7.inner_ref, f32[528,512]{1,0:T(8,128)S(1)} %convert_element_type.7.outer_ref), custom_call_target="tpu_custom_call" | custom-call | flops 1000 | bytes 1000 | tf_op jit(solution)/shard_map/pallas_call | solution.py:370
  44.8 1.4 %collective-permute-done.8.there_ref = f32[128,128]{1,0:T(8,128)S(1)} collective-permute-done((f32[128,128]{1,0:T(8,128)S(1)}, f32[128,128]{1,0:T(8,128)S(1)}, u32[]{:S(2)}, u32[]{:S(2)}) %collective-permute-start.8) | collective-permute-done | bytes 65568 | tf_op jit(solution)/shard_map/ppermute | solution.py:285
  46.2 0.6 shard_map.67.mine_ref
  46.8 5.0 %collective-permute-done.9.there_ref = f32[256,128]{1,0:T(8,128)S(1)} collective-permute-done((f32[256,128]{1,0:T(8,128)S(1)}, f32[256,128]{1,0:T(8,128)S(1)}, u32[]{:S(2)}, u32[]{:S(2)}) %collective-permute-start.9) | collective-permute-done | bytes 131104 | tf_op jit(solution)/shard_map/ppermute | solution.py:285
  51.8 0.6 %shard_map.69.mine_ref = f32[512,128]{1,0:T(8,128)S(1)} custom-call(s32[3]{0:T(128)S(1)} %pad_add_fusion.core_ref.bits_ref, f32[256,128]{1,0:T(8,128)S(1)} %shard_map.67.mine_ref, f32[256,128]{1,0:T(8,128)S(1)} %collective-permute-done.9.there_ref), custom_call_target="tpu_custom_call" | custom-call | flops 1000 | bytes 1000 | tf_op jit(solution)/shard_map/pallas_call | solution.py:367
  52.4 1.5 %collective-permute-done.10.other_ref = f32[512,128]{1,0:T(8,128)S(1)} collective-permute-done((f32[512,128]{1,0:T(8,128)S(1)}, f32[512,128]{1,0:T(8,128)S(1)}, u32[]{:S(2)}, u32[]{:S(2)}) %collective-permute-start.10) | collective-permute-done | bytes 262176 | tf_op jit(solution)/shard_map/ppermute | solution.py:285
  54.0 1.7 %shard_map.70 = f32[4,512,64]{2,1,0:T(8,128)} custom-call(s32[3]{0:T(128)S(1)} %pad_add_fusion.core_ref.bits_ref, f32[512,128]{1,0:T(8,128)S(1)} %shard_map.69.mine_ref, f32[512,128]{1,0:T(8,128)S(1)} %collective-permute-done.10.other_ref), custom_call_target="tpu_custom_call" | custom-call | flops 1000 | bytes 1000 | tf_op jit(solution)/shard_map/pallas_call | solution.py:394
  (20 shorter events, 1.2 us)
Async XLA Ops:
  0.6 17.5 %collective-permute-start = (bf16[512,512]{1,0:T(8,128)(2,1)}, bf16[512,512]{1,0:T(8,128)(2,1)S(1)}, u32[]{:S(2)}, u32[]{:S(2)}) collective-permute-start(bf16[512,512]{1,0:T(8,128)(2,1)} %bitcast.17), channel_id=1, source_target_pairs={{0,1},{1,0},{2,3},{3,2},{4,5},{5,4},{6,7},{7,6},{8,9},{9,8},{10,11... | collective-permute-start | bytes 1572872 | tf_op jit(solution)/shard_map/ppermute | solution.py:285
  1.1 18.7 %collective-permute-start.1 = (bf16[512,512]{1,0:T(8,128)(2,1)}, bf16[512,512]{1,0:T(8,128)(2,1)S(1)}, u32[]{:S(2)}, u32[]{:S(2)}) collective-permute-start(bf16[512,512]{1,0:T(8,128)(2,1)} %bitcast.18), channel_id=1, source_target_pairs={{0,15},{1,2},{2,1},{3,4},{4,3},{5,6},{6,5},{7,8},{8,7},{9,10},{10,... | collective-permute-start | bytes 1572872 | tf_op jit(solution)/shard_map/ppermute | solution.py:288
  6.9 1.0 %copy-start = (bf16[4,4,4,64,32]{3,4,2,1,0:T(8,128)(2,1)S(1)}, bf16[4,4,4,64,32]{3,4,2,1,0:T(8,128)(2,1)}, u32[]{:S(2)}) copy-start(bf16[4,4,4,64,32]{3,4,2,1,0:T(8,128)(2,1)} %param.4) | copy-start | bytes 786436
  12.9 5.2 %copy-start.2 = (bf16[64,1,8,512]{3,2,1,0:T(8,128)(2,1)S(1)}, bf16[64,1,8,512]{3,2,1,0:T(8,128)(2,1)}, u32[]{:S(2)}) copy-start(bf16[64,1,8,512]{3,2,1,0:T(8,128)(2,1)} %param.3) | copy-start | bytes 1572868
  18.0 11.9 %collective-permute-start.4 = (f16[528,512]{1,0:T(8,128)(2,1)S(1)}, f16[528,512]{1,0:T(8,128)(2,1)S(1)}, u32[]{:S(2)}, u32[]{:S(2)}) collective-permute-start(f16[528,512]{1,0:T(8,128)(2,1)S(1)} %convert_element_type.6), channel_id=1, source_target_pairs={{0,15},{1,2},{2,1},{3,4},{4,3},{5,6},{6,5},{7,8},{8,7},{9,10},{10,... | collective-permute-start | bytes 1622024 | tf_op jit(solution)/shard_map/ppermute | solution.py:288
  19.7 3.5 %copy-start.1 = (bf16[4,4,4,64,32]{3,4,2,1,0:T(8,128)(2,1)S(1)}, bf16[4,4,4,64,32]{3,4,2,1,0:T(8,128)(2,1)}, u32[]{:S(2)}) copy-start(bf16[4,4,4,64,32]{3,4,2,1,0:T(8,128)(2,1)} %param.4) | copy-start | bytes 786436
  19.7 1.6 %collective-permute-start.2 = (f32[512,128]{1,0:T(8,128)S(1)}, f32[512,128]{1,0:T(8,128)S(1)}, u32[]{:S(2)}, u32[]{:S(2)}) collective-permute-start(f32[512,128]{1,0:T(8,128)S(1)} %get-tuple-element.40), channel_id=1, source_target_pairs={{0,1},{1,0},{2,3},{3,2},{4,5},{5,4},{6,7},{7,6},{8,9},{9,8},{10,11... | collective-permute-start | bytes 786440 | tf_op jit(solution)/shard_map/ppermute | solution.py:285
  23.2 5.6 %collective-permute-start.3 = (f32[256,128]{1,0:T(8,128)S(1)}, f32[256,128]{1,0:T(8,128)S(1)}, u32[]{:S(2)}, u32[]{:S(2)}) collective-permute-start(f32[256,128]{1,0:T(8,128)S(1)} %get-tuple-element.44), channel_id=1, source_target_pairs={{0,4},{1,5},{2,6},{3,7},{4,0},{5,1},{6,2},{7,3},{8,12},{9,13},{10,... | collective-permute-start | bytes 393224 | tf_op jit(solution)/shard_map/ppermute | solution.py:285
  29.9 6.0 %collective-permute-start.5 = (f32[128,128]{1,0:T(8,128)S(1)}, f32[128,128]{1,0:T(8,128)S(1)}, u32[]{:S(2)}, u32[]{:S(2)}) collective-permute-start(f32[128,128]{1,0:T(8,128)S(1)} %get-tuple-element.49), channel_id=1, source_target_pairs={{0,2},{1,3},{2,0},{3,1},{4,6},{5,7},{6,4},{7,5},{8,10},{9,11},{10,... | collective-permute-start | bytes 196616 | tf_op jit(solution)/shard_map/ppermute | solution.py:285
  36.0 5.9 %collective-permute-start.7 = (f32[512,512]{1,0:T(8,128)S(1)}, f32[512,512]{1,0:T(8,128)S(1)}, u32[]{:S(2)}, u32[]{:S(2)}) collective-permute-start(f32[512,512]{1,0:T(8,128)S(1)} %get-tuple-element.56), channel_id=1, source_target_pairs={{0,1},{1,0},{2,3},{3,2},{4,5},{5,4},{6,7},{7,6},{8,9},{9,8},{10,11... | collective-permute-start | bytes 3145736 | tf_op jit(solution)/shard_map/ppermute | solution.py:285
  36.0 5.8 %collective-permute-start.6 = (f32[128,128]{1,0:T(8,128)S(1)}, f32[128,128]{1,0:T(8,128)S(1)}, u32[]{:S(2)}, u32[]{:S(2)}) collective-permute-start(f32[128,128]{1,0:T(8,128)S(1)} %shard_map.64.a_ref), channel_id=1, source_target_pairs={{0,8},{1,9},{2,10},{3,11},{4,12},{5,13},{6,14},{7,15},{8,0},{9,1},... | collective-permute-start | bytes 196616 | tf_op jit(solution)/shard_map/ppermute | solution.py:285
  41.9 4.3 %collective-permute-start.8 = (f32[128,128]{1,0:T(8,128)S(1)}, f32[128,128]{1,0:T(8,128)S(1)}, u32[]{:S(2)}, u32[]{:S(2)}) collective-permute-start(f32[128,128]{1,0:T(8,128)S(1)} %shard_map.65.mine_ref), channel_id=1, source_target_pairs={{0,2},{1,3},{2,0},{3,1},{4,6},{5,7},{6,4},{7,5},{8,10},{9,11},{10,... | collective-permute-start | bytes 196616 | tf_op jit(solution)/shard_map/ppermute | solution.py:285
  46.7 5.0 %collective-permute-start.9 = (f32[256,128]{1,0:T(8,128)S(1)}, f32[256,128]{1,0:T(8,128)S(1)}, u32[]{:S(2)}, u32[]{:S(2)}) collective-permute-start(f32[256,128]{1,0:T(8,128)S(1)} %shard_map.67.mine_ref), channel_id=1, source_target_pairs={{0,4},{1,5},{2,6},{3,7},{4,0},{5,1},{6,2},{7,3},{8,12},{9,13},{10,... | collective-permute-start | bytes 393224 | tf_op jit(solution)/shard_map/ppermute | solution.py:285
  52.3 1.6 %collective-permute-start.10 = (f32[512,128]{1,0:T(8,128)S(1)}, f32[512,128]{1,0:T(8,128)S(1)}, u32[]{:S(2)}, u32[]{:S(2)}) collective-permute-start(f32[512,128]{1,0:T(8,128)S(1)} %shard_map.69.mine_ref), channel_id=1, source_target_pairs={{0,1},{1,0},{2,3},{3,2},{4,5},{5,4},{6,7},{7,6},{8,9},{9,8},{10,11... | collective-permute-start | bytes 786440 | tf_op jit(solution)/shard_map/ppermute | solution.py:285

commit v3 on v2

--- a/solution.py
+++ b/solution.py
@@ -10,15 +10,32 @@
 
 F32 = jnp.float32
 BF16 = jnp.bfloat16
+F16 = jnp.float16
 NT = (((1,), (1,)), ((), ()))
 TOP = 14.0
-COSTS = (1_000, 1_000, 1_000, 500_000_000, 500_000_000)
+TAIL = 16
+COSTS = (1_000, 1_000, 1_000, 1_000, 500_000_000)
 
 
 def roles(core):
     inner = (1 - core, 2 - core, 3 * core)
     outer = (core, 1 + core, 3 - 3 * core)
     return inner, outer
+
+
+def level_of(most):
+    return jnp.ceil(jnp.log2(jnp.maximum(jnp.max(most, axis=1, keepdims=True), 1e-30)))
+
+
+def shrink_into(value, out_ref):
+    level = level_of(jnp.max(jnp.abs(value), axis=0, keepdims=True))
+    out_ref[: value.shape[0], :] = value * jnp.exp2(TOP - level)
+    out_ref[value.shape[0] :, :] = jnp.broadcast_to(level, (TAIL, value.shape[1]))
+
+
+def grown(ref):
+    rows = ref.shape[0] - TAIL
+    return ref[:rows, :] * jnp.exp2(ref[rows : rows + 1, :] - TOP)
 
 
 def dot(a, b):
@@ -104,17 +121,19 @@
 
 
 def outer_kernel(
-    core_ref, cot_ref, w_ref, taps_ref, vg_ref, partial_ref,
-    plane_ref, even_ref, odd_ref, vg_blocks, partial_blocks, sems,
+    core_ref, cot_ref, w_hbm_ref, taps_ref, vg_ref, partial_ref,
+    plane_ref, even_ref, odd_ref, vg_blocks, partial_blocks, w_ref, sems, w_sem,
 ):
     dout, ny2, _ = plane_ref.shape
     ny, group, chans = ny2 // 2, 4 * dout, w_ref.shape[2]
     side, own, nbr = roles(core_ref[0])[1]
     copies = fetches(cot_ref, side, plane_ref, sems)
-    for copy in copies:
+    w_copy = pltpu.make_async_copy(w_hbm_ref, w_ref, w_sem)
+    for copy in copies + [w_copy]:
         copy.start()
+    tap_rows(copies, plane_ref, even_ref, odd_ref, taps_ref)
+    w_copy.wait()
     weights = grad_weights(w_ref, own, nbr)
-    tap_rows(copies, plane_ref, even_ref, odd_ref, taps_ref)
     most = jnp.zeros((chans, vg_ref.shape[1]), F32)
     for y in range(ny):
         sums = dot(weights, taps_ref[y * 2 * group : (y * 2 + 4) * group, :])
@@ -123,26 +142,42 @@
         most = jnp.maximum(most, jnp.abs(sums[chans:]))
     flatten(vg_blocks, vg_ref)
     rows = chans * ny
-    most = jnp.max(jnp.max(most, axis=0, keepdims=True), axis=1, keepdims=True)
-    level = jnp.ceil(jnp.log2(jnp.maximum(most, 1e-30)))
+    level = level_of(jnp.max(most, axis=0, keepdims=True))
     shrink = jnp.exp2(TOP - level)
     for b in range(partial_blocks.shape[0]):
         partial_ref[:rows, 128 * b : 128 * b + 128] = partial_blocks[b] * shrink
-    partial_ref[rows:, :] = jnp.broadcast_to(level, (partial_ref.shape[0] - rows, partial_ref.shape[1]))
-
-
-def inner_kernel(
-    core_ref, cot_ref, w_ref, vg_part_ref, taps_ref, vg_ref, partial_ref,
-    plane_ref, even_ref, odd_ref, vg_blocks, partial_blocks, sems,
+    partial_ref[rows:, :] = jnp.broadcast_to(level, (TAIL, partial_ref.shape[1]))
+
+
+def tap_sums(taps_ref, own_t_ref, nbr_t_ref, sum_ref, before_ref):
+    rows, chans = sum_ref.shape[0], sum_ref.shape[1] // 2
+    for y in range(own_t_ref.shape[0] // chans):
+        taps = taps_ref[y * rows // 2 : y * rows // 2 + rows, :]
+        cells = jnp.concatenate([r[y * chans : (y + 1) * chans, :] for r in (own_t_ref, nbr_t_ref)], 0)
+        grads = lax.dot_general(taps, cells, NT, preferred_element_type=F32)
+        before = before_ref if y == 0 else sum_ref
+        sum_ref[...] = grads if before is None else before[...] + grads
+
+
+def inner_sums_kernel(
+    core_ref, cot_ref, own_ref, inner_ref, taps_ref, own_t_ref, inner_t_ref, wg_ref,
+    plane_ref, even_ref, odd_ref, wide_ref, sems,
 ):
-    dout, ny2, _ = plane_ref.shape
-    ny, group, chans = ny2 // 2, 4 * dout, w_ref.shape[2]
-    side, own, nbr = roles(core_ref[0])[0]
-    copies = fetches(cot_ref, side, plane_ref, sems)
+    ny = plane_ref.shape[1] // 2
+    copies = fetches(cot_ref, roles(core_ref[0])[0][0], plane_ref, sems)
     for copy in copies:
         copy.start()
+    rows_by_y(own_ref, wide_ref, own_t_ref, ny)
+    rows_by_y(inner_ref, wide_ref, inner_t_ref, ny)
+    tap_rows(copies, plane_ref, even_ref, odd_ref, taps_ref)
+    tap_sums(taps_ref, own_t_ref, inner_t_ref, wg_ref, None)
+
+
+def inner_cells_kernel(core_ref, taps_ref, w_ref, vg_part_ref, vg_ref, partial_ref, vg_blocks, partial_blocks):
+    chans, dout = w_ref.shape[2], w_ref.shape[1] // 16
+    ny, group = vg_ref.shape[0] // chans, 4 * dout
+    _, own, nbr = roles(core_ref[0])[0]
     weights = grad_weights(w_ref, own, nbr)
-    tap_rows(copies, plane_ref, even_ref, odd_ref, taps_ref)
     for y in range(ny):
         sums = dot(weights, taps_ref[y * 2 * group : (y * 2 + 4) * group, :])
         store_rows(vg_blocks, y, ny, sums[:chans])
@@ -153,23 +188,6 @@
     flatten(partial_blocks, partial_ref)
 
 
-def tap_sums(taps_ref, own_t_ref, nbr_t_ref, sum_ref, before_ref):
-    rows, chans = sum_ref.shape[0], sum_ref.shape[1] // 2
-    for y in range(own_t_ref.shape[0] // chans):
-        taps = taps_ref[y * rows // 2 : y * rows // 2 + rows, :]
-        cells = jnp.concatenate([r[y * chans : (y + 1) * chans, :] for r in (own_t_ref, nbr_t_ref)], 0)
-        grads = lax.dot_general(taps, cells, NT, preferred_element_type=F32)
-        before = before_ref if y == 0 else sum_ref
-        sum_ref[...] = grads if before is None else before[...] + grads
-
-
-def inner_sums_kernel(taps_ref, own_ref, inner_ref, own_t_ref, inner_t_ref, wg_ref, wide_ref):
-    ny = own_ref.shape[0] * 2 // wg_ref.shape[1]
-    rows_by_y(own_ref, wide_ref, own_t_ref, ny)
-    rows_by_y(inner_ref, wide_ref, inner_t_ref, ny)
-    tap_sums(taps_ref, own_t_ref, inner_t_ref, wg_ref, None)
-
-
 def split(bit, whole_ref, keep_ref, send_ref):
     half = keep_ref.shape[0]
     keep_ref[...] = whole_ref[pl.ds(pl.multiple_of(bit * half, half), half), :]
@@ -185,35 +203,38 @@
     split(bits_ref[1], sum_ref, keep_ref, send_ref)
 
 
-def add_split_kernel(which, bits_ref, a_ref, b_ref, keep_ref, send_ref, sum_ref):
-    sum_ref[...] = a_ref[...] + b_ref[...]
-    split(bits_ref[which], sum_ref, keep_ref, send_ref)
-
-
-def add_kernel(a_ref, b_ref, out_ref):
-    out_ref[...] = a_ref[...] + b_ref[...]
-
-
-def join_kernel(which, bits_ref, mine_ref, there_ref, out_ref):
-    bit, half = bits_ref[which], mine_ref.shape[0]
+def add_kernel(travelled, a_ref, b_ref, out_ref):
+    shrink_into(grown(a_ref) + grown(b_ref) if travelled else a_ref[...] + b_ref[...], out_ref)
+
+
+def join_kernel(bits_ref, mine_ref, there_ref, out_ref):
+    bit, half = bits_ref[1], mine_ref.shape[0]
     out_ref[pl.ds(pl.multiple_of(bit * half, half), half), :] = mine_ref[...]
     out_ref[pl.ds(pl.multiple_of((1 - bit) * half, half), half), :] = there_ref[...]
 
 
-def taps_kernel(scale, bits_ref, mine_ref, other_ref, out_ref):
+def taps_kernel(scale, other, bits_ref, mine_ref, there_ref, *refs):
+    out_ref, planes_ref, sems = refs[-3:]
     chans = out_ref.shape[2]
-    core = bits_ref[0]
-    for ref, side in ((mine_ref, core), (other_ref, 1 - core)):
-        _, own, nbr = roles(side)[1]
-        both = ref[...] * scale
-        out_ref[own] = both[:, :chans]
-        out_ref[nbr] = both[:, chans:]
+    core, bit = bits_ref[0], bits_ref[1]
+    _, own, nbr = roles(1 - core if other else core)[1]
+    for ref, place in ((mine_ref, bit), (there_ref, 1 - bit)):
+        both = grown(ref) * scale
+        half = both.shape[0]
+        at = pl.ds(pl.multiple_of(place * half, half), half)
+        planes_ref[0, at, :] = both[:, :chans]
+        planes_ref[1, at, :] = both[:, chans:]
+    copies = [
+        pltpu.make_async_copy(planes_ref.at[i], out_ref.at[plane], sems.at[i]) for i, plane in enumerate((own, nbr))
+    ]
+    for copy in copies:
+        copy.start()
+    for copy in copies:
+        copy.wait()
 
 
 def cells_kernel(vg_ref, inner_ref, outer_ref, out_ref):
-    rows = vg_ref.shape[0]
-    grow = jnp.exp2(outer_ref[rows : rows + 1, :] - TOP)
-    out_ref[...] = (vg_ref[...] + inner_ref[...] + outer_ref[:rows, :] * grow).astype(BF16)
+    out_ref[...] = (vg_ref[...] + inner_ref[...] + grown(outer_ref)).astype(BF16)
 
 
 def fine_kernel(which, core_ref, own_t_ref, nbr_t_ref, w_ref, *refs):
@@ -295,49 +316,40 @@
 
     taps_o, vg_o, to_outer = call(
         outer_kernel,
-        [SMEM, HBM, VMEM],
+        [SMEM, HBM, HBM],
         [VMEM] * 3,
-        [struct(taps_shape, BF16), wide_cells, struct((rows + 16, nz), F32)],
-        work + [pltpu.VMEM(blocks_c, F32), pltpu.VMEM(blocks_c, F32), chunks],
-        8,
+        [struct(taps_shape, BF16), wide_cells, struct((rows + TAIL, nz), F32)],
+        work + [pltpu.VMEM(blocks_c, F32), pltpu.VMEM(blocks_c, F32), pltpu.VMEM(kernels.shape, BF16), chunks, pltpu.SemaphoreType.DMA],
+        10,
         flops=COSTS[0],
-    )(bits, cotangent, kernels)
-    to_outer = to_outer.astype(jnp.float16)
-
-    taps_i, vg, to_inner = call(
-        inner_kernel,
+    )(bits, cotangent, pltpu.with_memory_space_constraint(kernels, pltpu.HBM))
+    to_outer = to_outer.astype(F16)
+    own, vg_o = together(own, vg_o)
+
+    taps_i, own_t, inner_t, wg_i = call(
+        inner_sums_kernel,
         [SMEM, HBM, VMEM, VMEM],
-        [VMEM] * 3,
-        [struct(taps_shape, BF16), wide_cells, wide_cells],
-        work + [pltpu.VMEM(blocks_c, F32), pltpu.VMEM(blocks_c, F32), chunks],
+        [VMEM] * 4,
+        [struct(taps_shape, BF16), cells, cells, struct((wide, 2 * chans), F32)],
+        work + [pltpu.VMEM(blocks_c, F32), chunks],
         8,
         flops=COSTS[1],
-    )(bits, cotangent, kernels, vg_o)
+    )(bits, cotangent, own, inner)
+    wg_arrived = swap(wg_i, 1)
     to_outer, taps_i = together(to_outer, taps_i)
     from_outer = beyond(to_outer)
-    own_t, inner_t, wg_i = call(
-        inner_sums_kernel,
-        [VMEM] * 3,
-        [VMEM] * 3,
-        [cells, cells, struct((wide, 2 * chans), F32)],
-        [pltpu.VMEM(blocks_c, F32)],
-        4,
+    vg, to_inner = call(
+        inner_cells_kernel,
+        [SMEM, VMEM, VMEM, VMEM],
+        [VMEM] * 2,
+        [wide_cells, wide_cells],
+        [pltpu.VMEM(blocks_c, F32), pltpu.VMEM(blocks_c, F32)],
+        6,
         flops=COSTS[2],
-    )(taps_i, own, inner)
-    wg_arrived = swap(wg_i, 1)
+    )(bits, taps_i, kernels, vg_o)
 
     def piece(n):
         return struct((wide // n, 2 * chans), F32)
-
-    keep, send, outer_t = call(
-        outer_sums_kernel,
-        [SMEM] + [VMEM] * 4,
-        [VMEM] * 3,
-        [piece(2), piece(2), cells],
-        [pltpu.VMEM(blocks_c, F32), pltpu.VMEM((wide, 2 * chans), F32)],
-        6,
-        flops=COSTS[3],
-    )(bits, taps_o, own_t, outer, wg_arrived)
 
     def fine(which, nbr_t, so_far):
         more = {} if so_far is None else {"input_output_aliases": {4: 0}}
@@ -352,19 +364,21 @@
             **more,
         )(bits, own_t, nbr_t, kernels, *([] if so_far is None else [so_far]))[0]
 
-    def add(a, b):
-        return call(add_kernel, [VMEM] * 2, [VMEM], [struct(a.shape, F32)], [], 2)(a, b)[0]
-
-    def add_split(which, a, b):
-        half = struct((a.shape[0] // 2, a.shape[1]), F32)
-        return call(
-            functools.partial(add_split_kernel, which),
-            [SMEM, VMEM, VMEM], [VMEM] * 2, [half, half], [pltpu.VMEM(a.shape, F32)], 2,
-        )(bits, a, b)
-
-    def join(which, a, b):
-        whole = struct((2 * a.shape[0], a.shape[1]), F32)
-        return call(functools.partial(join_kernel, which), [SMEM, VMEM, VMEM], [VMEM], [whole], [], 2)(bits, a, b)[0]
+    own_t, vg = together(own_t, vg)
+    keep, send, outer_t = call(
+        outer_sums_kernel,
+        [SMEM] + [VMEM] * 4,
+        [VMEM] * 3,
+        [piece(2), piece(2), cells],
+        [pltpu.VMEM(blocks_c, F32), pltpu.VMEM((wide, 2 * chans), F32)],
+        6,
+        flops=COSTS[3],
+    )(bits, taps_o, own_t, outer, wg_arrived)
+
+    def add(travelled, a, b):
+        rows = a.shape[0] + (0 if travelled else TAIL)
+        kernel = functools.partial(add_kernel, travelled)
+        return call(kernel, [VMEM] * 2, [VMEM], [struct((rows, a.shape[1]), F32)], [], 2)(a, b)[0].astype(F16)
 
     def cell_grads(from_inner, from_outer):
         return call(cells_kernel, [VMEM] * 3, [VMEM], [cells], [], 4)(vg, from_inner, from_outer)[0]
@@ -373,27 +387,42 @@
     upsampled = fine(0, inner_t, None)
     if peers & (peers - 1) or peers < 8:
         groups = [[i for i in range(peers) if i % 2 == c] for c in range(2)]
-        total = lax.psum(join(1, keep, send), "gx", axis_index_groups=groups)
+        total = call(join_kernel, [SMEM, VMEM, VMEM], [VMEM], [struct((wide, 2 * chans), F32)], [], 2)(bits, keep, send)
+        total = lax.psum(total[0], "gx", axis_index_groups=groups).reshape(2, wide // 2, 2 * chans)
+        mine, there = (lax.dynamic_index_in_dim(total, bit, 0, keepdims=False) for bit in (bits[1], 1 - bits[1]))
+        mine, there = (add(False, x, jnp.zeros_like(x)) for x in (mine, there))
+        other_mine = swap(mine, 1)
         upsampled = fine(1, outer_t, upsampled)
         volume_grad = cell_grads(swap(to_inner, 1), from_outer.astype(F32))
     else:
-        keep, send = add_split(2, keep, swap(send, 4))
-        send, upsampled, from_outer = together(send, upsampled, from_outer)
-        mine = add(keep, swap(send, 2))
-        mine, outer_t, to_inner, from_outer = together(mine, outer_t, to_inner, from_outer)
+        mine = add(False, keep, swap(send, 4))
+        mine, from_outer, to_inner, upsampled = together(mine, from_outer, to_inner, upsampled)
+        from_inner = swap(to_inner, 1)
+        mine = add(True, mine.astype(F32), swap(mine, 2).astype(F32))
+        mine, outer_t, from_inner, from_outer = together(mine, outer_t, from_inner, from_outer)
+        volume_grad = cell_grads(from_inner, from_outer.astype(F32))
         upsampled = fine(1, outer_t, upsampled)
-        from_inner, from_outer = swap(to_inner, 1), from_outer.astype(F32)
         for k in range(3, peers.bit_length() - 1):
-            mine = add(mine, swap(mine, 1 << k))
-        mine, upsampled, from_inner, from_outer = together(mine, upsampled, from_inner, from_outer)
-        volume_grad = cell_grads(from_inner, from_outer)
-        mine = join(2, mine, swap(mine, 2))
-        mine, volume_grad = together(mine, volume_grad)
-        total = join(1, mine, swap(mine, 4))
+            mine = add(True, mine.astype(F32), swap(mine, 1 << k).astype(F32))
+        mine, upsampled, volume_grad = together(mine, upsampled, volume_grad)
+        there = swap(mine, 4)
+        other_mine = swap(mine, 1)
     scale = 1.0 / math.sqrt(peers * planes * ny * nz)
-    (weight_grad,) = call(
-        functools.partial(taps_kernel, scale), [SMEM, VMEM, VMEM], [VMEM], [struct((4, wide, chans), F32)], [], 4
-    )(bits, total, swap(total, 1))
+
+    def taps(other, mine, there, so_far):
+        more = {} if so_far is None else {"input_output_aliases": {3: 0}}
+        return call(
+            functools.partial(taps_kernel, scale, other),
+            [SMEM, VMEM, VMEM] + [HBM] * (so_far is not None),
+            [HBM],
+            [struct((4, wide, chans), F32)],
+            [pltpu.VMEM((2, wide, chans), F32), pltpu.SemaphoreType.DMA((2,))],
+            4,
+            **more,
+        )(bits, mine.astype(F32), there.astype(F32), *([] if so_far is None else [so_far]))[0]
+
+    other_there = swap(there, 1)
+    weight_grad = taps(True, other_mine, other_there, taps(False, mine, there, None))
     weight_grad = jnp.transpose(weight_grad.reshape(4, 4, 4, dout, chans), (0, 1, 2, 4, 3))
     return (upsampled, volume_grad.reshape(volume.shape), weight_grad)
 

time: 55.9 us -> 49.8 us (0.89)
  starting transfers between devices: 12.8 us -> 9.65 us
  waiting for transfers between devices: 16.2 us -> 13.7 us
  local copies, waits for them, and re-layouts: 1.06 us -> 0.01 us
    ppermute x9, waiting for transfers between devices: 15.7 us -> 11 us  [swap(): return lax.ppermute(value, 'gx', [(i, i ^ k) for i in range(peers)])]
    ppermute x9, starting transfers between devices: 7.06 us -> 3.94 us  [swap(): return lax.ppermute(value, 'gx', [(i, i ^ k) for i in range(peers)])]
    ppermute x2, waiting for transfers between devices: 0.54 us -> 2.74 us  [beyond(): lax.ppermute(value, 'gx', [(i, (i + (1 if i % 2 else -1)) % peers) for i...]
    unnamed x6 -> x4, local copies, waits for them, and re-layouts: 1.06 us -> 0.01 us
    pallas_call x9 -> x8, Pallas kernels: 15 us -> 15.4 us  [the longest x1 5.18 us: on_device(): call(outer_kernel, [SMEM, HBM, HBM], [VMEM] * 3, [struct(taps_shape, BF16...]
  transfers between devices with their start and end apart: 11 -> 11, of which waited for: 8 -> 5; matrix products, arithmetic and copies ran while one was open for 1% -> 1% of each run, Pallas kernels for 39% -> 45%
where the time goes in v3:
time: 49.8 us; the launch traced here: 49.6 us
  Pallas kernels  24.9 us (50%)
  waiting for transfers between devices  13.7 us (28%)
  starting transfers between devices  9.65 us (19%)
  between operations  0.89 us (2%)
    ppermute x9, waiting for transfers between devices, swap(): return lax.ppermute(value, 'gx', [(i, i ^ k) for i in range(peers)])  11 us
    pallas_call x2, Pallas kernels, fine(): call(functools.partial(fine_kernel, which), [SMEM, VMEM, VMEM, VMEM] + [H...  6.73 us
    ppermute x2, starting transfers between devices, beyond(): lax.ppermute(value, 'gx', [(i, (i + (1 if i % 2 else -1)) % peers) for i...  5.71 us
    pallas_call x1, Pallas kernels, on_device(): call(outer_kernel, [SMEM, HBM, HBM], [VMEM] * 3, [struct(taps_shape, BF16...  5.18 us
    pallas_call x1, Pallas kernels, on_device(): call(inner_sums_kernel, [SMEM, HBM, VMEM, VMEM], [VMEM] * 4, [struct(taps...  4.98 us
    ppermute x9, starting transfers between devices, swap(): return lax.ppermute(value, 'gx', [(i, i ^ k) for i in range(peers)])  3.94 us
    pallas_call x2, Pallas kernels, taps(): call(functools.partial(taps_kernel, scale, other), [SMEM, VMEM, VMEM] + [...  2.98 us
    ppermute x2, waiting for transfers between devices, beyond(): lax.ppermute(value, 'gx', [(i, (i + (1 if i % 2 else -1)) % peers) for i...  2.74 us
  transfers between devices with their start and end apart: 11, of which 5 were waited for; matrix products, arithmetic and copies ran while one was open for 1% of the time, Pallas kernels for 45%

profile of v3, /device:TPU:0, one launch (start us, length us, event | category | flops | bytes accessed | tf_op | source)
XLA Modules:
  0.0 49.6 jit_solution(16565816438744129202)
XLA Ops:
  0.6 0.5 %collective-permute-start = (bf16[512,512]{1,0:T(8,128)(2,1)}, bf16[512,512]{1,0:T(8,128)(2,1)S(1)}, u32[]{:S(2)}, u32[]{:S(2)}) collective-permute-start(bf16[512,512]{1,0:T(8,128)(2,1)} %bitcast.17), channel_id=1, source_target_pairs={{0,1},{1,0},{2,3},{3,2},{4,5},{5,4},{6,7},{7,6},{8,9},{9,8},{10,11... | collective-permute-start | bytes 1572872 | tf_op jit(solution)/shard_map/ppermute | solution.py:306
  1.1 5.6 %collective-permute-start.1 = (bf16[512,512]{1,0:T(8,128)(2,1)}, bf16[512,512]{1,0:T(8,128)(2,1)S(1)}, u32[]{:S(2)}, u32[]{:S(2)}) collective-permute-start(bf16[512,512]{1,0:T(8,128)(2,1)} %bitcast.18), channel_id=1, source_target_pairs={{0,15},{1,2},{2,1},{3,4},{4,3},{5,6},{6,5},{7,8},{8,7},{9,10},{10,... | collective-permute-start | bytes 1572872 | tf_op jit(solution)/shard_map/ppermute | solution.py:309
  6.9 5.2 %shard_map.58 = (bf16[2304,512]{1,0:T(8,128)(2,1)S(1)}, f32[512,512]{1,0:T(8,128)S(1)}, f32[528,512]{1,0:T(8,128)S(1)}) custom-call(s32[3]{0:T(128)S(1)} %pad_add_fusion.core_ref.bits_ref, bf16[32,2,16,1024]{3,2,1,0:T(8,128)(2,1)} %cot_ref.3, bf16[4,512,64]{2,1,0:T(8,128)(2,1)} %bitcast.13), custom_call_target="tpu_custom_call" | custom-call | flops 1000 | bytes 1000 | tf_op jit(solution)/shard_map/pallas_call | solution.py:317
  12.1 0.1 convert_element_type.39
  12.2 5.0 %shard_map.59 = (bf16[2304,512]{1,0:T(8,128)(2,1)S(1)}, bf16[512,512]{1,0:T(8,128)(2,1)S(1)}, bf16[512,512]{1,0:T(8,128)(2,1)S(1)}, f32[512,128]{1,0:T(8,128)S(1)}) custom-call(s32[3]{0:T(128)S(1)} %pad_add_fusion.core_ref.bits_ref, bf16[32,2,16,1024]{3,2,1,0:T(8,128)(2,1)} %cot_ref.3, bf16[512,512]{1,0:T(8,128)(2,1)S(1)} %bitcast.19, ...), custom_call_target="tpu_custom_call" | custom-call | flops 1000 | bytes 1000 | tf_op jit(solution)/shard_map/pallas_call | solution.py:329
  17.4 1.8 %shard_map.60 = (f32[512,512]{1,0:T(8,128)S(1)}, f32[512,512]{1,0:T(8,128)S(1)}) custom-call(s32[3]{0:T(128)S(1)} %pad_add_fusion.core_ref.bits_ref, bf16[2304,512]{1,0:T(8,128)(2,1)S(1)} %get-tuple-element.40.taps_ref, bf16[4,512,64]{2,1,0:T(8,128)(2,1)S(1)} %bitcast.14, f32[512,512]{1,0:T(8,128)S(1)} %get-tuple-element.41.vg_part_ref), custom_call_target="tpu_custom_call" | custom-call | flops 1000 | bytes 1000 | tf_op jit(solution)/shard_map/pallas_call | solution.py:341
  19.2 1.8 %shard_map.61 = (f32[256,128]{1,0:T(8,128)S(1)}, f32[256,128]{1,0:T(8,128)S(1)}, bf16[512,512]{1,0:T(8,128)(2,1)S(1)}) custom-call(s32[3]{0:T(128)S(1)} %pad_add_fusion.core_ref.bits_ref, bf16[2304,512]{1,0:T(8,128)(2,1)S(1)} %get-tuple-element.34.taps_ref, bf16[512,512]{1,0:T(8,128)(2,1)S(1)} %get-tuple-element.43.own_t_ref, ...), custom_call_target="tpu_custom_call" | custom-call | flops 1000 | bytes 1000 | tf_op jit(solution)/shard_map/pallas_call | solution.py:368
  21.2 3.4 %shard_map.63.refs_0_ = bf16[32,2,16,1024]{3,2,1,0:T(8,128)(2,1)} custom-call(s32[3]{0:T(128)S(1)} %pad_add_fusion.core_ref.bits_ref, bf16[512,512]{1,0:T(8,128)(2,1)S(1)} %get-tuple-element.43.own_t_ref, bf16[512,512]{1,0:T(8,128)(2,1)S(1)} %get-tuple-element.51.nbr_t_ref, bf16[4,512,64]{2,1,0:T(8,128)(2,1)S(1)} %bitcast.15), custom_call_target="tpu_custom_call" | custom-call | flops 500000000 | bytes 1000 | tf_op jit(solution)/shard_map/pallas_call | solution.py:356
  24.5 2.6 %collective-permute-done.3.b_ref = f32[256,128]{1,0:T(8,128)S(1)} collective-permute-done((f32[256,128]{1,0:T(8,128)S(1)}, f32[256,128]{1,0:T(8,128)S(1)}, u32[]{:S(2)}, u32[]{:S(2)}) %collective-permute-start.3) | collective-permute-done | bytes 131104 | tf_op jit(solution)/shard_map/ppermute | solution.py:306
  27.1 0.1 shard_map.62
  27.2 2.7 %collective-permute-done.4 = f16[528,512]{1,0:T(8,128)(2,1)S(1)} collective-permute-done((f16[528,512]{1,0:T(8,128)(2,1)S(1)}, f16[528,512]{1,0:T(8,128)(2,1)S(1)}, u32[]{:S(2)}, u32[]{:S(2)}) %collective-permute-start.4) | collective-permute-done | bytes 540704 | tf_op jit(solution)/shard_map/ppermute | solution.py:309
  30.0 2.4 %collective-permute-start.5 = (f16[272,128]{1,0:T(8,128)(2,1)S(1)}, f16[272,128]{1,0:T(8,128)(2,1)S(1)}, u32[]{:S(2)}, u32[]{:S(2)}) collective-permute-start(f16[272,128]{1,0:T(8,128)(2,1)S(1)} %convert_element_type.40), channel_id=1, source_target_pairs={{0,2},{1,3},{2,0},{3,1},{4,6},{5,7},{6,4},{7,5},{8,10},{9,11},{10,... | collective-permute-start | bytes 208904 | tf_op jit(solution)/shard_map/ppermute | solution.py:306
  32.4 2.8 %collective-permute-done.5 = f16[272,128]{1,0:T(8,128)(2,1)S(1)} collective-permute-done((f16[272,128]{1,0:T(8,128)(2,1)S(1)}, f16[272,128]{1,0:T(8,128)(2,1)S(1)}, u32[]{:S(2)}, u32[]{:S(2)}) %collective-permute-start.5) | collective-permute-done | bytes 69664 | tf_op jit(solution)/shard_map/ppermute | solution.py:306
  35.2 0.1 shard_map.64
  35.4 0.7 %collective-permute-start.7 = (f16[272,128]{1,0:T(8,128)(2,1)S(1)}, f16[272,128]{1,0:T(8,128)(2,1)S(1)}, u32[]{:S(2)}, u32[]{:S(2)}) collective-permute-start(f16[272,128]{1,0:T(8,128)(2,1)S(1)} %convert_element_type.43), channel_id=1, source_target_pairs={{0,8},{1,9},{2,10},{3,11},{4,12},{5,13},{6,14},{7,15},{8,0},{9,1},... | collective-permute-start | bytes 208904 | tf_op jit(solution)/shard_map/ppermute | solution.py:306
  36.0 0.1 convert_element_type.47.outer_ref
  36.2 3.4 %shard_map.66 = bf16[32,2,16,1024]{3,2,1,0:T(8,128)(2,1)} custom-call(s32[3]{0:T(128)S(1)} %pad_add_fusion.core_ref.bits_ref, bf16[512,512]{1,0:T(8,128)(2,1)S(1)} %get-tuple-element.43.own_t_ref, bf16[512,512]{1,0:T(8,128)(2,1)S(1)} %get-tuple-element.57.nbr_t_ref, bf16[4,512,64]{2,1,0:T(8,128)(2,1)S(1)} %bitcast.16, ...), custom_call_target="tpu_custom_call", output_to_operand_aliasing={{}: (4, {})} | custom-call | flops 500000000 | bytes 1000 | tf_op jit(solution)/shard_map/pallas_call | solution.py:356
  39.5 1.5 %collective-permute-done.7 = f16[272,128]{1,0:T(8,128)(2,1)S(1)} collective-permute-done((f16[272,128]{1,0:T(8,128)(2,1)S(1)}, f16[272,128]{1,0:T(8,128)(2,1)S(1)}, u32[]{:S(2)}, u32[]{:S(2)}) %collective-permute-start.7) | collective-permute-done | bytes 69664 | tf_op jit(solution)/shard_map/ppermute | solution.py:306
  41.0 0.9 %shard_map.67 = bf16[512,512]{1,0:T(8,128)(2,1)} custom-call(f32[512,512]{1,0:T(8,128)S(1)} %get-tuple-element.59.vg_ref, f32[512,512]{1,0:T(8,128)S(1)} %collective-permute-done.6.inner_ref, f32[528,512]{1,0:T(8,128)S(1)} %convert_element_type.47.outer_ref), custom_call_target="tpu_custom_call" | custom-call | flops 1000 | bytes 1000 | tf_op jit(solution)/shard_map/pallas_call | solution.py:384
  42.0 0.1 shard_map.65
  42.1 0.2 collective-permute-start.9
  42.3 4.2 %collective-permute-done.9 = f16[272,128]{1,0:T(8,128)(2,1)S(1)} collective-permute-done((f16[272,128]{1,0:T(8,128)(2,1)S(1)}, f16[272,128]{1,0:T(8,128)(2,1)S(1)}, u32[]{:S(2)}, u32[]{:S(2)}) %collective-permute-start.9) | collective-permute-done | bytes 69664 | tf_op jit(solution)/shard_map/ppermute | solution.py:306
  46.5 1.5 %shard_map.68.refs_0_ = f32[4,512,64]{2,1,0:T(8,128)} custom-call(s32[3]{0:T(128)S(1)} %pad_add_fusion.core_ref.bits_ref, f32[272,128]{1,0:T(8,128)S(1)} %convert_element_type.50.mine_ref, f32[272,128]{1,0:T(8,128)S(1)} %convert_element_type.51.there_ref), custom_call_target="tpu_custom_call" | custom-call | flops 1000 | bytes 1000 | tf_op jit(solution)/shard_map/pallas_call | solution.py:414
  48.1 1.5 %shard_map.69 = f32[4,512,64]{2,1,0:T(8,128)} custom-call(s32[3]{0:T(128)S(1)} %pad_add_fusion.core_ref.bits_ref, f32[272,128]{1,0:T(8,128)S(1)} %convert_element_type.48.mine_ref, f32[272,128]{1,0:T(8,128)S(1)} %convert_element_type.49.there_ref, f32[4,512,64]{2,1,0:T(8,128)} %shard_map.68.refs_0_), custom_call_target="tpu_custom_call", output_to_operand_aliasing={{}: (3, {})} | custom-call | flops 1000 | bytes 1000 | tf_op jit(solution)/shard_map/pallas_call | solution.py:414
  (28 shorter events, 0.5 us)
Async XLA Ops:
  0.6 11.6 %collective-permute-start = (bf16[512,512]{1,0:T(8,128)(2,1)}, bf16[512,512]{1,0:T(8,128)(2,1)S(1)}, u32[]{:S(2)}, u32[]{:S(2)}) collective-permute-start(bf16[512,512]{1,0:T(8,128)(2,1)} %bitcast.17), channel_id=1, source_target_pairs={{0,1},{1,0},{2,3},{3,2},{4,5},{5,4},{6,7},{7,6},{8,9},{9,8},{10,11... | collective-permute-start | bytes 1572872 | tf_op jit(solution)/shard_map/ppermute | solution.py:306
  1.1 18.1 %collective-permute-start.1 = (bf16[512,512]{1,0:T(8,128)(2,1)}, bf16[512,512]{1,0:T(8,128)(2,1)S(1)}, u32[]{:S(2)}, u32[]{:S(2)}) collective-permute-start(bf16[512,512]{1,0:T(8,128)(2,1)} %bitcast.18), channel_id=1, source_target_pairs={{0,15},{1,2},{2,1},{3,4},{4,3},{5,6},{6,5},{7,8},{8,7},{9,10},{10,... | collective-permute-start | bytes 1572872 | tf_op jit(solution)/shard_map/ppermute | solution.py:309
  6.9 5.3 %copy-start.1 = (bf16[64,1,8,512]{3,2,1,0:T(8,128)(2,1)S(1)}, bf16[64,1,8,512]{3,2,1,0:T(8,128)(2,1)}, u32[]{:S(2)}) copy-start(bf16[64,1,8,512]{3,2,1,0:T(8,128)(2,1)} %param.3) | copy-start | bytes 1572868
  12.1 5.3 %copy-start = (bf16[4,4,4,64,32]{3,4,2,1,0:T(8,128)(2,1)S(1)}, bf16[4,4,4,64,32]{3,4,2,1,0:T(8,128)(2,1)}, u32[]{:S(2)}) copy-start(bf16[4,4,4,64,32]{3,4,2,1,0:T(8,128)(2,1)} %param.4) | copy-start | bytes 786436
  17.2 12.8 %collective-permute-start.4 = (f16[528,512]{1,0:T(8,128)(2,1)S(1)}, f16[528,512]{1,0:T(8,128)(2,1)S(1)}, u32[]{:S(2)}, u32[]{:S(2)}) collective-permute-start(f16[528,512]{1,0:T(8,128)(2,1)S(1)} %convert_element_type.39), channel_id=1, source_target_pairs={{0,15},{1,2},{2,1},{3,4},{4,3},{5,6},{6,5},{7,8},{8,7},{9,10},{10,... | collective-permute-start | bytes 1622024 | tf_op jit(solution)/shard_map/ppermute | solution.py:309
  17.3 2.0 %collective-permute-start.2 = (f32[512,128]{1,0:T(8,128)S(1)}, f32[512,128]{1,0:T(8,128)S(1)}, u32[]{:S(2)}, u32[]{:S(2)}) collective-permute-start(f32[512,128]{1,0:T(8,128)S(1)} %get-tuple-element.44), channel_id=1, source_target_pairs={{0,1},{1,0},{2,3},{3,2},{4,5},{5,4},{6,7},{7,6},{8,9},{9,8},{10,11... | collective-permute-start | bytes 786440 | tf_op jit(solution)/shard_map/ppermute | solution.py:306
  21.1 6.0 %collective-permute-start.3 = (f32[256,128]{1,0:T(8,128)S(1)}, f32[256,128]{1,0:T(8,128)S(1)}, u32[]{:S(2)}, u32[]{:S(2)}) collective-permute-start(f32[256,128]{1,0:T(8,128)S(1)} %get-tuple-element.48), channel_id=1, source_target_pairs={{0,4},{1,5},{2,6},{3,7},{4,0},{5,1},{6,2},{7,3},{8,12},{9,13},{10,... | collective-permute-start | bytes 393224 | tf_op jit(solution)/shard_map/ppermute | solution.py:306
  30.0 5.4 %collective-permute-start.6 = (f32[512,512]{1,0:T(8,128)S(1)}, f32[512,512]{1,0:T(8,128)S(1)}, u32[]{:S(2)}, u32[]{:S(2)}) collective-permute-start(f32[512,512]{1,0:T(8,128)S(1)} %get-tuple-element.54), channel_id=1, source_target_pairs={{0,1},{1,0},{2,3},{3,2},{4,5},{5,4},{6,7},{7,6},{8,9},{9,8},{10,11... | collective-permute-start | bytes 3145736 | tf_op jit(solution)/shard_map/ppermute | solution.py:306
  30.0 5.2 %collective-permute-start.5 = (f16[272,128]{1,0:T(8,128)(2,1)S(1)}, f16[272,128]{1,0:T(8,128)(2,1)S(1)}, u32[]{:S(2)}, u32[]{:S(2)}) collective-permute-start(f16[272,128]{1,0:T(8,128)(2,1)S(1)} %convert_element_type.40), channel_id=1, source_target_pairs={{0,2},{1,3},{2,0},{3,1},{4,6},{5,7},{6,4},{7,5},{8,10},{9,11},{10,... | collective-permute-start | bytes 208904 | tf_op jit(solution)/shard_map/ppermute | solution.py:306
  35.4 5.6 %collective-permute-start.7 = (f16[272,128]{1,0:T(8,128)(2,1)S(1)}, f16[272,128]{1,0:T(8,128)(2,1)S(1)}, u32[]{:S(2)}, u32[]{:S(2)}) collective-permute-start(f16[272,128]{1,0:T(8,128)(2,1)S(1)} %convert_element_type.43), channel_id=1, source_target_pairs={{0,8},{1,9},{2,10},{3,11},{4,12},{5,13},{6,14},{7,15},{8,0},{9,1},... | collective-permute-start | bytes 208904 | tf_op jit(solution)/shard_map/ppermute | solution.py:306
  42.1 4.4 %collective-permute-start.9 = (f16[272,128]{1,0:T(8,128)(2,1)S(1)}, f16[272,128]{1,0:T(8,128)(2,1)S(1)}, u32[]{:S(2)}, u32[]{:S(2)}) collective-permute-start(f16[272,128]{1,0:T(8,128)(2,1)S(1)} %convert_element_type.46), channel_id=1, source_target_pairs={{0,4},{1,5},{2,6},{3,7},{4,0},{5,1},{6,2},{7,3},{8,12},{9,13},{10,... | collective-permute-start | bytes 208904 | tf_op jit(solution)/shard_map/ppermute | solution.py:306
  42.3 5.7 %collective-permute-start.8 = (f16[272,128]{1,0:T(8,128)(2,1)S(1)}, f16[272,128]{1,0:T(8,128)(2,1)S(1)}, u32[]{:S(2)}, u32[]{:S(2)}) collective-permute-start(f16[272,128]{1,0:T(8,128)(2,1)S(1)} %convert_element_type.46), channel_id=1, source_target_pairs={{0,1},{1,0},{2,3},{3,2},{4,5},{5,4},{6,7},{7,6},{8,9},{9,8},{10,11... | collective-permute-start | bytes 208904 | tf_op jit(solution)/shard_map/ppermute | solution.py:306
  46.5 1.6 %collective-permute-start.10 = (f16[272,128]{1,0:T(8,128)(2,1)S(1)}, f16[272,128]{1,0:T(8,128)(2,1)S(1)}, u32[]{:S(2)}, u32[]{:S(2)}) collective-permute-start(f16[272,128]{1,0:T(8,128)(2,1)S(1)} %collective-permute-done.9), channel_id=1, source_target_pairs={{0,1},{1,0},{2,3},{3,2},{4,5},{5,4},{6,7},{7,6},{8,9},{9,8},{10,11... | collective-permute-start | bytes 208904 | tf_op jit(solution)/shard_map/ppermute | solution.py:306

commit v4 on v3

--- a/solution.py
+++ b/solution.py
@@ -14,7 +14,7 @@
 NT = (((1,), (1,)), ((), ()))
 TOP = 14.0
 TAIL = 16
-COSTS = (1_000, 1_000, 1_000, 1_000, 500_000_000)
+COSTS = (1_000, 1_000, 1_000, 1_000, 1_000, 1_000, 12_000_000_000, 3_500_000_000)
 
 
 def roles(core):
@@ -121,7 +121,7 @@
 
 
 def outer_kernel(
-    core_ref, cot_ref, w_hbm_ref, taps_ref, vg_ref, partial_ref,
+    core_ref, cot_ref, w_hbm_ref, taps_ref, vg_ref, low_ref, high_ref,
     plane_ref, even_ref, odd_ref, vg_blocks, partial_blocks, w_ref, sems, w_sem,
 ):
     dout, ny2, _ = plane_ref.shape
@@ -141,12 +141,15 @@
         store_rows(partial_blocks, y, ny, sums[chans:])
         most = jnp.maximum(most, jnp.abs(sums[chans:]))
     flatten(vg_blocks, vg_ref)
-    rows = chans * ny
     level = level_of(jnp.max(most, axis=0, keepdims=True))
     shrink = jnp.exp2(TOP - level)
-    for b in range(partial_blocks.shape[0]):
-        partial_ref[:rows, 128 * b : 128 * b + 128] = partial_blocks[b] * shrink
-    partial_ref[rows:, :] = jnp.broadcast_to(level, (TAIL, partial_ref.shape[1]))
+    start = 0
+    for ref in (low_ref, high_ref):
+        count = ref.shape[0] - TAIL
+        for b in range(partial_blocks.shape[0]):
+            ref[:count, 128 * b : 128 * b + 128] = partial_blocks[b, start : start + count, :] * shrink
+        ref[count:, :] = jnp.broadcast_to(level, (TAIL, ref.shape[1]))
+        start += count
 
 
 def tap_sums(taps_ref, own_t_ref, nbr_t_ref, sum_ref, before_ref):
@@ -188,53 +191,47 @@
     flatten(partial_blocks, partial_ref)
 
 
-def split(bit, whole_ref, keep_ref, send_ref):
-    half = keep_ref.shape[0]
-    keep_ref[...] = whole_ref[pl.ds(pl.multiple_of(bit * half, half), half), :]
-    send_ref[...] = whole_ref[pl.ds(pl.multiple_of((1 - bit) * half, half), half), :]
-
-
-def outer_sums_kernel(
-    bits_ref, taps_ref, own_t_ref, outer_ref, arrived_ref, keep_ref, send_ref, outer_t_ref, wide_ref, sum_ref
-):
+def outer_sums_kernel(taps_ref, own_t_ref, outer_ref, arrived_ref, send_ref, outer_t_ref, wide_ref, sum_ref):
     ny = outer_ref.shape[0] * 2 // arrived_ref.shape[1]
     rows_by_y(outer_ref, wide_ref, outer_t_ref, ny)
     tap_sums(taps_ref, own_t_ref, outer_t_ref, sum_ref, arrived_ref)
-    split(bits_ref[1], sum_ref, keep_ref, send_ref)
+    shrink_into(sum_ref[...], send_ref)
+
+
+def split_kernel(bits_ref, a_ref, b_ref, keep_ref, send_ref, sum_ref):
+    bit, half = bits_ref[1], keep_ref.shape[0]
+    sum_ref[...] = grown(a_ref) + grown(b_ref)
+    keep_ref[...] = sum_ref[pl.ds(pl.multiple_of(bit * half, half), half), :]
+    shrink_into(sum_ref[pl.ds(pl.multiple_of((1 - bit) * half, half), half), :], send_ref)
 
 
 def add_kernel(travelled, a_ref, b_ref, out_ref):
-    shrink_into(grown(a_ref) + grown(b_ref) if travelled else a_ref[...] + b_ref[...], out_ref)
-
-
-def join_kernel(bits_ref, mine_ref, there_ref, out_ref):
-    bit, half = bits_ref[1], mine_ref.shape[0]
-    out_ref[pl.ds(pl.multiple_of(bit * half, half), half), :] = mine_ref[...]
-    out_ref[pl.ds(pl.multiple_of((1 - bit) * half, half), half), :] = there_ref[...]
-
-
-def taps_kernel(scale, other, bits_ref, mine_ref, there_ref, *refs):
-    out_ref, planes_ref, sems = refs[-3:]
+    shrink_into((grown(a_ref) if travelled else a_ref[...]) + grown(b_ref), out_ref)
+
+
+def taps_kernel(scale, bits_ref, mine_ref, there_ref, other_mine_ref, other_there_ref, out_ref, planes_ref, sems):
     chans = out_ref.shape[2]
     core, bit = bits_ref[0], bits_ref[1]
-    _, own, nbr = roles(1 - core if other else core)[1]
-    for ref, place in ((mine_ref, bit), (there_ref, 1 - bit)):
-        both = grown(ref) * scale
-        half = both.shape[0]
-        at = pl.ds(pl.multiple_of(place * half, half), half)
-        planes_ref[0, at, :] = both[:, :chans]
-        planes_ref[1, at, :] = both[:, chans:]
-    copies = [
-        pltpu.make_async_copy(planes_ref.at[i], out_ref.at[plane], sems.at[i]) for i, plane in enumerate((own, nbr))
-    ]
-    for copy in copies:
-        copy.start()
+    copies = []
+    for i, (side, refs) in enumerate(((core, (mine_ref, there_ref)), (1 - core, (other_mine_ref, other_there_ref)))):
+        _, own, nbr = roles(side)[1]
+        for ref, place in zip(refs, (bit, 1 - bit)):
+            both = grown(ref) * scale
+            half = both.shape[0]
+            at = pl.ds(pl.multiple_of(place * half, half), half)
+            planes_ref[2 * i, at, :] = both[:, :chans]
+            planes_ref[2 * i + 1, at, :] = both[:, chans:]
+        for j, plane in ((2 * i, own), (2 * i + 1, nbr)):
+            copies.append(pltpu.make_async_copy(planes_ref.at[j], out_ref.at[plane], sems.at[j]))
+            copies[-1].start()
     for copy in copies:
         copy.wait()
 
 
-def cells_kernel(vg_ref, inner_ref, outer_ref, out_ref):
-    out_ref[...] = (vg_ref[...] + inner_ref[...] + grown(outer_ref)).astype(BF16)
+def cells_kernel(vg_ref, inner_ref, low_ref, high_ref, out_ref):
+    count = low_ref.shape[0] - TAIL
+    for at, ref in ((slice(0, count), low_ref), (slice(count, None), high_ref)):
+        out_ref[at, :] = (vg_ref[at, :] + inner_ref[at, :] + grown(ref)).astype(BF16)
 
 
 def fine_kernel(which, core_ref, own_t_ref, nbr_t_ref, w_ref, *refs):
@@ -257,13 +254,19 @@
             store_rows(even_ref, 2 * y + phase, ny2, even)
             store_rows(odd_ref, 2 * y + phase, ny2, odd)
     table = join_table()
-    for b in range(nz // 128):
-        halves = jnp.concatenate([even_ref[b].astype(BF16), odd_ref[b].astype(BF16)], 1)
-        fine = dot(halves, table).astype(BF16)
-        plane_ref[:, :, 256 * b : 256 * b + 256] = fine.reshape(dout, ny2, 256)
-    copy = pltpu.make_async_copy(plane_ref, out_ref.at[:, side], sem)
-    copy.start()
-    copy.wait()
+    chunk = dout // sem.shape[0]
+    copies = []
+    for i in range(sem.shape[0]):
+        at = slice(chunk * i * ny2, chunk * (i + 1) * ny2)
+        for b in range(nz // 128):
+            halves = jnp.concatenate([even_ref[b, at, :].astype(BF16), odd_ref[b, at, :].astype(BF16)], 1)
+            fine = dot(halves, table).astype(BF16)
+            plane_ref[chunk * i : chunk * (i + 1), :, 256 * b : 256 * b + 256] = fine.reshape(chunk, ny2, 256)
+        here = pl.ds(chunk * i, chunk)
+        copies.append(pltpu.make_async_copy(plane_ref.at[here], out_ref.at[here, side], sem.at[i]))
+        copies[-1].start()
+    for copy in copies:
+        copy.wait()
 
 
 VMEM = pl.BlockSpec(memory_space=pltpu.VMEM)
@@ -292,10 +295,12 @@
     chans, planes, ny, nz = volume.shape
     dout = cotangent.shape[0]
     peers = lax.axis_size("gx")
+    assert peers >= 16 and not peers & (peers - 1)
     me = lax.axis_index("gx")
     bits = jnp.stack([me & 1, (me >> 2) & 1, (me >> 1) & 1]).astype(jnp.int32)
     rows, wide, group = chans * ny, 16 * dout, 4 * dout
     struct = jax.ShapeDtypeStruct
+    early = rows * 3 // 128 * 16
     blocks_c, blocks_d = (nz // 128, rows, 128), (nz // 128, dout * 2 * ny, 128)
     taps_shape, plane_shape = ((2 * ny + 2) * group, nz), (dout, 2 * ny, 2 * nz)
     cells, wide_cells = struct((rows, nz), BF16), struct((rows, nz), F32)
@@ -314,16 +319,16 @@
     inner = swap(own, 1)
     kernels = jnp.transpose(weights, (0, 1, 2, 4, 3)).reshape(4, wide, chans)
 
-    taps_o, vg_o, to_outer = call(
+    taps_o, vg_o, low, high = call(
         outer_kernel,
         [SMEM, HBM, HBM],
-        [VMEM] * 3,
-        [struct(taps_shape, BF16), wide_cells, struct((rows + TAIL, nz), F32)],
+        [VMEM] * 4,
+        [struct(taps_shape, BF16), wide_cells] + [struct((part + TAIL, nz), F32) for part in (early, rows - early)],
         work + [pltpu.VMEM(blocks_c, F32), pltpu.VMEM(blocks_c, F32), pltpu.VMEM(kernels.shape, BF16), chunks, pltpu.SemaphoreType.DMA],
         10,
         flops=COSTS[0],
     )(bits, cotangent, pltpu.with_memory_space_constraint(kernels, pltpu.HBM))
-    to_outer = to_outer.astype(F16)
+    low = low.astype(F16)
     own, vg_o = together(own, vg_o)
 
     taps_i, own_t, inner_t, wg_i = call(
@@ -336,8 +341,8 @@
         flops=COSTS[1],
     )(bits, cotangent, own, inner)
     wg_arrived = swap(wg_i, 1)
-    to_outer, taps_i = together(to_outer, taps_i)
-    from_outer = beyond(to_outer)
+    low, taps_i = together(low, taps_i)
+    low = beyond(low)
     vg, to_inner = call(
         inner_cells_kernel,
         [SMEM, VMEM, VMEM, VMEM],
@@ -348,9 +353,6 @@
         flops=COSTS[2],
     )(bits, taps_i, kernels, vg_o)
 
-    def piece(n):
-        return struct((wide // n, 2 * chans), F32)
-
     def fine(which, nbr_t, so_far):
         more = {} if so_far is None else {"input_output_aliases": {4: 0}}
         return call(
@@ -358,71 +360,69 @@
             [SMEM, VMEM, VMEM, VMEM] + [HBM] * (so_far is not None),
             [HBM],
             [struct(cotangent.shape, BF16)],
-            work + [pltpu.SemaphoreType.DMA],
+            work + [chunks],
             8,
-            flops=COSTS[4],
+            flops=COSTS[4 + which],
             **more,
         )(bits, own_t, nbr_t, kernels, *([] if so_far is None else [so_far]))[0]
 
     own_t, vg = together(own_t, vg)
-    keep, send, outer_t = call(
+    send, outer_t = call(
         outer_sums_kernel,
-        [SMEM] + [VMEM] * 4,
-        [VMEM] * 3,
-        [piece(2), piece(2), cells],
+        [VMEM] * 4,
+        [VMEM] * 2,
+        [struct((wide + TAIL, 2 * chans), F32), cells],
         [pltpu.VMEM(blocks_c, F32), pltpu.VMEM((wide, 2 * chans), F32)],
         6,
         flops=COSTS[3],
-    )(bits, taps_o, own_t, outer, wg_arrived)
-
-    def add(travelled, a, b):
+    )(taps_o, own_t, outer, wg_arrived)
+    send = send.astype(F16)
+
+    def add(travelled, cost, a, b):
         rows = a.shape[0] + (0 if travelled else TAIL)
         kernel = functools.partial(add_kernel, travelled)
-        return call(kernel, [VMEM] * 2, [VMEM], [struct((rows, a.shape[1]), F32)], [], 2)(a, b)[0].astype(F16)
-
-    def cell_grads(from_inner, from_outer):
-        return call(cells_kernel, [VMEM] * 3, [VMEM], [cells], [], 4)(vg, from_inner, from_outer)[0]
+        return call(kernel, [VMEM] * 2, [VMEM], [struct((rows, a.shape[1]), F32)], [], 2, flops=cost)(a, b)[0].astype(F16)
 
     send, inner_t = together(send, inner_t)
+    there = swap(send, 2)
     upsampled = fine(0, inner_t, None)
-    if peers & (peers - 1) or peers < 8:
-        groups = [[i for i in range(peers) if i % 2 == c] for c in range(2)]
-        total = call(join_kernel, [SMEM, VMEM, VMEM], [VMEM], [struct((wide, 2 * chans), F32)], [], 2)(bits, keep, send)
-        total = lax.psum(total[0], "gx", axis_index_groups=groups).reshape(2, wide // 2, 2 * chans)
-        mine, there = (lax.dynamic_index_in_dim(total, bit, 0, keepdims=False) for bit in (bits[1], 1 - bits[1]))
-        mine, there = (add(False, x, jnp.zeros_like(x)) for x in (mine, there))
-        other_mine = swap(mine, 1)
-        upsampled = fine(1, outer_t, upsampled)
-        volume_grad = cell_grads(swap(to_inner, 1), from_outer.astype(F32))
-    else:
-        mine = add(False, keep, swap(send, 4))
-        mine, from_outer, to_inner, upsampled = together(mine, from_outer, to_inner, upsampled)
-        from_inner = swap(to_inner, 1)
-        mine = add(True, mine.astype(F32), swap(mine, 2).astype(F32))
-        mine, outer_t, from_inner, from_outer = together(mine, outer_t, from_inner, from_outer)
-        volume_grad = cell_grads(from_inner, from_outer.astype(F32))
-        upsampled = fine(1, outer_t, upsampled)
-        for k in range(3, peers.bit_length() - 1):
-            mine = add(True, mine.astype(F32), swap(mine, 1 << k).astype(F32))
-        mine, upsampled, volume_grad = together(mine, upsampled, volume_grad)
-        there = swap(mine, 4)
-        other_mine = swap(mine, 1)
+    there, upsampled = together(there, upsampled)
+    keep, send = call(
+        split_kernel,
+        [SMEM, VMEM, VMEM],
+        [VMEM] * 2,
+        [struct((wide // 2, 2 * chans), F32), struct((wide // 2 + TAIL, 2 * chans), F32)],
+        [pltpu.VMEM((wide, 2 * chans), F32)],
+        2,
+    )(bits, send.astype(F32), there.astype(F32))
+    send = send.astype(F16)
+    send, low, outer_t = together(send, low, outer_t)
+    mine = add(False, COSTS[6], keep, swap(send, 4).astype(F32))
+    mine, high, outer_t = together(mine, high.astype(F16), outer_t)
+    there = swap(mine, 8)
+    high = beyond(high)
+    upsampled = fine(1, outer_t, upsampled)
+    mine = add(True, COSTS[7], mine.astype(F32), there.astype(F32))
+    for k in range(4, peers.bit_length() - 1):
+        mine = add(True, COSTS[7], mine.astype(F32), swap(mine, 1 << k).astype(F32))
+    mine, upsampled = together(mine, upsampled)
+    from_inner = swap(to_inner, 1)
+    there = swap(mine, 4)
+    other_mine = swap(mine, 1)
+    (volume_grad,) = call(cells_kernel, [VMEM] * 4, [VMEM], [cells], [], 4)(
+        vg, from_inner, low.astype(F32), high.astype(F32)
+    )
+    there, volume_grad = together(there, volume_grad)
+    other_there = swap(there, 1)
     scale = 1.0 / math.sqrt(peers * planes * ny * nz)
-
-    def taps(other, mine, there, so_far):
-        more = {} if so_far is None else {"input_output_aliases": {3: 0}}
-        return call(
-            functools.partial(taps_kernel, scale, other),
-            [SMEM, VMEM, VMEM] + [HBM] * (so_far is not None),
-            [HBM],
-            [struct((4, wide, chans), F32)],
-            [pltpu.VMEM((2, wide, chans), F32), pltpu.SemaphoreType.DMA((2,))],
-            4,
-            **more,
-        )(bits, mine.astype(F32), there.astype(F32), *([] if so_far is None else [so_far]))[0]
-
-    other_there = swap(there, 1)
-    weight_grad = taps(True, other_mine, other_there, taps(False, mine, there, None))
+    (weight_grad,) = call(
+        functools.partial(taps_kernel, scale),
+        [SMEM] + [VMEM] * 4,
+        [HBM],
+        [struct((4, wide, chans), F32)],
+        [pltpu.VMEM((4, wide, chans), F32), pltpu.SemaphoreType.DMA((4,))],
+        4,
+    )(bits, *(value.astype(F32) for value in (mine, there, other_mine, other_there)))
     weight_grad = jnp.transpose(weight_grad.reshape(4, 4, 4, dout, chans), (0, 1, 2, 4, 3))
     return (upsampled, volume_grad.reshape(volume.shape), weight_grad)
 

time: 49.8 us -> 47.7 us (0.958)
  Pallas kernels: 24.9 us -> 23.3 us
  waiting for transfers between devices: 13.7 us -> 12.6 us
  starting transfers between devices: 9.65 us -> 10.2 us
    pallas_call x8 -> x7, Pallas kernels: 11.3 us -> 10.2 us  [the longest x1 5.17 us: on_device(): call(outer_kernel, [SMEM, HBM, HBM], [VMEM] * 4, [struct(taps_shape, BF16...]
    ppermute x9, waiting for transfers between devices: 11 us -> 9.92 us  [swap(): return lax.ppermute(value, 'gx', [(i, i ^ k) for i in range(peers)])]
    ppermute x2 -> x3, starting transfers between devices: 5.71 us -> 6.57 us  [beyond(): lax.ppermute(value, 'gx', [(i, (i + (1 if i % 2 else -1)) % peers) for i...]
    ppermute x2 -> x3, waiting for transfers between devices: 2.74 us -> 2.72 us  [beyond(): lax.ppermute(value, 'gx', [(i, (i + (1 if i % 2 else -1)) % peers) for i...]
  transfers between devices with their start and end apart: 11 -> 12, of which waited for: 5 -> 5; matrix products, arithmetic and copies ran while one was open for 1% -> 1% of each run, Pallas kernels for 45% -> 45%
where the time goes in v4:
time: 47.7 us; the launch traced here: 47.6 us
  Pallas kernels  23.3 us (49%)
  waiting for transfers between devices  12.6 us (26%)
  starting transfers between devices  10.2 us (21%)
  between operations  0.93 us (2%)
    ppermute x9, waiting for transfers between devices, swap(): return lax.ppermute(value, 'gx', [(i, i ^ k) for i in range(peers)])  9.92 us
    ppermute x3, starting transfers between devices, beyond(): lax.ppermute(value, 'gx', [(i, (i + (1 if i % 2 else -1)) % peers) for i...  6.57 us
    pallas_call x2, Pallas kernels, fine(): call(functools.partial(fine_kernel, which), [SMEM, VMEM, VMEM, VMEM] + [H...  6.29 us
    pallas_call x1, Pallas kernels, on_device(): call(outer_kernel, [SMEM, HBM, HBM], [VMEM] * 4, [struct(taps_shape, BF16...  5.17 us
    pallas_call x1, Pallas kernels, on_device(): call(inner_sums_kernel, [SMEM, HBM, VMEM, VMEM], [VMEM] * 4, [struct(taps...  4.97 us
    ppermute x9, starting transfers between devices, swap(): return lax.ppermute(value, 'gx', [(i, i ^ k) for i in range(peers)])  3.67 us
    ppermute x3, waiting for transfers between devices, beyond(): lax.ppermute(value, 'gx', [(i, (i + (1 if i % 2 else -1)) % peers) for i...  2.72 us
    pallas_call x1, Pallas kernels, on_device(): call(inner_cells_kernel, [SMEM, VMEM, VMEM, VMEM], [VMEM] * 2, [wide_cell...  1.86 us
  transfers between devices with their start and end apart: 12, of which 5 were waited for; matrix products, arithmetic and copies ran while one was open for 1% of the time, Pallas kernels for 45%

profile of v4, /device:TPU:0, one launch (start us, length us, event | category | flops | bytes accessed | tf_op | source)
XLA Modules:
  0.0 47.6 jit_solution(10490526297061927892)
XLA Ops:
  0.6 0.5 %collective-permute-start = (bf16[512,512]{1,0:T(8,128)(2,1)}, bf16[512,512]{1,0:T(8,128)(2,1)S(1)}, u32[]{:S(2)}, u32[]{:S(2)}) collective-permute-start(bf16[512,512]{1,0:T(8,128)(2,1)} %bitcast.17), channel_id=1, source_target_pairs={{0,1},{1,0},{2,3},{3,2},{4,5},{5,4},{6,7},{7,6},{8,9},{9,8},{10,11... | collective-permute-start | bytes 1572872 | tf_op jit(solution)/shard_map/ppermute | solution.py:311
  1.2 5.6 %collective-permute-start.1 = (bf16[512,512]{1,0:T(8,128)(2,1)}, bf16[512,512]{1,0:T(8,128)(2,1)S(1)}, u32[]{:S(2)}, u32[]{:S(2)}) collective-permute-start(bf16[512,512]{1,0:T(8,128)(2,1)} %bitcast.18), channel_id=1, source_target_pairs={{0,15},{1,2},{2,1},{3,4},{4,3},{5,6},{6,5},{7,8},{8,7},{9,10},{10,... | collective-permute-start | bytes 1572872 | tf_op jit(solution)/shard_map/ppermute | solution.py:314
  6.8 0.1 pad_add_fusion.core_ref.bits_ref
  6.9 5.2 %shard_map.58 = (bf16[2304,512]{1,0:T(8,128)(2,1)S(1)}, f32[512,512]{1,0:T(8,128)S(1)}, f32[208,512]{1,0:T(8,128)S(1)}, f32[336,512]{1,0:T(8,128)S(1)}) custom-call(s32[3]{0:T(128)S(1)} %pad_add_fusion.core_ref.bits_ref, bf16[32,2,16,1024]{3,2,1,0:T(8,128)(2,1)} %cot_ref.3, bf16[4,512,64]{2,1,0:T(8,128)(2,1)} %bitcast.13), custom_call_target="tpu_custom_call" | custom-call | flops 1000 | bytes 1000 | tf_op jit(solution)/shard_map/pallas_call | solution.py:322
  12.1 5.0 %shard_map.59 = (bf16[2304,512]{1,0:T(8,128)(2,1)S(1)}, bf16[512,512]{1,0:T(8,128)(2,1)S(1)}, bf16[512,512]{1,0:T(8,128)(2,1)S(1)}, f32[512,128]{1,0:T(8,128)S(1)}) custom-call(s32[3]{0:T(128)S(1)} %pad_add_fusion.core_ref.bits_ref, bf16[32,2,16,1024]{3,2,1,0:T(8,128)(2,1)} %cot_ref.3, bf16[512,512]{1,0:T(8,128)(2,1)S(1)} %bitcast.19, ...), custom_call_target="tpu_custom_call" | custom-call | flops 1000 | bytes 1000 | tf_op jit(solution)/shard_map/pallas_call | solution.py:334
  17.2 0.7 %collective-permute-start.4 = (f16[208,512]{1,0:T(8,128)(2,1)S(1)}, f16[208,512]{1,0:T(8,128)(2,1)S(1)}, u32[]{:S(2)}, u32[]{:S(2)}) collective-permute-start(f16[208,512]{1,0:T(8,128)(2,1)S(1)} %convert_element_type.51), channel_id=1, source_target_pairs={{0,15},{1,2},{2,1},{3,4},{4,3},{5,6},{6,5},{7,8},{8,7},{9,10},{10,... | collective-permute-start | bytes 638984 | tf_op jit(solution)/shard_map/ppermute | solution.py:314
  17.9 1.9 %shard_map.60 = (f32[512,512]{1,0:T(8,128)S(1)}, f32[512,512]{1,0:T(8,128)S(1)}) custom-call(s32[3]{0:T(128)S(1)} %pad_add_fusion.core_ref.bits_ref, bf16[2304,512]{1,0:T(8,128)(2,1)S(1)} %get-tuple-element.43.taps_ref, bf16[4,512,64]{2,1,0:T(8,128)(2,1)S(1)} %bitcast.14, f32[512,512]{1,0:T(8,128)S(1)} %get-tuple-element.44.vg_part_ref), custom_call_target="tpu_custom_call" | custom-call | flops 1000 | bytes 1000 | tf_op jit(solution)/shard_map/pallas_call | solution.py:346
  19.8 1.4 %shard_map.61 = (f32[528,128]{1,0:T(8,128)S(1)}, bf16[512,512]{1,0:T(8,128)(2,1)S(1)}) custom-call(bf16[2304,512]{1,0:T(8,128)(2,1)S(1)} %get-tuple-element.37.taps_ref, bf16[512,512]{1,0:T(8,128)(2,1)S(1)} %get-tuple-element.46.own_t_ref, bf16[512,512]{1,0:T(8,128)(2,1)S(1)} %collective-permute-done.1.outer_ref, ...), custom_call_target="tpu_custom_call" | custom-call | flops 1000 | bytes 1000 | tf_op jit(solution)/shard_map/pallas_call | solution.py:370
  21.2 1.6 %collective-permute-start.3 = (f16[528,128]{1,0:T(8,128)(2,1)S(1)}, f16[528,128]{1,0:T(8,128)(2,1)S(1)}, u32[]{:S(2)}, u32[]{:S(2)}) collective-permute-start(f16[528,128]{1,0:T(8,128)(2,1)S(1)} %convert_element_type.52), channel_id=1, source_target_pairs={{0,2},{1,3},{2,0},{3,1},{4,6},{5,7},{6,4},{7,5},{8,10},{9,11},{10,... | collective-permute-start | bytes 405512 | tf_op jit(solution)/shard_map/ppermute | solution.py:311
  22.8 3.1 %shard_map.62.refs_0_ = bf16[32,2,16,1024]{3,2,1,0:T(8,128)(2,1)} custom-call(s32[3]{0:T(128)S(1)} %pad_add_fusion.core_ref.bits_ref, bf16[512,512]{1,0:T(8,128)(2,1)S(1)} %get-tuple-element.46.own_t_ref, bf16[512,512]{1,0:T(8,128)(2,1)S(1)} %get-tuple-element.51.nbr_t_ref, bf16[4,512,64]{2,1,0:T(8,128)(2,1)S(1)} %bitcast.15), custom_call_target="tpu_custom_call" | custom-call | flops 1000 | bytes 1000 | tf_op jit(solution)/shard_map/pallas_call | solution.py:358
  25.9 2.4 %collective-permute-done.3 = f16[528,128]{1,0:T(8,128)(2,1)S(1)} collective-permute-done((f16[528,128]{1,0:T(8,128)(2,1)S(1)}, f16[528,128]{1,0:T(8,128)(2,1)S(1)}, u32[]{:S(2)}, u32[]{:S(2)}) %collective-permute-start.3) | collective-permute-done | bytes 135200 | tf_op jit(solution)/shard_map/ppermute | solution.py:311
  28.4 0.7 %shard_map.63 = (f32[256,128]{1,0:T(8,128)S(1)}, f32[272,128]{1,0:T(8,128)S(1)}) custom-call(s32[3]{0:T(128)S(1)} %pad_add_fusion.core_ref.bits_ref, f32[528,128]{1,0:T(8,128)S(1)} %convert_element_type.53.a_ref, f32[528,128]{1,0:T(8,128)S(1)} %convert_element_type.54.b_ref), custom_call_target="tpu_custom_call" | custom-call | flops 1000 | bytes 1000 | tf_op jit(solution)/shard_map/pallas_call | solution.py:390
  29.3 0.1 collective-permute-start.8
  29.4 4.2 %collective-permute-done.5 = f16[272,128]{1,0:T(8,128)(2,1)S(1)} collective-permute-done((f16[272,128]{1,0:T(8,128)(2,1)S(1)}, f16[272,128]{1,0:T(8,128)(2,1)S(1)}, u32[]{:S(2)}, u32[]{:S(2)}) %collective-permute-start.5) | collective-permute-done | bytes 69664 | tf_op jit(solution)/shard_map/ppermute | solution.py:311
  33.5 0.1 shard_map.64
  33.8 0.2 collective-permute-start.9
  34.0 3.2 %shard_map.66 = bf16[32,2,16,1024]{3,2,1,0:T(8,128)(2,1)} custom-call(s32[3]{0:T(128)S(1)} %pad_add_fusion.core_ref.bits_ref, bf16[512,512]{1,0:T(8,128)(2,1)S(1)} %get-tuple-element.46.own_t_ref, bf16[512,512]{1,0:T(8,128)(2,1)S(1)} %get-tuple-element.61.nbr_t_ref, bf16[4,512,64]{2,1,0:T(8,128)(2,1)S(1)} %bitcast.16, ...), custom_call_target="tpu_custom_call", output_to_operand_aliasing={{}: (4, {})} | custom-call | flops 1000 | bytes 1000 | tf_op jit(solution)/shard_map/pallas_call | solution.py:358
  37.2 2.1 %collective-permute-done.6 = f16[272,128]{1,0:T(8,128)(2,1)S(1)} collective-permute-done((f16[272,128]{1,0:T(8,128)(2,1)S(1)}, f16[272,128]{1,0:T(8,128)(2,1)S(1)}, u32[]{:S(2)}, u32[]{:S(2)}) %collective-permute-start.6) | collective-permute-done | bytes 69664 | tf_op jit(solution)/shard_map/ppermute | solution.py:311
  39.3 0.1 shard_map.65
  39.5 1.2 %collective-permute-start.7 = (f16[272,128]{1,0:T(8,128)(2,1)S(1)}, f16[272,128]{1,0:T(8,128)(2,1)S(1)}, u32[]{:S(2)}, u32[]{:S(2)}) collective-permute-start(f16[272,128]{1,0:T(8,128)(2,1)S(1)} %convert_element_type.61), channel_id=1, source_target_pairs={{0,4},{1,5},{2,6},{3,7},{4,0},{5,1},{6,2},{7,3},{8,12},{9,13},{10,... | collective-permute-start | bytes 208904 | tf_op jit(solution)/shard_map/ppermute | solution.py:311
  40.8 2.7 %collective-permute-done.9 = f16[336,512]{1,0:T(8,128)(2,1)S(1)} collective-permute-done((f16[336,512]{1,0:T(8,128)(2,1)S(1)}, f16[336,512]{1,0:T(8,128)(2,1)S(1)}, u32[]{:S(2)}, u32[]{:S(2)}) %collective-permute-start.9) | collective-permute-done | bytes 344096 | tf_op jit(solution)/shard_map/ppermute | solution.py:314
  43.7 0.9 %shard_map.67 = bf16[512,512]{1,0:T(8,128)(2,1)} custom-call(f32[512,512]{1,0:T(8,128)S(1)} %get-tuple-element.65.vg_ref, f32[512,512]{1,0:T(8,128)S(1)} %collective-permute-done.8.inner_ref, f32[208,512]{1,0:T(8,128)S(1)} %convert_element_type.62.low_ref, f32[336,512]{1,0:T(8,128)S(1)} %convert_element_type.63.high_ref), custom_call_target="tpu_custom_call" | custom-call | flops 1000 | bytes 1000 | tf_op jit(solution)/shard_map/pallas_call | solution.py:412
  44.7 1.2 %collective-permute-done.11 = f16[272,128]{1,0:T(8,128)(2,1)S(1)} collective-permute-done((f16[272,128]{1,0:T(8,128)(2,1)S(1)}, f16[272,128]{1,0:T(8,128)(2,1)S(1)}, u32[]{:S(2)}, u32[]{:S(2)}) %collective-permute-start.11) | collective-permute-done | bytes 69664 | tf_op jit(solution)/shard_map/ppermute | solution.py:311
  45.9 1.7 %shard_map.68 = f32[4,512,64]{2,1,0:T(8,128)} custom-call(s32[3]{0:T(128)S(1)} %pad_add_fusion.core_ref.bits_ref, f32[272,128]{1,0:T(8,128)S(1)} %convert_element_type.64.mine_ref, f32[272,128]{1,0:T(8,128)S(1)} %convert_element_type.65.there_ref, f32[272,128]{1,0:T(8,128)S(1)} %convert_element_type.66.other_mine_ref, ...), custom_call_target="tpu_custom_call" | custom-call | flops 1000 | bytes 1000 | tf_op jit(solution)/shard_map/pallas_call | solution.py:418
  (33 shorter events, 0.7 us)
Async XLA Ops:
  0.6 11.4 %copy-start.1 = (bf16[64,1,8,512]{3,2,1,0:T(8,128)(2,1)S(1)}, bf16[64,1,8,512]{3,2,1,0:T(8,128)(2,1)}, u32[]{:S(2)}) copy-start(bf16[64,1,8,512]{3,2,1,0:T(8,128)(2,1)} %param.3) | copy-start | bytes 1572868
  0.6 11.4 %collective-permute-start = (bf16[512,512]{1,0:T(8,128)(2,1)}, bf16[512,512]{1,0:T(8,128)(2,1)S(1)}, u32[]{:S(2)}, u32[]{:S(2)}) collective-permute-start(bf16[512,512]{1,0:T(8,128)(2,1)} %bitcast.17), channel_id=1, source_target_pairs={{0,1},{1,0},{2,3},{3,2},{4,5},{5,4},{6,7},{7,6},{8,9},{9,8},{10,11... | collective-permute-start | bytes 1572872 | tf_op jit(solution)/shard_map/ppermute | solution.py:311
  1.2 18.6 %collective-permute-start.1 = (bf16[512,512]{1,0:T(8,128)(2,1)}, bf16[512,512]{1,0:T(8,128)(2,1)S(1)}, u32[]{:S(2)}, u32[]{:S(2)}) collective-permute-start(bf16[512,512]{1,0:T(8,128)(2,1)} %bitcast.18), channel_id=1, source_target_pairs={{0,15},{1,2},{2,1},{3,4},{4,3},{5,6},{6,5},{7,8},{8,7},{9,10},{10,... | collective-permute-start | bytes 1572872 | tf_op jit(solution)/shard_map/ppermute | solution.py:314
  12.0 5.8 %copy-start = (bf16[4,4,4,64,32]{3,4,2,1,0:T(8,128)(2,1)S(1)}, bf16[4,4,4,64,32]{3,4,2,1,0:T(8,128)(2,1)}, u32[]{:S(2)}) copy-start(bf16[4,4,4,64,32]{3,4,2,1,0:T(8,128)(2,1)} %param.4) | copy-start | bytes 786436
  17.1 2.7 %collective-permute-start.2 = (f32[512,128]{1,0:T(8,128)S(1)}, f32[512,128]{1,0:T(8,128)S(1)}, u32[]{:S(2)}, u32[]{:S(2)}) collective-permute-start(f32[512,128]{1,0:T(8,128)S(1)} %get-tuple-element.47), channel_id=1, source_target_pairs={{0,1},{1,0},{2,3},{3,2},{4,5},{5,4},{6,7},{7,6},{8,9},{9,8},{10,11... | collective-permute-start | bytes 786440 | tf_op jit(solution)/shard_map/ppermute | solution.py:311
  17.2 12.0 %collective-permute-start.4 = (f16[208,512]{1,0:T(8,128)(2,1)S(1)}, f16[208,512]{1,0:T(8,128)(2,1)S(1)}, u32[]{:S(2)}, u32[]{:S(2)}) collective-permute-start(f16[208,512]{1,0:T(8,128)(2,1)S(1)} %convert_element_type.51), channel_id=1, source_target_pairs={{0,15},{1,2},{2,1},{3,4},{4,3},{5,6},{6,5},{7,8},{8,7},{9,10},{10,... | collective-permute-start | bytes 638984 | tf_op jit(solution)/shard_map/ppermute | solution.py:314
  21.2 7.2 %collective-permute-start.3 = (f16[528,128]{1,0:T(8,128)(2,1)S(1)}, f16[528,128]{1,0:T(8,128)(2,1)S(1)}, u32[]{:S(2)}, u32[]{:S(2)}) collective-permute-start(f16[528,128]{1,0:T(8,128)(2,1)S(1)} %convert_element_type.52), channel_id=1, source_target_pairs={{0,2},{1,3},{2,0},{3,1},{4,6},{5,7},{6,4},{7,5},{8,10},{9,11},{10,... | collective-permute-start | bytes 405512 | tf_op jit(solution)/shard_map/ppermute | solution.py:311
  29.1 4.4 %collective-permute-start.5 = (f16[272,128]{1,0:T(8,128)(2,1)S(1)}, f16[272,128]{1,0:T(8,128)(2,1)S(1)}, u32[]{:S(2)}, u32[]{:S(2)}) collective-permute-start(f16[272,128]{1,0:T(8,128)(2,1)S(1)} %convert_element_type.55), channel_id=1, source_target_pairs={{0,4},{1,5},{2,6},{3,7},{4,0},{5,1},{6,2},{7,3},{8,12},{9,13},{10,... | collective-permute-start | bytes 208904 | tf_op jit(solution)/shard_map/ppermute | solution.py:311
  29.3 14.4 %collective-permute-start.8 = (f32[512,512]{1,0:T(8,128)S(1)}, f32[512,512]{1,0:T(8,128)S(1)}, u32[]{:S(2)}, u32[]{:S(2)}) collective-permute-start(f32[512,512]{1,0:T(8,128)S(1)} %get-tuple-element.66), channel_id=1, source_target_pairs={{0,1},{1,0},{2,3},{3,2},{4,5},{5,4},{6,7},{7,6},{8,9},{9,8},{10,11... | collective-permute-start | bytes 3145736 | tf_op jit(solution)/shard_map/ppermute | solution.py:311
  33.7 5.6 %collective-permute-start.6 = (f16[272,128]{1,0:T(8,128)(2,1)S(1)}, f16[272,128]{1,0:T(8,128)(2,1)S(1)}, u32[]{:S(2)}, u32[]{:S(2)}) collective-permute-start(f16[272,128]{1,0:T(8,128)(2,1)S(1)} %convert_element_type.57), channel_id=1, source_target_pairs={{0,8},{1,9},{2,10},{3,11},{4,12},{5,13},{6,14},{7,15},{8,0},{9,1},... | collective-permute-start | bytes 208904 | tf_op jit(solution)/shard_map/ppermute | solution.py:311
  33.8 9.8 %collective-permute-start.9 = (f16[336,512]{1,0:T(8,128)(2,1)S(1)}, f16[336,512]{1,0:T(8,128)(2,1)S(1)}, u32[]{:S(2)}, u32[]{:S(2)}) collective-permute-start(f16[336,512]{1,0:T(8,128)(2,1)S(1)} %convert_element_type.58), channel_id=1, source_target_pairs={{0,15},{1,2},{2,1},{3,4},{4,3},{5,6},{6,5},{7,8},{8,7},{9,10},{10,... | collective-permute-start | bytes 1032200 | tf_op jit(solution)/shard_map/ppermute | solution.py:314
  39.5 5.1 %collective-permute-start.7 = (f16[272,128]{1,0:T(8,128)(2,1)S(1)}, f16[272,128]{1,0:T(8,128)(2,1)S(1)}, u32[]{:S(2)}, u32[]{:S(2)}) collective-permute-start(f16[272,128]{1,0:T(8,128)(2,1)S(1)} %convert_element_type.61), channel_id=1, source_target_pairs={{0,4},{1,5},{2,6},{3,7},{4,0},{5,1},{6,2},{7,3},{8,12},{9,13},{10,... | collective-permute-start | bytes 208904 | tf_op jit(solution)/shard_map/ppermute | solution.py:311
  40.8 3.9 %collective-permute-start.10 = (f16[272,128]{1,0:T(8,128)(2,1)S(1)}, f16[272,128]{1,0:T(8,128)(2,1)S(1)}, u32[]{:S(2)}, u32[]{:S(2)}) collective-permute-start(f16[272,128]{1,0:T(8,128)(2,1)S(1)} %convert_element_type.61), channel_id=1, source_target_pairs={{0,1},{1,0},{2,3},{3,2},{4,5},{5,4},{6,7},{7,6},{8,9},{9,8},{10,11... | collective-permute-start | bytes 208904 | tf_op jit(solution)/shard_map/ppermute | solution.py:311
  44.6 1.3 %collective-permute-start.11 = (f16[272,128]{1,0:T(8,128)(2,1)S(1)}, f16[272,128]{1,0:T(8,128)(2,1)S(1)}, u32[]{:S(2)}, u32[]{:S(2)}) collective-permute-start(f16[272,128]{1,0:T(8,128)(2,1)S(1)} %collective-permute-done.7), channel_id=1, source_target_pairs={{0,1},{1,0},{2,3},{3,2},{4,5},{5,4},{6,7},{7,6},{8,9},{9,8},{10,11... | collective-permute-start | bytes 208904 | tf_op jit(solution)/shard_map/ppermute | solution.py:311

commit v5 on v4

--- a/solution.py
+++ b/solution.py
@@ -14,7 +14,7 @@
 NT = (((1,), (1,)), ((), ()))
 TOP = 14.0
 TAIL = 16
-COSTS = (1_000, 1_000, 1_000, 1_000, 1_000, 1_000, 12_000_000_000, 3_500_000_000)
+COSTS = (1_000, 1_000, 1_000, 1_000, 1_000, 1_000, 8_000_000_000, 2_000_000_000, 1_000)
 
 
 def roles(core):
@@ -71,26 +71,17 @@
         target_ref[y * chans : (y + 1) * chans, :] = load_rows(wide_ref, y, chans, ny).astype(BF16)
 
 
-def fetches(cot_ref, side, plane_ref, sems):
-    chunk = plane_ref.shape[0] // sems.shape[0]
-    return [
-        pltpu.make_async_copy(
-            cot_ref.at[pl.ds(chunk * i, chunk), side], plane_ref.at[pl.ds(chunk * i, chunk)], sems.at[i]
-        )
-        for i in range(sems.shape[0])
-    ]
-
-
-def tap_rows(copies, plane_ref, even_ref, odd_ref, taps_ref):
-    dout, ny2, nz2 = plane_ref.shape
+def tap_rows(cot_ref, side, even_ref, odd_ref, taps_ref, copies=(None,)):
+    dout, _, ny2, nz2 = cot_ref.shape
     nz = nz2 // 2
     table = split_table()
     chunk = dout // len(copies)
     for i, copy in enumerate(copies):
-        copy.wait()
-        at = pl.ds(chunk * i * ny2, chunk * ny2)
+        if copy is not None:
+            copy.wait()
+        at = slice(chunk * i * ny2, chunk * (i + 1) * ny2)
         for b in range(nz2 // 256):
-            block = plane_ref[chunk * i : chunk * i + chunk, :, 256 * b : 256 * b + 256]
+            block = cot_ref[chunk * i : chunk * (i + 1), side, :, 256 * b : 256 * b + 256]
             halves = dot(block.reshape(chunk * ny2, 256), table)
             even_ref[b, at, :] = halves[:, :128]
             odd_ref[b, at, :] = halves[:, 128:]
@@ -104,7 +95,7 @@
             taps_ref[pl.ds(base + k * dout, dout), :] = piece.astype(BF16)
         return carry
 
-    lax.fori_loop(0, ny2, row, 0, unroll=4)
+    lax.fori_loop(0, ny2, row, 0, unroll=True)
     group = 4 * dout
     taps_ref[:group, :] = taps_ref[ny2 * group : (ny2 + 1) * group, :]
     taps_ref[(ny2 + 1) * group :, :] = taps_ref[group : 2 * group, :]
@@ -122,17 +113,22 @@
 
 def outer_kernel(
     core_ref, cot_ref, w_hbm_ref, taps_ref, vg_ref, low_ref, high_ref,
-    plane_ref, even_ref, odd_ref, vg_blocks, partial_blocks, w_ref, sems, w_sem,
+    plane_ref, even_ref, odd_ref, vg_blocks, partial_blocks, w_ref, sems,
 ):
-    dout, ny2, _ = plane_ref.shape
+    dout, _, ny2, _ = cot_ref.shape
     ny, group, chans = ny2 // 2, 4 * dout, w_ref.shape[2]
     side, own, nbr = roles(core_ref[0])[1]
-    copies = fetches(cot_ref, side, plane_ref, sems)
-    w_copy = pltpu.make_async_copy(w_hbm_ref, w_ref, w_sem)
-    for copy in copies + [w_copy]:
+    chunk = dout // 4
+    copies = [
+        pltpu.make_async_copy(
+            cot_ref.at[pl.ds(chunk * i, chunk), pl.ds(side, 1)], plane_ref.at[pl.ds(chunk * i, chunk)], sems.at[i]
+        )
+        for i in range(4)
+    ] + [pltpu.make_async_copy(w_hbm_ref, w_ref, sems.at[4])]
+    for copy in copies:
         copy.start()
-    tap_rows(copies, plane_ref, even_ref, odd_ref, taps_ref)
-    w_copy.wait()
+    tap_rows(plane_ref, 0, even_ref, odd_ref, taps_ref, copies[:4])
+    copies[4].wait()
     weights = grad_weights(w_ref, own, nbr)
     most = jnp.zeros((chans, vg_ref.shape[1]), F32)
     for y in range(ny):
@@ -163,16 +159,12 @@
 
 
 def inner_sums_kernel(
-    core_ref, cot_ref, own_ref, inner_ref, taps_ref, own_t_ref, inner_t_ref, wg_ref,
-    plane_ref, even_ref, odd_ref, wide_ref, sems,
+    core_ref, cot_ref, own_ref, inner_ref, taps_ref, own_t_ref, inner_t_ref, wg_ref, even_ref, odd_ref, wide_ref
 ):
-    ny = plane_ref.shape[1] // 2
-    copies = fetches(cot_ref, roles(core_ref[0])[0][0], plane_ref, sems)
-    for copy in copies:
-        copy.start()
+    ny = cot_ref.shape[2] // 2
     rows_by_y(own_ref, wide_ref, own_t_ref, ny)
     rows_by_y(inner_ref, wide_ref, inner_t_ref, ny)
-    tap_rows(copies, plane_ref, even_ref, odd_ref, taps_ref)
+    tap_rows(cot_ref, roles(core_ref[0])[0][0], even_ref, odd_ref, taps_ref)
     tap_sums(taps_ref, own_t_ref, inner_t_ref, wg_ref, None)
 
 
@@ -198,30 +190,19 @@
     shrink_into(sum_ref[...], send_ref)
 
 
-def split_kernel(bits_ref, a_ref, b_ref, keep_ref, send_ref, sum_ref):
-    bit, half = bits_ref[1], keep_ref.shape[0]
-    sum_ref[...] = grown(a_ref) + grown(b_ref)
-    keep_ref[...] = sum_ref[pl.ds(pl.multiple_of(bit * half, half), half), :]
-    shrink_into(sum_ref[pl.ds(pl.multiple_of((1 - bit) * half, half), half), :], send_ref)
-
-
-def add_kernel(travelled, a_ref, b_ref, out_ref):
-    shrink_into((grown(a_ref) if travelled else a_ref[...]) + grown(b_ref), out_ref)
-
-
-def taps_kernel(scale, bits_ref, mine_ref, there_ref, other_mine_ref, other_there_ref, out_ref, planes_ref, sems):
+def add_kernel(a_ref, b_ref, out_ref):
+    shrink_into(grown(a_ref) + grown(b_ref), out_ref)
+
+
+def taps_kernel(scale, bits_ref, mine_ref, other_ref, out_ref, planes_ref, sems):
     chans = out_ref.shape[2]
-    core, bit = bits_ref[0], bits_ref[1]
+    core = bits_ref[0]
     copies = []
-    for i, (side, refs) in enumerate(((core, (mine_ref, there_ref)), (1 - core, (other_mine_ref, other_there_ref)))):
+    for i, (side, ref) in enumerate(((core, mine_ref), (1 - core, other_ref))):
         _, own, nbr = roles(side)[1]
-        for ref, place in zip(refs, (bit, 1 - bit)):
-            both = grown(ref) * scale
-            half = both.shape[0]
-            at = pl.ds(pl.multiple_of(place * half, half), half)
-            planes_ref[2 * i, at, :] = both[:, :chans]
-            planes_ref[2 * i + 1, at, :] = both[:, chans:]
-        for j, plane in ((2 * i, own), (2 * i + 1, nbr)):
+        both = grown(ref) * scale
+        for j, plane, part in ((2 * i, own, both[:, :chans]), (2 * i + 1, nbr, both[:, chans:])):
+            planes_ref[j] = part
             copies.append(pltpu.make_async_copy(planes_ref.at[j], out_ref.at[plane], sems.at[j]))
             copies[-1].start()
     for copy in copies:
@@ -297,10 +278,10 @@
     peers = lax.axis_size("gx")
     assert peers >= 16 and not peers & (peers - 1)
     me = lax.axis_index("gx")
-    bits = jnp.stack([me & 1, (me >> 2) & 1, (me >> 1) & 1]).astype(jnp.int32)
+    bits = (me & 1).astype(jnp.int32).reshape(1)
     rows, wide, group = chans * ny, 16 * dout, 4 * dout
     struct = jax.ShapeDtypeStruct
-    early = rows * 3 // 128 * 16
+    early = rows // 512 * 16 * 12
     blocks_c, blocks_d = (nz // 128, rows, 128), (nz // 128, dout * 2 * ny, 128)
     taps_shape, plane_shape = ((2 * ny + 2) * group, nz), (dout, 2 * ny, 2 * nz)
     cells, wide_cells = struct((rows, nz), BF16), struct((rows, nz), F32)
@@ -313,7 +294,6 @@
     def beyond(value):
         return lax.ppermute(value, "gx", [(i, (i + (1 if i % 2 else -1)) % peers) for i in range(peers)])
 
-    cotangent = pltpu.with_memory_space_constraint(cotangent, pltpu.HBM)
     own = volume.reshape(rows, nz)
     outer = beyond(own)
     inner = swap(own, 1)
@@ -324,20 +304,21 @@
         [SMEM, HBM, HBM],
         [VMEM] * 4,
         [struct(taps_shape, BF16), wide_cells] + [struct((part + TAIL, nz), F32) for part in (early, rows - early)],
-        work + [pltpu.VMEM(blocks_c, F32), pltpu.VMEM(blocks_c, F32), pltpu.VMEM(kernels.shape, BF16), chunks, pltpu.SemaphoreType.DMA],
+        [pltpu.VMEM((dout, 1, 2 * ny, 2 * nz), BF16)] + work[1:]
+        + [pltpu.VMEM(blocks_c, F32), pltpu.VMEM(blocks_c, F32), pltpu.VMEM(kernels.shape, BF16), pltpu.SemaphoreType.DMA((5,))],
         10,
         flops=COSTS[0],
-    )(bits, cotangent, pltpu.with_memory_space_constraint(kernels, pltpu.HBM))
+    )(bits, *(pltpu.with_memory_space_constraint(value, pltpu.HBM) for value in (cotangent, kernels)))
     low = low.astype(F16)
     own, vg_o = together(own, vg_o)
 
     taps_i, own_t, inner_t, wg_i = call(
         inner_sums_kernel,
-        [SMEM, HBM, VMEM, VMEM],
+        [SMEM, VMEM, VMEM, VMEM],
         [VMEM] * 4,
         [struct(taps_shape, BF16), cells, cells, struct((wide, 2 * chans), F32)],
-        work + [pltpu.VMEM(blocks_c, F32), chunks],
-        8,
+        work[1:] + [pltpu.VMEM(blocks_c, F32)],
+        6,
         flops=COSTS[1],
     )(bits, cotangent, own, inner)
     wg_arrived = swap(wg_i, 1)
@@ -378,51 +359,40 @@
     )(taps_o, own_t, outer, wg_arrived)
     send = send.astype(F16)
 
-    def add(travelled, cost, a, b):
-        rows = a.shape[0] + (0 if travelled else TAIL)
-        kernel = functools.partial(add_kernel, travelled)
-        return call(kernel, [VMEM] * 2, [VMEM], [struct((rows, a.shape[1]), F32)], [], 2, flops=cost)(a, b)[0].astype(F16)
-
-    send, inner_t = together(send, inner_t)
-    there = swap(send, 2)
+    def add(cost, a, b):
+        out = struct(a.shape, F32)
+        return call(add_kernel, [VMEM] * 2, [VMEM], [out], [], 2, flops=cost)(a.astype(F32), b.astype(F32))[0].astype(F16)
+
+    mine, inner_t = together(send, inner_t)
+    there = swap(mine, 2)
     upsampled = fine(0, inner_t, None)
     there, upsampled = together(there, upsampled)
-    keep, send = call(
-        split_kernel,
-        [SMEM, VMEM, VMEM],
-        [VMEM] * 2,
-        [struct((wide // 2, 2 * chans), F32), struct((wide // 2 + TAIL, 2 * chans), F32)],
-        [pltpu.VMEM((wide, 2 * chans), F32)],
-        2,
-    )(bits, send.astype(F32), there.astype(F32))
-    send = send.astype(F16)
-    send, low, outer_t = together(send, low, outer_t)
-    mine = add(False, COSTS[6], keep, swap(send, 4).astype(F32))
+    mine = add(COSTS[8], mine, there)
+    mine, low, outer_t = together(mine, low, outer_t)
+    from_inner = swap(to_inner, 1)
+    mine = add(COSTS[6], mine, swap(mine, 4))
     mine, high, outer_t = together(mine, high.astype(F16), outer_t)
     there = swap(mine, 8)
     high = beyond(high)
     upsampled = fine(1, outer_t, upsampled)
-    mine = add(True, COSTS[7], mine.astype(F32), there.astype(F32))
+    there, upsampled = together(there, upsampled)
+    mine = add(COSTS[7], mine, there)
     for k in range(4, peers.bit_length() - 1):
-        mine = add(True, COSTS[7], mine.astype(F32), swap(mine, 1 << k).astype(F32))
-    mine, upsampled = together(mine, upsampled)
-    from_inner = swap(to_inner, 1)
-    there = swap(mine, 4)
-    other_mine = swap(mine, 1)
-    (volume_grad,) = call(cells_kernel, [VMEM] * 4, [VMEM], [cells], [], 4)(
-        vg, from_inner, low.astype(F32), high.astype(F32)
-    )
-    there, volume_grad = together(there, volume_grad)
-    other_there = swap(there, 1)
+        mine = add(COSTS[7], mine, swap(mine, 1 << k))
+    other = swap(mine, 1)
     scale = 1.0 / math.sqrt(peers * planes * ny * nz)
     (weight_grad,) = call(
         functools.partial(taps_kernel, scale),
-        [SMEM] + [VMEM] * 4,
+        [SMEM] + [VMEM] * 2,
         [HBM],
         [struct((4, wide, chans), F32)],
         [pltpu.VMEM((4, wide, chans), F32), pltpu.SemaphoreType.DMA((4,))],
         4,
-    )(bits, *(value.astype(F32) for value in (mine, there, other_mine, other_there)))
+    )(bits, mine.astype(F32), other.astype(F32))
+    high, weight_grad = together(high, weight_grad)
+    (volume_grad,) = call(cells_kernel, [VMEM] * 4, [VMEM], [cells], [], 4)(
+        vg, from_inner, low.astype(F32), high.astype(F32)
+    )
     weight_grad = jnp.transpose(weight_grad.reshape(4, 4, 4, dout, chans), (0, 1, 2, 4, 3))
     return (upsampled, volume_grad.reshape(volume.shape), weight_grad)
 

time: 47.7 us -> 46.6 us (0.977); the launches traced: 47.6 us -> 45.7 us
  starting transfers between devices: 10.2 us -> 15.3 us
  Pallas kernels: 23.3 us -> 18.4 us
  waiting for transfers between devices: 12.6 us -> 10.7 us
    ppermute x9 -> x7, starting transfers between devices: 3.67 us -> 8.8 us  [swap(): return lax.ppermute(value, 'gx', [(i, i ^ k) for i in range(peers)])]
    pallas_call x5, Pallas kernels: 7.62 us -> 5.64 us  [the longest x1 4.11 us: on_device(): call(inner_sums_kernel, [SMEM, VMEM, VMEM, VMEM], [VMEM] * 4, [struct(tap...]
    ppermute x3, waiting for transfers between devices: 2.72 us -> 0.82 us  [beyond(): lax.ppermute(value, 'gx', [(i, (i + (1 if i % 2 else -1)) % peers) for i...]
    pallas_call x1, Pallas kernels: 5.17 us -> 3.92 us  [on_device(): call(outer_kernel, [SMEM, HBM, HBM], [VMEM] * 4, [struct(taps_shape, BF16...]
    pallas_call x2, Pallas kernels: 6.29 us -> 5.21 us  [fine(): call(functools.partial(fine_kernel, which), [SMEM, VMEM, VMEM, VMEM] + [H...]
    pallas_call x1, Pallas kernels: 1.86 us -> 1.32 us  [on_device(): call(inner_cells_kernel, [SMEM, VMEM, VMEM, VMEM], [VMEM] * 2, [wide_cell...]
    ppermute x9 -> x7, waiting for transfers between devices: 9.92 us -> 9.88 us  [swap(): return lax.ppermute(value, 'gx', [(i, i ^ k) for i in range(peers)])]
  transfers between devices with their start and end apart: 12 -> 10, of which waited for: 5 -> 5; matrix products, arithmetic and copies ran while one was open for 1% -> 1% of each run, Pallas kernels for 45% -> 38%
where the time goes in v5:
time: 46.6 us; the launch traced here: 45.7 us
  Pallas kernels  18.4 us (39%)
  starting transfers between devices  15.3 us (33%)
  waiting for transfers between devices  10.7 us (23%)
  between operations  0.92 us (2%)
    ppermute x7, waiting for transfers between devices, swap(): return lax.ppermute(value, 'gx', [(i, i ^ k) for i in range(peers)])  9.88 us
    ppermute x7, starting transfers between devices, swap(): return lax.ppermute(value, 'gx', [(i, i ^ k) for i in range(peers)])  8.8 us
    ppermute x3, starting transfers between devices, beyond(): lax.ppermute(value, 'gx', [(i, (i + (1 if i % 2 else -1)) % peers) for i...  6.45 us
    pallas_call x2, Pallas kernels, fine(): call(functools.partial(fine_kernel, which), [SMEM, VMEM, VMEM, VMEM] + [H...  5.21 us
    pallas_call x1, Pallas kernels, on_device(): call(inner_sums_kernel, [SMEM, VMEM, VMEM, VMEM], [VMEM] * 4, [struct(tap...  4.11 us
    pallas_call x1, Pallas kernels, on_device(): call(outer_kernel, [SMEM, HBM, HBM], [VMEM] * 4, [struct(taps_shape, BF16...  3.92 us
    pallas_call x1, Pallas kernels, on_device(): call(outer_sums_kernel, [VMEM] * 4, [VMEM] * 2, [struct((wide + TAIL, 2 *...  1.4 us
    pallas_call x1, Pallas kernels, on_device(): call(inner_cells_kernel, [SMEM, VMEM, VMEM, VMEM], [VMEM] * 2, [wide_cell...  1.32 us
  transfers between devices with their start and end apart: 10, of which 5 were waited for; matrix products, arithmetic and copies ran while one was open for 1% of the time, Pallas kernels for 38%

profile of v5, /device:TPU:0, one launch (start us, length us, event | category | flops | bytes accessed | tf_op | source)
XLA Modules:
  0.0 45.7 jit_solution(3064989072774237270)
XLA Ops:
  0.6 0.5 %collective-permute-start = (bf16[512,512]{1,0:T(8,128)(2,1)}, bf16[512,512]{1,0:T(8,128)(2,1)}, u32[]{:S(2)}, u32[]{:S(2)}) collective-permute-start(bf16[512,512]{1,0:T(8,128)(2,1)} %bitcast.15), channel_id=1, source_target_pairs={{0,1},{1,0},{2,3},{3,2},{4,5},{5,4},{6,7},{7,6},{8,9},{9,8},{10,11... | collective-permute-start | bytes 1572872 | tf_op jit(solution)/shard_map/ppermute | solution.py:292
  1.2 5.6 %collective-permute-start.1 = (bf16[512,512]{1,0:T(8,128)(2,1)}, bf16[512,512]{1,0:T(8,128)(2,1)S(1)}, u32[]{:S(2)}, u32[]{:S(2)}) collective-permute-start(bf16[512,512]{1,0:T(8,128)(2,1)} %bitcast.16), channel_id=1, source_target_pairs={{0,15},{1,2},{2,1},{3,4},{4,3},{5,6},{6,5},{7,8},{8,7},{9,10},{10,... | collective-permute-start | bytes 1572872 | tf_op jit(solution)/shard_map/ppermute | solution.py:295
  6.8 3.9 %shard_map.58 = (bf16[2304,512]{1,0:T(8,128)(2,1)S(1)}, f32[512,512]{1,0:T(8,128)S(1)}, f32[208,512]{1,0:T(8,128)S(1)}, f32[336,512]{1,0:T(8,128)S(1)}) custom-call(s32[1]{0:T(128)} %bitcast.core_ref.bits_ref, bf16[32,2,16,1024]{3,2,1,0:T(8,128)(2,1)} %cot_ref.3, bf16[4,512,64]{2,1,0:T(8,128)(2,1)} %bitcast.11), custom_call_target="tpu_custom_call" | custom-call | flops 1000 | bytes 1000 | tf_op jit(solution)/shard_map/pallas_call | solution.py:302
  10.8 4.1 %shard_map.59 = (bf16[2304,512]{1,0:T(8,128)(2,1)S(1)}, bf16[512,512]{1,0:T(8,128)(2,1)S(1)}, bf16[512,512]{1,0:T(8,128)(2,1)S(1)}, f32[512,128]{1,0:T(8,128)S(1)}) custom-call(s32[1]{0:T(128)} %bitcast.core_ref.bits_ref, bf16[32,2,16,1024]{3,2,1,0:T(8,128)(2,1)S(1)} %copy-done, bf16[512,512]{1,0:T(8,128)(2,1)S(1)} %bitcast.17, ...), custom_call_target="tpu_custom_call" | custom-call | flops 1000 | bytes 1000 | tf_op jit(solution)/shard_map/pallas_call | solution.py:315
  14.9 0.1 collective-permute-start.2
  15.0 0.7 %collective-permute-start.4 = (f16[208,512]{1,0:T(8,128)(2,1)S(1)}, f16[208,512]{1,0:T(8,128)(2,1)S(1)}, u32[]{:S(2)}, u32[]{:S(2)}) collective-permute-start(f16[208,512]{1,0:T(8,128)(2,1)S(1)} %convert_element_type.48), channel_id=1, source_target_pairs={{0,15},{1,2},{2,1},{3,4},{4,3},{5,6},{6,5},{7,8},{8,7},{9,10},{10,... | collective-permute-start | bytes 638984 | tf_op jit(solution)/shard_map/ppermute | solution.py:295
  15.8 1.3 %shard_map.60 = (f32[512,512]{1,0:T(8,128)S(1)}, f32[512,512]{1,0:T(8,128)S(1)}) custom-call(s32[1]{0:T(128)} %bitcast.core_ref.bits_ref, bf16[2304,512]{1,0:T(8,128)(2,1)S(1)} %get-tuple-element.41.taps_ref, bf16[4,512,64]{2,1,0:T(8,128)(2,1)S(1)} %bitcast.12, f32[512,512]{1,0:T(8,128)S(1)} %get-tuple-element.42.vg_part_ref), custom_call_target="tpu_custom_call" | custom-call | flops 1000 | bytes 1000 | tf_op jit(solution)/shard_map/pallas_call | solution.py:327
  17.1 1.4 %shard_map.61 = (f32[528,128]{1,0:T(8,128)S(1)}, bf16[512,512]{1,0:T(8,128)(2,1)S(1)}) custom-call(bf16[2304,512]{1,0:T(8,128)(2,1)S(1)} %get-tuple-element.35.taps_ref, bf16[512,512]{1,0:T(8,128)(2,1)S(1)} %get-tuple-element.44.own_t_ref, bf16[512,512]{1,0:T(8,128)(2,1)S(1)} %collective-permute-done.1.outer_ref, ...), custom_call_target="tpu_custom_call" | custom-call | flops 1000 | bytes 1000 | tf_op jit(solution)/shard_map/pallas_call | solution.py:351
  18.5 3.4 %collective-permute-start.3 = (f16[528,128]{1,0:T(8,128)(2,1)S(1)}, f16[528,128]{1,0:T(8,128)(2,1)S(1)}, u32[]{:S(2)}, u32[]{:S(2)}) collective-permute-start(f16[528,128]{1,0:T(8,128)(2,1)S(1)} %convert_element_type.49), channel_id=1, source_target_pairs={{0,2},{1,3},{2,0},{3,1},{4,6},{5,7},{6,4},{7,5},{8,10},{9,11},{10,... | collective-permute-start | bytes 405512 | tf_op jit(solution)/shard_map/ppermute | solution.py:292
  22.0 2.6 %shard_map.62.refs_0_ = bf16[32,2,16,1024]{3,2,1,0:T(8,128)(2,1)} custom-call(s32[1]{0:T(128)} %bitcast.core_ref.bits_ref, bf16[512,512]{1,0:T(8,128)(2,1)S(1)} %get-tuple-element.44.own_t_ref, bf16[512,512]{1,0:T(8,128)(2,1)S(1)} %get-tuple-element.49.nbr_t_ref, bf16[4,512,64]{2,1,0:T(8,128)(2,1)S(1)} %bitcast.13), custom_call_target="tpu_custom_call" | custom-call | flops 1000 | bytes 1000 | tf_op jit(solution)/shard_map/pallas_call | solution.py:339
  24.6 1.6 %collective-permute-done.3 = f16[528,128]{1,0:T(8,128)(2,1)S(1)} collective-permute-done((f16[528,128]{1,0:T(8,128)(2,1)S(1)}, f16[528,128]{1,0:T(8,128)(2,1)S(1)}, u32[]{:S(2)}, u32[]{:S(2)}) %collective-permute-start.3) | collective-permute-done | bytes 135200 | tf_op jit(solution)/shard_map/ppermute | solution.py:292
  26.2 0.2 shard_map.63
  26.4 1.8 %collective-permute-start.5 = (f16[528,128]{1,0:T(8,128)(2,1)S(1)}, f16[528,128]{1,0:T(8,128)(2,1)S(1)}, u32[]{:S(2)}, u32[]{:S(2)}) collective-permute-start(f16[528,128]{1,0:T(8,128)(2,1)S(1)} %convert_element_type.52), channel_id=1, source_target_pairs={{0,4},{1,5},{2,6},{3,7},{4,0},{5,1},{6,2},{7,3},{8,12},{9,13},{10,... | collective-permute-start | bytes 405512 | tf_op jit(solution)/shard_map/ppermute | solution.py:292
  28.4 3.7 %collective-permute-done.5 = f16[528,128]{1,0:T(8,128)(2,1)S(1)} collective-permute-done((f16[528,128]{1,0:T(8,128)(2,1)S(1)}, f16[528,128]{1,0:T(8,128)(2,1)S(1)}, u32[]{:S(2)}, u32[]{:S(2)}) %collective-permute-start.5) | collective-permute-done | bytes 135200 | tf_op jit(solution)/shard_map/ppermute | solution.py:292
  32.1 0.2 shard_map.64
  32.3 2.8 %collective-permute-start.6 = (f16[528,128]{1,0:T(8,128)(2,1)S(1)}, f16[528,128]{1,0:T(8,128)(2,1)S(1)}, u32[]{:S(2)}, u32[]{:S(2)}) collective-permute-start(f16[528,128]{1,0:T(8,128)(2,1)S(1)} %convert_element_type.55), channel_id=1, source_target_pairs={{0,8},{1,9},{2,10},{3,11},{4,12},{5,13},{6,14},{7,15},{8,0},{9,1},... | collective-permute-start | bytes 405512 | tf_op jit(solution)/shard_map/ppermute | solution.py:292
  35.2 2.6 %shard_map.65 = bf16[32,2,16,1024]{3,2,1,0:T(8,128)(2,1)} custom-call(s32[1]{0:T(128)} %bitcast.core_ref.bits_ref, bf16[512,512]{1,0:T(8,128)(2,1)S(1)} %get-tuple-element.44.own_t_ref, bf16[512,512]{1,0:T(8,128)(2,1)S(1)} %get-tuple-element.57.nbr_t_ref, bf16[4,512,64]{2,1,0:T(8,128)(2,1)S(1)} %bitcast.14, ...), custom_call_target="tpu_custom_call", output_to_operand_aliasing={{}: (4, {})} | custom-call | flops 1000 | bytes 1000 | tf_op jit(solution)/shard_map/pallas_call | solution.py:339
  37.9 3.3 %collective-permute-done.6 = f16[528,128]{1,0:T(8,128)(2,1)S(1)} collective-permute-done((f16[528,128]{1,0:T(8,128)(2,1)S(1)}, f16[528,128]{1,0:T(8,128)(2,1)S(1)}, u32[]{:S(2)}, u32[]{:S(2)}) %collective-permute-start.6) | collective-permute-done | bytes 135200 | tf_op jit(solution)/shard_map/ppermute | solution.py:292
  41.2 0.2 shard_map.66
  41.5 1.3 %collective-permute-done.9 = f16[528,128]{1,0:T(8,128)(2,1)S(1)} collective-permute-done((f16[528,128]{1,0:T(8,128)(2,1)S(1)}, f16[528,128]{1,0:T(8,128)(2,1)S(1)}, u32[]{:S(2)}, u32[]{:S(2)}) %collective-permute-start.9) | collective-permute-done | bytes 135200 | tf_op jit(solution)/shard_map/ppermute | solution.py:292
  42.8 1.1 %shard_map.67 = f32[4,512,64]{2,1,0:T(8,128)} custom-call(s32[1]{0:T(128)} %bitcast.core_ref.bits_ref, f32[528,128]{1,0:T(8,128)S(1)} %get-tuple-element.70.mine_ref, f32[528,128]{1,0:T(8,128)S(1)} %convert_element_type.62.other_ref), custom_call_target="tpu_custom_call" | custom-call | flops 1000 | bytes 1000 | tf_op jit(solution)/shard_map/pallas_call | solution.py:384
  43.9 0.8 %collective-permute-done.8 = f16[336,512]{1,0:T(8,128)(2,1)S(1)} collective-permute-done((f16[336,512]{1,0:T(8,128)(2,1)S(1)}, f16[336,512]{1,0:T(8,128)(2,1)S(1)}, u32[]{:S(2)}, u32[]{:S(2)}) %collective-permute-start.8) | collective-permute-done | bytes 344096 | tf_op jit(solution)/shard_map/ppermute | solution.py:295
  44.7 0.1 convert_element_type.63.high_ref
  44.8 0.9 %shard_map.68 = bf16[512,512]{1,0:T(8,128)(2,1)} custom-call(f32[512,512]{1,0:T(8,128)S(1)} %get-tuple-element.60.vg_ref, f32[512,512]{1,0:T(8,128)S(1)} %collective-permute-done.7.inner_ref, f32[208,512]{1,0:T(8,128)S(1)} %convert_element_type.57.low_ref, f32[336,512]{1,0:T(8,128)S(1)} %convert_element_type.63.high_ref), custom_call_target="tpu_custom_call" | custom-call | flops 1000 | bytes 1000 | tf_op jit(solution)/shard_map/pallas_call | solution.py:393
  (28 shorter events, 0.6 us)
Async XLA Ops:
  0.6 10.1 %copy-start.2 = (bf16[64,1,8,512]{3,2,1,0:T(8,128)(2,1)S(1)}, bf16[64,1,8,512]{3,2,1,0:T(8,128)(2,1)}, u32[]{:S(2)}) copy-start(bf16[64,1,8,512]{3,2,1,0:T(8,128)(2,1)} %param.3) | copy-start | bytes 1572868
  0.6 10.1 %copy-start = (bf16[32,2,16,1024]{3,2,1,0:T(8,128)(2,1)S(1)}, bf16[32,2,16,1024]{3,2,1,0:T(8,128)(2,1)}, u32[]{:S(2)}) copy-start(bf16[32,2,16,1024]{3,2,1,0:T(8,128)(2,1)} %cot_ref.3) | copy-start | bytes 6291460
  0.6 10.1 %collective-permute-start = (bf16[512,512]{1,0:T(8,128)(2,1)}, bf16[512,512]{1,0:T(8,128)(2,1)}, u32[]{:S(2)}, u32[]{:S(2)}) collective-permute-start(bf16[512,512]{1,0:T(8,128)(2,1)} %bitcast.15), channel_id=1, source_target_pairs={{0,1},{1,0},{2,3},{3,2},{4,5},{5,4},{6,7},{7,6},{8,9},{9,8},{10,11... | collective-permute-start | bytes 1572872 | tf_op jit(solution)/shard_map/ppermute | solution.py:292
  1.2 15.9 %collective-permute-start.1 = (bf16[512,512]{1,0:T(8,128)(2,1)}, bf16[512,512]{1,0:T(8,128)(2,1)S(1)}, u32[]{:S(2)}, u32[]{:S(2)}) collective-permute-start(bf16[512,512]{1,0:T(8,128)(2,1)} %bitcast.16), channel_id=1, source_target_pairs={{0,15},{1,2},{2,1},{3,4},{4,3},{5,6},{6,5},{7,8},{8,7},{9,10},{10,... | collective-permute-start | bytes 1572872 | tf_op jit(solution)/shard_map/ppermute | solution.py:295
  10.7 5.0 %copy-start.1 = (bf16[4,4,4,64,32]{3,4,2,1,0:T(8,128)(2,1)S(1)}, bf16[4,4,4,64,32]{3,4,2,1,0:T(8,128)(2,1)}, u32[]{:S(2)}) copy-start(bf16[4,4,4,64,32]{3,4,2,1,0:T(8,128)(2,1)} %param.4) | copy-start | bytes 786436
  14.9 2.2 %collective-permute-start.2 = (f32[512,128]{1,0:T(8,128)S(1)}, f32[512,128]{1,0:T(8,128)S(1)}, u32[]{:S(2)}, u32[]{:S(2)}) collective-permute-start(f32[512,128]{1,0:T(8,128)S(1)} %get-tuple-element.45), channel_id=1, source_target_pairs={{0,1},{1,0},{2,3},{3,2},{4,5},{5,4},{6,7},{7,6},{8,9},{9,8},{10,11... | collective-permute-start | bytes 786440 | tf_op jit(solution)/shard_map/ppermute | solution.py:292
  15.0 11.4 %collective-permute-start.4 = (f16[208,512]{1,0:T(8,128)(2,1)S(1)}, f16[208,512]{1,0:T(8,128)(2,1)S(1)}, u32[]{:S(2)}, u32[]{:S(2)}) collective-permute-start(f16[208,512]{1,0:T(8,128)(2,1)S(1)} %convert_element_type.48), channel_id=1, source_target_pairs={{0,15},{1,2},{2,1},{3,4},{4,3},{5,6},{6,5},{7,8},{8,7},{9,10},{10,... | collective-permute-start | bytes 638984 | tf_op jit(solution)/shard_map/ppermute | solution.py:295
  18.5 7.7 %collective-permute-start.3 = (f16[528,128]{1,0:T(8,128)(2,1)S(1)}, f16[528,128]{1,0:T(8,128)(2,1)S(1)}, u32[]{:S(2)}, u32[]{:S(2)}) collective-permute-start(f16[528,128]{1,0:T(8,128)(2,1)S(1)} %convert_element_type.49), channel_id=1, source_target_pairs={{0,2},{1,3},{2,0},{3,1},{4,6},{5,7},{6,4},{7,5},{8,10},{9,11},{10,... | collective-permute-start | bytes 405512 | tf_op jit(solution)/shard_map/ppermute | solution.py:292
  26.4 5.7 %collective-permute-start.5 = (f16[528,128]{1,0:T(8,128)(2,1)S(1)}, f16[528,128]{1,0:T(8,128)(2,1)S(1)}, u32[]{:S(2)}, u32[]{:S(2)}) collective-permute-start(f16[528,128]{1,0:T(8,128)(2,1)S(1)} %convert_element_type.52), channel_id=1, source_target_pairs={{0,4},{1,5},{2,6},{3,7},{4,0},{5,1},{6,2},{7,3},{8,12},{9,13},{10,... | collective-permute-start | bytes 405512 | tf_op jit(solution)/shard_map/ppermute | solution.py:292
  28.3 16.5 %collective-permute-start.7 = (f32[512,512]{1,0:T(8,128)S(1)}, f32[512,512]{1,0:T(8,128)S(1)}, u32[]{:S(2)}, u32[]{:S(2)}) collective-permute-start(f32[512,512]{1,0:T(8,128)S(1)} %get-tuple-element.61), channel_id=1, source_target_pairs={{0,1},{1,0},{2,3},{3,2},{4,5},{5,4},{6,7},{7,6},{8,9},{9,8},{10,11... | collective-permute-start | bytes 3145736 | tf_op jit(solution)/shard_map/ppermute | solution.py:292
  32.3 8.8 %collective-permute-start.6 = (f16[528,128]{1,0:T(8,128)(2,1)S(1)}, f16[528,128]{1,0:T(8,128)(2,1)S(1)}, u32[]{:S(2)}, u32[]{:S(2)}) collective-permute-start(f16[528,128]{1,0:T(8,128)(2,1)S(1)} %convert_element_type.55), channel_id=1, source_target_pairs={{0,8},{1,9},{2,10},{3,11},{4,12},{5,13},{6,14},{7,15},{8,0},{9,1},... | collective-permute-start | bytes 405512 | tf_op jit(solution)/shard_map/ppermute | solution.py:292
  35.2 9.5 %collective-permute-start.8 = (f16[336,512]{1,0:T(8,128)(2,1)S(1)}, f16[336,512]{1,0:T(8,128)(2,1)S(1)}, u32[]{:S(2)}, u32[]{:S(2)}) collective-permute-start(f16[336,512]{1,0:T(8,128)(2,1)S(1)} %convert_element_type.56), channel_id=1, source_target_pairs={{0,15},{1,2},{2,1},{3,4},{4,3},{5,6},{6,5},{7,8},{8,7},{9,10},{10,... | collective-permute-start | bytes 1032200 | tf_op jit(solution)/shard_map/ppermute | solution.py:295
  41.4 1.4 %collective-permute-start.9 = (f16[528,128]{1,0:T(8,128)(2,1)S(1)}, f16[528,128]{1,0:T(8,128)(2,1)S(1)}, u32[]{:S(2)}, u32[]{:S(2)}) collective-permute-start(f16[528,128]{1,0:T(8,128)(2,1)S(1)} %get-tuple-element.71), channel_id=1, source_target_pairs={{0,1},{1,0},{2,3},{3,2},{4,5},{5,4},{6,7},{7,6},{8,9},{9,8},{10,11... | collective-permute-start | bytes 405512 | tf_op jit(solution)/shard_map/ppermute | solution.py:292

commit v6 on v5

--- a/solution.py
+++ b/solution.py
@@ -14,7 +14,7 @@
 NT = (((1,), (1,)), ((), ()))
 TOP = 14.0
 TAIL = 16
-COSTS = (1_000, 1_000, 1_000, 1_000, 1_000, 1_000, 8_000_000_000, 2_000_000_000, 1_000)
+COSTS = (1_000, 1_000, 1_000, 1_000, 1_000, 1_000, 1_000, 1_000, 8_000_000_000)
 
 
 def roles(core):
@@ -112,7 +112,7 @@
 
 
 def outer_kernel(
-    core_ref, cot_ref, w_hbm_ref, taps_ref, vg_ref, low_ref, high_ref,
+    core_ref, cot_ref, w_hbm_ref, taps_ref, vg_ref, partial_ref,
     plane_ref, even_ref, odd_ref, vg_blocks, partial_blocks, w_ref, sems,
 ):
     dout, _, ny2, _ = cot_ref.shape
@@ -139,13 +139,10 @@
     flatten(vg_blocks, vg_ref)
     level = level_of(jnp.max(most, axis=0, keepdims=True))
     shrink = jnp.exp2(TOP - level)
-    start = 0
-    for ref in (low_ref, high_ref):
-        count = ref.shape[0] - TAIL
-        for b in range(partial_blocks.shape[0]):
-            ref[:count, 128 * b : 128 * b + 128] = partial_blocks[b, start : start + count, :] * shrink
-        ref[count:, :] = jnp.broadcast_to(level, (TAIL, ref.shape[1]))
-        start += count
+    rows = chans * ny
+    for b in range(partial_blocks.shape[0]):
+        partial_ref[:rows, 128 * b : 128 * b + 128] = partial_blocks[b] * shrink
+    partial_ref[rows:, :] = jnp.broadcast_to(level, (TAIL, partial_ref.shape[1]))
 
 
 def tap_sums(taps_ref, own_t_ref, nbr_t_ref, sum_ref, before_ref):
@@ -209,10 +206,8 @@
         copy.wait()
 
 
-def cells_kernel(vg_ref, inner_ref, low_ref, high_ref, out_ref):
-    count = low_ref.shape[0] - TAIL
-    for at, ref in ((slice(0, count), low_ref), (slice(count, None), high_ref)):
-        out_ref[at, :] = (vg_ref[at, :] + inner_ref[at, :] + grown(ref)).astype(BF16)
+def cells_kernel(vg_ref, inner_ref, outer_ref, out_ref):
+    out_ref[...] = (vg_ref[...] + inner_ref[...] + grown(outer_ref)).astype(BF16)
 
 
 def fine_kernel(which, core_ref, own_t_ref, nbr_t_ref, w_ref, *refs):
@@ -281,7 +276,6 @@
     bits = (me & 1).astype(jnp.int32).reshape(1)
     rows, wide, group = chans * ny, 16 * dout, 4 * dout
     struct = jax.ShapeDtypeStruct
-    early = rows // 512 * 16 * 12
     blocks_c, blocks_d = (nz // 128, rows, 128), (nz // 128, dout * 2 * ny, 128)
     taps_shape, plane_shape = ((2 * ny + 2) * group, nz), (dout, 2 * ny, 2 * nz)
     cells, wide_cells = struct((rows, nz), BF16), struct((rows, nz), F32)
@@ -299,11 +293,11 @@
     inner = swap(own, 1)
     kernels = jnp.transpose(weights, (0, 1, 2, 4, 3)).reshape(4, wide, chans)
 
-    taps_o, vg_o, low, high = call(
+    taps_o, vg_o, low = call(
         outer_kernel,
         [SMEM, HBM, HBM],
-        [VMEM] * 4,
-        [struct(taps_shape, BF16), wide_cells] + [struct((part + TAIL, nz), F32) for part in (early, rows - early)],
+        [VMEM] * 3,
+        [struct(taps_shape, BF16), wide_cells] + [struct((rows + TAIL, nz), F32)],
         [pltpu.VMEM((dout, 1, 2 * ny, 2 * nz), BF16)] + work[1:]
         + [pltpu.VMEM(blocks_c, F32), pltpu.VMEM(blocks_c, F32), pltpu.VMEM(kernels.shape, BF16), pltpu.SemaphoreType.DMA((5,))],
         10,
@@ -364,18 +358,18 @@
         return call(add_kernel, [VMEM] * 2, [VMEM], [out], [], 2, flops=cost)(a.astype(F32), b.astype(F32))[0].astype(F16)
 
     mine, inner_t = together(send, inner_t)
-    there = swap(mine, 2)
+    there = swap(mine, 4)
     upsampled = fine(0, inner_t, None)
     there, upsampled = together(there, upsampled)
-    mine = add(COSTS[8], mine, there)
+    mine = add(COSTS[6], mine, there)
     mine, low, outer_t = together(mine, low, outer_t)
     from_inner = swap(to_inner, 1)
-    mine = add(COSTS[6], mine, swap(mine, 4))
-    mine, high, outer_t = together(mine, high.astype(F16), outer_t)
+    mine = add(COSTS[8], mine, swap(mine, 2))
+    mine, outer_t, low, from_inner = together(mine, outer_t, low, from_inner)
     there = swap(mine, 8)
-    high = beyond(high)
     upsampled = fine(1, outer_t, upsampled)
-    there, upsampled = together(there, upsampled)
+    (volume_grad,) = call(cells_kernel, [VMEM] * 3, [VMEM], [cells], [], 4)(vg, from_inner, low.astype(F32))
+    there, upsampled, volume_grad = together(there, upsampled, volume_grad)
     mine = add(COSTS[7], mine, there)
     for k in range(4, peers.bit_length() - 1):
         mine = add(COSTS[7], mine, swap(mine, 1 << k))
@@ -389,10 +383,6 @@
         [pltpu.VMEM((4, wide, chans), F32), pltpu.SemaphoreType.DMA((4,))],
         4,
     )(bits, mine.astype(F32), other.astype(F32))
-    high, weight_grad = together(high, weight_grad)
-    (volume_grad,) = call(cells_kernel, [VMEM] * 4, [VMEM], [cells], [], 4)(
-        vg, from_inner, low.astype(F32), high.astype(F32)
-    )
     weight_grad = jnp.transpose(weight_grad.reshape(4, 4, 4, dout, chans), (0, 1, 2, 4, 3))
     return (upsampled, volume_grad.reshape(volume.shape), weight_grad)
 

time: 46.6 us -> 46.3 us (level); the launches traced: 45.7 us -> 46.1 us
  waiting for transfers between devices: 10.7 us -> 12.5 us
  starting transfers between devices: 15.3 us -> 14.6 us
  Pallas kernels: 18.4 us -> 17.7 us
    ppermute x3 -> x2, waiting for transfers between devices: 0.82 us -> 2.91 us  [beyond(): lax.ppermute(value, 'gx', [(i, (i + (1 if i % 2 else -1)) % peers) for i...]
    pallas_call x1, Pallas kernels: 4.11 us -> 3.07 us  [on_device(): call(inner_sums_kernel, [SMEM, VMEM, VMEM, VMEM], [VMEM] * 4, [struct(tap...]
    ppermute x3 -> x2, starting transfers between devices: 6.45 us -> 5.71 us  [beyond(): lax.ppermute(value, 'gx', [(i, (i + (1 if i % 2 else -1)) % peers) for i...]
  transfers between devices with their start and end apart: 10 -> 9, of which waited for: 5 -> 5; matrix products, arithmetic and copies ran while one was open for 1% -> 1% of each run, Pallas kernels for 38% -> 36%
where the time goes in v6:
time: 46.3 us; the launch traced here: 46.1 us
  Pallas kernels  17.7 us (38%)
  starting transfers between devices  14.6 us (32%)
  waiting for transfers between devices  12.5 us (27%)
  between operations  0.86 us (2%)
  other arithmetic  0.47 us (1%)
    ppermute x7, waiting for transfers between devices, swap(): return lax.ppermute(value, 'gx', [(i, i ^ k) for i in range(peers)])  9.6 us
    ppermute x7, starting transfers between devices, swap(): return lax.ppermute(value, 'gx', [(i, i ^ k) for i in range(peers)])  8.88 us
    ppermute x2, starting transfers between devices, beyond(): lax.ppermute(value, 'gx', [(i, (i + (1 if i % 2 else -1)) % peers) for i...  5.71 us
    pallas_call x2, Pallas kernels, fine(): call(functools.partial(fine_kernel, which), [SMEM, VMEM, VMEM, VMEM] + [H...  5.2 us
    pallas_call x1, Pallas kernels, on_device(): call(outer_kernel, [SMEM, HBM, HBM], [VMEM] * 3, [struct(taps_shape, BF16...  4.08 us
    pallas_call x1, Pallas kernels, on_device(): call(inner_sums_kernel, [SMEM, VMEM, VMEM, VMEM], [VMEM] * 4, [struct(tap...  3.07 us
    ppermute x2, waiting for transfers between devices, beyond(): lax.ppermute(value, 'gx', [(i, (i + (1 if i % 2 else -1)) % peers) for i...  2.91 us
    pallas_call x1, Pallas kernels, on_device(): call(outer_sums_kernel, [VMEM] * 4, [VMEM] * 2, [struct((wide + TAIL, 2 *...  1.4 us
  transfers between devices with their start and end apart: 9, of which 5 were waited for; matrix products, arithmetic and copies ran while one was open for 1% of the time, Pallas kernels for 36%

profile of v6, /device:TPU:0, one launch (start us, length us, event | category | flops | bytes accessed | tf_op | source)
XLA Modules:
  0.0 46.1 jit_solution(17171779731631641271)
XLA Ops:
  0.6 0.5 %collective-permute-start = (bf16[512,512]{1,0:T(8,128)(2,1)}, bf16[512,512]{1,0:T(8,128)(2,1)S(1)}, u32[]{:S(2)}, u32[]{:S(2)}) collective-permute-start(bf16[512,512]{1,0:T(8,128)(2,1)} %bitcast.15), channel_id=1, source_target_pairs={{0,1},{1,0},{2,3},{3,2},{4,5},{5,4},{6,7},{7,6},{8,9},{9,8},{10,11... | collective-permute-start | bytes 1572872 | tf_op jit(solution)/shard_map/ppermute | solution.py:286
  1.1 5.6 %collective-permute-start.1 = (bf16[512,512]{1,0:T(8,128)(2,1)}, bf16[512,512]{1,0:T(8,128)(2,1)S(1)}, u32[]{:S(2)}, u32[]{:S(2)}) collective-permute-start(bf16[512,512]{1,0:T(8,128)(2,1)} %bitcast.16), channel_id=1, source_target_pairs={{0,15},{1,2},{2,1},{3,4},{4,3},{5,6},{6,5},{7,8},{8,7},{9,10},{10,... | collective-permute-start | bytes 1572872 | tf_op jit(solution)/shard_map/ppermute | solution.py:289
  6.8 4.1 %shard_map.58 = (bf16[2304,512]{1,0:T(8,128)(2,1)S(1)}, f32[512,512]{1,0:T(8,128)S(1)}, f32[528,512]{1,0:T(8,128)S(1)}) custom-call(s32[1]{0:T(128)} %bitcast.core_ref.bits_ref, bf16[32,2,16,1024]{3,2,1,0:T(8,128)(2,1)} %cot_ref.3, bf16[4,512,64]{2,1,0:T(8,128)(2,1)} %bitcast.11), custom_call_target="tpu_custom_call" | custom-call | flops 1000 | bytes 1000 | tf_op jit(solution)/shard_map/pallas_call | solution.py:296
  10.9 0.1 convert_element_type.42
  11.0 3.1 %shard_map.59 = (bf16[2304,512]{1,0:T(8,128)(2,1)S(1)}, bf16[512,512]{1,0:T(8,128)(2,1)S(1)}, bf16[512,512]{1,0:T(8,128)(2,1)S(1)}, f32[512,128]{1,0:T(8,128)S(1)}) custom-call(s32[1]{0:T(128)} %bitcast.core_ref.bits_ref, bf16[32,2,16,1024]{3,2,1,0:T(8,128)(2,1)S(1)} %copy-done, bf16[512,512]{1,0:T(8,128)(2,1)S(1)} %bitcast.17, ...), custom_call_target="tpu_custom_call" | custom-call | flops 1000 | bytes 1000 | tf_op jit(solution)/shard_map/pallas_call | solution.py:309
  14.1 0.1 collective-permute-start.4
  14.3 1.3 %shard_map.60 = (f32[512,512]{1,0:T(8,128)S(1)}, f32[512,512]{1,0:T(8,128)S(1)}) custom-call(s32[1]{0:T(128)} %bitcast.core_ref.bits_ref, bf16[2304,512]{1,0:T(8,128)(2,1)S(1)} %get-tuple-element.40.taps_ref, bf16[4,512,64]{2,1,0:T(8,128)(2,1)S(1)} %bitcast.12, f32[512,512]{1,0:T(8,128)S(1)} %get-tuple-element.41.vg_part_ref), custom_call_target="tpu_custom_call" | custom-call | flops 1000 | bytes 1000 | tf_op jit(solution)/shard_map/pallas_call | solution.py:321
  15.6 0.6 %collective-permute-start.6 = (f32[512,512]{1,0:T(8,128)S(1)}, f32[512,512]{1,0:T(8,128)S(1)}, u32[]{:S(2)}, u32[]{:S(2)}) collective-permute-start(f32[512,512]{1,0:T(8,128)S(1)} %get-tuple-element.55), channel_id=1, source_target_pairs={{0,1},{1,0},{2,3},{3,2},{4,5},{5,4},{6,7},{7,6},{8,9},{9,8},{10,11... | collective-permute-start | bytes 3145736 | tf_op jit(solution)/shard_map/ppermute | solution.py:286
  16.2 1.4 %shard_map.61 = (f32[528,128]{1,0:T(8,128)S(1)}, bf16[512,512]{1,0:T(8,128)(2,1)S(1)}) custom-call(bf16[2304,512]{1,0:T(8,128)(2,1)S(1)} %get-tuple-element.34.taps_ref, bf16[512,512]{1,0:T(8,128)(2,1)S(1)} %get-tuple-element.43.own_t_ref, bf16[512,512]{1,0:T(8,128)(2,1)S(1)} %collective-permute-done.1.outer_ref, ...), custom_call_target="tpu_custom_call" | custom-call | flops 1000 | bytes 1000 | tf_op jit(solution)/shard_map/pallas_call | solution.py:345
  17.7 2.6 %shard_map.62.refs_0_ = bf16[32,2,16,1024]{3,2,1,0:T(8,128)(2,1)} custom-call(s32[1]{0:T(128)} %bitcast.core_ref.bits_ref, bf16[512,512]{1,0:T(8,128)(2,1)S(1)} %get-tuple-element.43.own_t_ref, bf16[512,512]{1,0:T(8,128)(2,1)S(1)} %get-tuple-element.48.nbr_t_ref, bf16[4,512,64]{2,1,0:T(8,128)(2,1)S(1)} %bitcast.13), custom_call_target="tpu_custom_call" | custom-call | flops 1000 | bytes 1000 | tf_op jit(solution)/shard_map/pallas_call | solution.py:333
  20.3 2.3 %collective-permute-done.3 = f16[528,128]{1,0:T(8,128)(2,1)S(1)} collective-permute-done((f16[528,128]{1,0:T(8,128)(2,1)S(1)}, f16[528,128]{1,0:T(8,128)(2,1)S(1)}, u32[]{:S(2)}, u32[]{:S(2)}) %collective-permute-start.3) | collective-permute-done | bytes 135200 | tf_op jit(solution)/shard_map/ppermute | solution.py:286
  22.7 0.2 shard_map.63
  22.9 2.9 %collective-permute-done.4 = f16[528,512]{1,0:T(8,128)(2,1)S(1)} collective-permute-done((f16[528,512]{1,0:T(8,128)(2,1)S(1)}, f16[528,512]{1,0:T(8,128)(2,1)S(1)}, u32[]{:S(2)}, u32[]{:S(2)}) %collective-permute-start.4) | collective-permute-done | bytes 540704 | tf_op jit(solution)/shard_map/ppermute | solution.py:289
  25.8 4.9 %collective-permute-start.5 = (f16[528,128]{1,0:T(8,128)(2,1)S(1)}, f16[528,128]{1,0:T(8,128)(2,1)S(1)}, u32[]{:S(2)}, u32[]{:S(2)}) collective-permute-start(f16[528,128]{1,0:T(8,128)(2,1)S(1)} %convert_element_type.46), channel_id=1, source_target_pairs={{0,2},{1,3},{2,0},{3,1},{4,6},{5,7},{6,4},{7,5},{8,10},{9,11},{10,... | collective-permute-start | bytes 405512 | tf_op jit(solution)/shard_map/ppermute | solution.py:286
  30.8 3.6 %collective-permute-done.5 = f16[528,128]{1,0:T(8,128)(2,1)S(1)} collective-permute-done((f16[528,128]{1,0:T(8,128)(2,1)S(1)}, f16[528,128]{1,0:T(8,128)(2,1)S(1)}, u32[]{:S(2)}, u32[]{:S(2)}) %collective-permute-start.5) | collective-permute-done | bytes 135200 | tf_op jit(solution)/shard_map/ppermute | solution.py:286
  34.5 0.2 shard_map.64
  34.7 2.6 %collective-permute-start.7 = (f16[528,128]{1,0:T(8,128)(2,1)S(1)}, f16[528,128]{1,0:T(8,128)(2,1)S(1)}, u32[]{:S(2)}, u32[]{:S(2)}) collective-permute-start(f16[528,128]{1,0:T(8,128)(2,1)S(1)} %convert_element_type.49), channel_id=1, source_target_pairs={{0,8},{1,9},{2,10},{3,11},{4,12},{5,13},{6,14},{7,15},{8,0},{9,1},... | collective-permute-start | bytes 405512 | tf_op jit(solution)/shard_map/ppermute | solution.py:286
  37.3 2.6 %shard_map.65 = bf16[32,2,16,1024]{3,2,1,0:T(8,128)(2,1)} custom-call(s32[1]{0:T(128)} %bitcast.core_ref.bits_ref, bf16[512,512]{1,0:T(8,128)(2,1)S(1)} %get-tuple-element.43.own_t_ref, bf16[512,512]{1,0:T(8,128)(2,1)S(1)} %get-tuple-element.57.nbr_t_ref, bf16[4,512,64]{2,1,0:T(8,128)(2,1)S(1)} %bitcast.14, ...), custom_call_target="tpu_custom_call", output_to_operand_aliasing={{}: (4, {})} | custom-call | flops 1000 | bytes 1000 | tf_op jit(solution)/shard_map/pallas_call | solution.py:333
  39.9 0.1 convert_element_type.50.outer_ref
  40.0 1.1 %shard_map.66 = bf16[512,512]{1,0:T(8,128)(2,1)} custom-call(f32[512,512]{1,0:T(8,128)S(1)} %get-tuple-element.59.vg_ref, f32[512,512]{1,0:T(8,128)S(1)} %collective-permute-done.6.inner_ref, f32[528,512]{1,0:T(8,128)S(1)} %convert_element_type.50.outer_ref), custom_call_target="tpu_custom_call" | custom-call | flops 1000 | bytes 1000 | tf_op jit(solution)/shard_map/pallas_call | solution.py:371
  41.1 2.3 %collective-permute-done.7 = f16[528,128]{1,0:T(8,128)(2,1)S(1)} collective-permute-done((f16[528,128]{1,0:T(8,128)(2,1)S(1)}, f16[528,128]{1,0:T(8,128)(2,1)S(1)}, u32[]{:S(2)}, u32[]{:S(2)}) %collective-permute-start.7) | collective-permute-done | bytes 135200 | tf_op jit(solution)/shard_map/ppermute | solution.py:286
  43.4 0.2 shard_map.67
  43.7 1.3 %collective-permute-done.8 = f16[528,128]{1,0:T(8,128)(2,1)S(1)} collective-permute-done((f16[528,128]{1,0:T(8,128)(2,1)S(1)}, f16[528,128]{1,0:T(8,128)(2,1)S(1)}, u32[]{:S(2)}, u32[]{:S(2)}) %collective-permute-start.8) | collective-permute-done | bytes 135200 | tf_op jit(solution)/shard_map/ppermute | solution.py:286
  45.1 1.1 %shard_map.68 = f32[4,512,64]{2,1,0:T(8,128)} custom-call(s32[1]{0:T(128)} %bitcast.core_ref.bits_ref, f32[528,128]{1,0:T(8,128)S(1)} %get-tuple-element.68.mine_ref, f32[528,128]{1,0:T(8,128)S(1)} %convert_element_type.55.other_ref), custom_call_target="tpu_custom_call" | custom-call | flops 1000 | bytes 1000 | tf_op jit(solution)/shard_map/pallas_call | solution.py:378
  (24 shorter events, 0.5 us)
Async XLA Ops:
  0.6 10.4 %collective-permute-start = (bf16[512,512]{1,0:T(8,128)(2,1)}, bf16[512,512]{1,0:T(8,128)(2,1)S(1)}, u32[]{:S(2)}, u32[]{:S(2)}) collective-permute-start(bf16[512,512]{1,0:T(8,128)(2,1)} %bitcast.15), channel_id=1, source_target_pairs={{0,1},{1,0},{2,3},{3,2},{4,5},{5,4},{6,7},{7,6},{8,9},{9,8},{10,11... | collective-permute-start | bytes 1572872 | tf_op jit(solution)/shard_map/ppermute | solution.py:286
  1.1 15.0 %collective-permute-start.1 = (bf16[512,512]{1,0:T(8,128)(2,1)}, bf16[512,512]{1,0:T(8,128)(2,1)S(1)}, u32[]{:S(2)}, u32[]{:S(2)}) collective-permute-start(bf16[512,512]{1,0:T(8,128)(2,1)} %bitcast.16), channel_id=1, source_target_pairs={{0,15},{1,2},{2,1},{3,4},{4,3},{5,6},{6,5},{7,8},{8,7},{9,10},{10,... | collective-permute-start | bytes 1572872 | tf_op jit(solution)/shard_map/ppermute | solution.py:289
  6.8 4.2 %copy-start = (bf16[32,2,16,1024]{3,2,1,0:T(8,128)(2,1)S(1)}, bf16[32,2,16,1024]{3,2,1,0:T(8,128)(2,1)}, u32[]{:S(2)}) copy-start(bf16[32,2,16,1024]{3,2,1,0:T(8,128)(2,1)} %cot_ref.3) | copy-start | bytes 6291460
  6.8 4.2 %copy-start.2 = (bf16[64,1,8,512]{3,2,1,0:T(8,128)(2,1)S(1)}, bf16[64,1,8,512]{3,2,1,0:T(8,128)(2,1)}, u32[]{:S(2)}) copy-start(bf16[64,1,8,512]{3,2,1,0:T(8,128)(2,1)} %param.3) | copy-start | bytes 1572868
  10.9 3.4 %copy-start.1 = (bf16[4,4,4,64,32]{3,4,2,1,0:T(8,128)(2,1)S(1)}, bf16[4,4,4,64,32]{3,4,2,1,0:T(8,128)(2,1)}, u32[]{:S(2)}) copy-start(bf16[4,4,4,64,32]{3,4,2,1,0:T(8,128)(2,1)} %param.4) | copy-start | bytes 786436
  14.1 11.7 %collective-permute-start.4 = (f16[528,512]{1,0:T(8,128)(2,1)S(1)}, f16[528,512]{1,0:T(8,128)(2,1)S(1)}, u32[]{:S(2)}, u32[]{:S(2)}) collective-permute-start(f16[528,512]{1,0:T(8,128)(2,1)S(1)} %convert_element_type.42), channel_id=1, source_target_pairs={{0,15},{1,2},{2,1},{3,4},{4,3},{5,6},{6,5},{7,8},{8,7},{9,10},{10,... | collective-permute-start | bytes 1622024 | tf_op jit(solution)/shard_map/ppermute | solution.py:289
  14.2 2.0 %collective-permute-start.2 = (f32[512,128]{1,0:T(8,128)S(1)}, f32[512,128]{1,0:T(8,128)S(1)}, u32[]{:S(2)}, u32[]{:S(2)}) collective-permute-start(f32[512,128]{1,0:T(8,128)S(1)} %get-tuple-element.44), channel_id=1, source_target_pairs={{0,1},{1,0},{2,3},{3,2},{4,5},{5,4},{6,7},{7,6},{8,9},{9,8},{10,11... | collective-permute-start | bytes 786440 | tf_op jit(solution)/shard_map/ppermute | solution.py:286
  15.6 19.0 %collective-permute-start.6 = (f32[512,512]{1,0:T(8,128)S(1)}, f32[512,512]{1,0:T(8,128)S(1)}, u32[]{:S(2)}, u32[]{:S(2)}) collective-permute-start(f32[512,512]{1,0:T(8,128)S(1)} %get-tuple-element.55), channel_id=1, source_target_pairs={{0,1},{1,0},{2,3},{3,2},{4,5},{5,4},{6,7},{7,6},{8,9},{9,8},{10,11... | collective-permute-start | bytes 3145736 | tf_op jit(solution)/shard_map/ppermute | solution.py:286
  17.6 5.1 %collective-permute-start.3 = (f16[528,128]{1,0:T(8,128)(2,1)S(1)}, f16[528,128]{1,0:T(8,128)(2,1)S(1)}, u32[]{:S(2)}, u32[]{:S(2)}) collective-permute-start(f16[528,128]{1,0:T(8,128)(2,1)S(1)} %convert_element_type.43), channel_id=1, source_target_pairs={{0,4},{1,5},{2,6},{3,7},{4,0},{5,1},{6,2},{7,3},{8,12},{9,13},{10,... | collective-permute-start | bytes 405512 | tf_op jit(solution)/shard_map/ppermute | solution.py:286
  25.8 8.6 %collective-permute-start.5 = (f16[528,128]{1,0:T(8,128)(2,1)S(1)}, f16[528,128]{1,0:T(8,128)(2,1)S(1)}, u32[]{:S(2)}, u32[]{:S(2)}) collective-permute-start(f16[528,128]{1,0:T(8,128)(2,1)S(1)} %convert_element_type.46), channel_id=1, source_target_pairs={{0,2},{1,3},{2,0},{3,1},{4,6},{5,7},{6,4},{7,5},{8,10},{9,11},{10,... | collective-permute-start | bytes 405512 | tf_op jit(solution)/shard_map/ppermute | solution.py:286
  34.7 8.7 %collective-permute-start.7 = (f16[528,128]{1,0:T(8,128)(2,1)S(1)}, f16[528,128]{1,0:T(8,128)(2,1)S(1)}, u32[]{:S(2)}, u32[]{:S(2)}) collective-permute-start(f16[528,128]{1,0:T(8,128)(2,1)S(1)} %convert_element_type.49), channel_id=1, source_target_pairs={{0,8},{1,9},{2,10},{3,11},{4,12},{5,13},{6,14},{7,15},{8,0},{9,1},... | collective-permute-start | bytes 405512 | tf_op jit(solution)/shard_map/ppermute | solution.py:286
  43.6 1.4 %collective-permute-start.8 = (f16[528,128]{1,0:T(8,128)(2,1)S(1)}, f16[528,128]{1,0:T(8,128)(2,1)S(1)}, u32[]{:S(2)}, u32[]{:S(2)}) collective-permute-start(f16[528,128]{1,0:T(8,128)(2,1)S(1)} %get-tuple-element.69), channel_id=1, source_target_pairs={{0,1},{1,0},{2,3},{3,2},{4,5},{5,4},{6,7},{7,6},{8,9},{9,8},{10,11... | collective-permute-start | bytes 405512 | tf_op jit(solution)/shard_map/ppermute | solution.py:286

commit v7 on v6

--- a/solution.py
+++ b/solution.py
@@ -364,12 +364,14 @@
     mine = add(COSTS[6], mine, there)
     mine, low, outer_t = together(mine, low, outer_t)
     from_inner = swap(to_inner, 1)
-    mine = add(COSTS[8], mine, swap(mine, 2))
-    mine, outer_t, low, from_inner = together(mine, outer_t, low, from_inner)
     there = swap(mine, 8)
     upsampled = fine(1, outer_t, upsampled)
+    there, upsampled = together(there, upsampled)
+    mine = add(COSTS[8], mine, there)
+    mine, low, from_inner = together(mine, low, from_inner)
+    there = swap(mine, 2)
     (volume_grad,) = call(cells_kernel, [VMEM] * 3, [VMEM], [cells], [], 4)(vg, from_inner, low.astype(F32))
-    there, upsampled, volume_grad = together(there, upsampled, volume_grad)
+    there, volume_grad = together(there, volume_grad)
     mine = add(COSTS[7], mine, there)
     for k in range(4, peers.bit_length() - 1):
         mine = add(COSTS[7], mine, swap(mine, 1 << k))

time: 46.3 us -> 44.2 us (0.955)
  starting transfers between devices: 14.6 us -> 11.8 us
  waiting for transfers between devices: 12.5 us -> 13.2 us
    ppermute x7, starting transfers between devices: 8.88 us -> 6.08 us  [swap(): return lax.ppermute(value, 'gx', [(i, i ^ k) for i in range(peers)])]
    ppermute x7, waiting for transfers between devices: 9.6 us -> 10.3 us  [swap(): return lax.ppermute(value, 'gx', [(i, i ^ k) for i in range(peers)])]
  transfers between devices with their start and end apart: 9 -> 9, of which waited for: 5 -> 5; matrix products, arithmetic and copies ran while one was open for 1% -> 1% of each run, Pallas kernels for 36% -> 37%
where the time goes in v7:
time: 44.2 us; the launch traced here: 44 us
  Pallas kernels  17.7 us (40%)
  waiting for transfers between devices  13.2 us (30%)
  starting transfers between devices  11.8 us (27%)
  between operations  0.86 us (2%)
  other arithmetic  0.48 us (1%)
    ppermute x7, waiting for transfers between devices, swap(): return lax.ppermute(value, 'gx', [(i, i ^ k) for i in range(peers)])  10.3 us
    ppermute x7, starting transfers between devices, swap(): return lax.ppermute(value, 'gx', [(i, i ^ k) for i in range(peers)])  6.08 us
    ppermute x2, starting transfers between devices, beyond(): lax.ppermute(value, 'gx', [(i, (i + (1 if i % 2 else -1)) % peers) for i...  5.71 us
    pallas_call x2, Pallas kernels, fine(): call(functools.partial(fine_kernel, which), [SMEM, VMEM, VMEM, VMEM] + [H...  5.2 us
    pallas_call x1, Pallas kernels, on_device(): call(outer_kernel, [SMEM, HBM, HBM], [VMEM] * 3, [struct(taps_shape, BF16...  4.08 us
    pallas_call x1, Pallas kernels, on_device(): call(inner_sums_kernel, [SMEM, VMEM, VMEM, VMEM], [VMEM] * 4, [struct(tap...  3.07 us
    ppermute x2, waiting for transfers between devices, beyond(): lax.ppermute(value, 'gx', [(i, (i + (1 if i % 2 else -1)) % peers) for i...  2.91 us
    pallas_call x1, Pallas kernels, on_device(): call(outer_sums_kernel, [VMEM] * 4, [VMEM] * 2, [struct((wide + TAIL, 2 *...  1.4 us
  transfers between devices with their start and end apart: 9, of which 5 were waited for; matrix products, arithmetic and copies ran while one was open for 1% of the time, Pallas kernels for 37%

profile of v7, /device:TPU:0, one launch (start us, length us, event | category | flops | bytes accessed | tf_op | source)
XLA Modules:
  0.0 44.0 jit_solution(16176148046871151003)
XLA Ops:
  0.6 0.5 %collective-permute-start = (bf16[512,512]{1,0:T(8,128)(2,1)}, bf16[512,512]{1,0:T(8,128)(2,1)S(1)}, u32[]{:S(2)}, u32[]{:S(2)}) collective-permute-start(bf16[512,512]{1,0:T(8,128)(2,1)} %bitcast.15), channel_id=1, source_target_pairs={{0,1},{1,0},{2,3},{3,2},{4,5},{5,4},{6,7},{7,6},{8,9},{9,8},{10,11... | collective-permute-start | bytes 1572872 | tf_op jit(solution)/shard_map/ppermute | solution.py:286
  1.1 5.6 %collective-permute-start.1 = (bf16[512,512]{1,0:T(8,128)(2,1)}, bf16[512,512]{1,0:T(8,128)(2,1)S(1)}, u32[]{:S(2)}, u32[]{:S(2)}) collective-permute-start(bf16[512,512]{1,0:T(8,128)(2,1)} %bitcast.16), channel_id=1, source_target_pairs={{0,15},{1,2},{2,1},{3,4},{4,3},{5,6},{6,5},{7,8},{8,7},{9,10},{10,... | collective-permute-start | bytes 1572872 | tf_op jit(solution)/shard_map/ppermute | solution.py:289
  6.8 4.1 %shard_map.58 = (bf16[2304,512]{1,0:T(8,128)(2,1)S(1)}, f32[512,512]{1,0:T(8,128)S(1)}, f32[528,512]{1,0:T(8,128)S(1)}) custom-call(s32[1]{0:T(128)} %bitcast.core_ref.bits_ref, bf16[32,2,16,1024]{3,2,1,0:T(8,128)(2,1)} %cot_ref.3, bf16[4,512,64]{2,1,0:T(8,128)(2,1)} %bitcast.11), custom_call_target="tpu_custom_call" | custom-call | flops 1000 | bytes 1000 | tf_op jit(solution)/shard_map/pallas_call | solution.py:296
  10.9 0.1 convert_element_type.42
  11.0 3.1 %shard_map.59 = (bf16[2304,512]{1,0:T(8,128)(2,1)S(1)}, bf16[512,512]{1,0:T(8,128)(2,1)S(1)}, bf16[512,512]{1,0:T(8,128)(2,1)S(1)}, f32[512,128]{1,0:T(8,128)S(1)}) custom-call(s32[1]{0:T(128)} %bitcast.core_ref.bits_ref, bf16[32,2,16,1024]{3,2,1,0:T(8,128)(2,1)S(1)} %copy-done, bf16[512,512]{1,0:T(8,128)(2,1)S(1)} %bitcast.17, ...), custom_call_target="tpu_custom_call" | custom-call | flops 1000 | bytes 1000 | tf_op jit(solution)/shard_map/pallas_call | solution.py:309
  14.1 0.1 collective-permute-start.4
  14.3 1.3 %shard_map.60 = (f32[512,512]{1,0:T(8,128)S(1)}, f32[512,512]{1,0:T(8,128)S(1)}) custom-call(s32[1]{0:T(128)} %bitcast.core_ref.bits_ref, bf16[2304,512]{1,0:T(8,128)(2,1)S(1)} %get-tuple-element.40.taps_ref, bf16[4,512,64]{2,1,0:T(8,128)(2,1)S(1)} %bitcast.12, f32[512,512]{1,0:T(8,128)S(1)} %get-tuple-element.41.vg_part_ref), custom_call_target="tpu_custom_call" | custom-call | flops 1000 | bytes 1000 | tf_op jit(solution)/shard_map/pallas_call | solution.py:321
  15.6 0.6 %collective-permute-start.6 = (f32[512,512]{1,0:T(8,128)S(1)}, f32[512,512]{1,0:T(8,128)S(1)}, u32[]{:S(2)}, u32[]{:S(2)}) collective-permute-start(f32[512,512]{1,0:T(8,128)S(1)} %get-tuple-element.58), channel_id=1, source_target_pairs={{0,1},{1,0},{2,3},{3,2},{4,5},{5,4},{6,7},{7,6},{8,9},{9,8},{10,11... | collective-permute-start | bytes 3145736 | tf_op jit(solution)/shard_map/ppermute | solution.py:286
  16.2 1.4 %shard_map.61 = (f32[528,128]{1,0:T(8,128)S(1)}, bf16[512,512]{1,0:T(8,128)(2,1)S(1)}) custom-call(bf16[2304,512]{1,0:T(8,128)(2,1)S(1)} %get-tuple-element.34.taps_ref, bf16[512,512]{1,0:T(8,128)(2,1)S(1)} %get-tuple-element.43.own_t_ref, bf16[512,512]{1,0:T(8,128)(2,1)S(1)} %collective-permute-done.1.outer_ref, ...), custom_call_target="tpu_custom_call" | custom-call | flops 1000 | bytes 1000 | tf_op jit(solution)/shard_map/pallas_call | solution.py:345
  17.7 2.6 %shard_map.62.refs_0_ = bf16[32,2,16,1024]{3,2,1,0:T(8,128)(2,1)} custom-call(s32[1]{0:T(128)} %bitcast.core_ref.bits_ref, bf16[512,512]{1,0:T(8,128)(2,1)S(1)} %get-tuple-element.43.own_t_ref, bf16[512,512]{1,0:T(8,128)(2,1)S(1)} %get-tuple-element.48.nbr_t_ref, bf16[4,512,64]{2,1,0:T(8,128)(2,1)S(1)} %bitcast.13), custom_call_target="tpu_custom_call" | custom-call | flops 1000 | bytes 1000 | tf_op jit(solution)/shard_map/pallas_call | solution.py:333
  20.3 2.3 %collective-permute-done.3 = f16[528,128]{1,0:T(8,128)(2,1)S(1)} collective-permute-done((f16[528,128]{1,0:T(8,128)(2,1)S(1)}, f16[528,128]{1,0:T(8,128)(2,1)S(1)}, u32[]{:S(2)}, u32[]{:S(2)}) %collective-permute-start.3) | collective-permute-done | bytes 135200 | tf_op jit(solution)/shard_map/ppermute | solution.py:286
  22.7 0.2 shard_map.63
  22.9 2.9 %collective-permute-done.4 = f16[528,512]{1,0:T(8,128)(2,1)S(1)} collective-permute-done((f16[528,512]{1,0:T(8,128)(2,1)S(1)}, f16[528,512]{1,0:T(8,128)(2,1)S(1)}, u32[]{:S(2)}, u32[]{:S(2)}) %collective-permute-start.4) | collective-permute-done | bytes 540704 | tf_op jit(solution)/shard_map/ppermute | solution.py:289
  25.8 2.6 %shard_map.64 = bf16[32,2,16,1024]{3,2,1,0:T(8,128)(2,1)} custom-call(s32[1]{0:T(128)} %bitcast.core_ref.bits_ref, bf16[512,512]{1,0:T(8,128)(2,1)S(1)} %get-tuple-element.43.own_t_ref, bf16[512,512]{1,0:T(8,128)(2,1)S(1)} %get-tuple-element.53.nbr_t_ref, bf16[4,512,64]{2,1,0:T(8,128)(2,1)S(1)} %bitcast.14, ...), custom_call_target="tpu_custom_call", output_to_operand_aliasing={{}: (4, {})} | custom-call | flops 1000 | bytes 1000 | tf_op jit(solution)/shard_map/pallas_call | solution.py:333
  28.4 4.2 %collective-permute-done.5 = f16[528,128]{1,0:T(8,128)(2,1)S(1)} collective-permute-done((f16[528,128]{1,0:T(8,128)(2,1)S(1)}, f16[528,128]{1,0:T(8,128)(2,1)S(1)}, u32[]{:S(2)}, u32[]{:S(2)}) %collective-permute-start.5) | collective-permute-done | bytes 135200 | tf_op jit(solution)/shard_map/ppermute | solution.py:286
  32.6 0.2 shard_map.65
  32.8 4.5 %collective-permute-start.7 = (f16[528,128]{1,0:T(8,128)(2,1)S(1)}, f16[528,128]{1,0:T(8,128)(2,1)S(1)}, u32[]{:S(2)}, u32[]{:S(2)}) collective-permute-start(f16[528,128]{1,0:T(8,128)(2,1)S(1)} %convert_element_type.49), channel_id=1, source_target_pairs={{0,2},{1,3},{2,0},{3,1},{4,6},{5,7},{6,4},{7,5},{8,10},{9,11},{10,... | collective-permute-start | bytes 405512 | tf_op jit(solution)/shard_map/ppermute | solution.py:286
  37.3 0.1 convert_element_type.50.outer_ref
  37.5 1.1 %shard_map.66 = bf16[512,512]{1,0:T(8,128)(2,1)} custom-call(f32[512,512]{1,0:T(8,128)S(1)} %get-tuple-element.60.vg_ref, f32[512,512]{1,0:T(8,128)S(1)} %collective-permute-done.6.inner_ref, f32[528,512]{1,0:T(8,128)S(1)} %convert_element_type.50.outer_ref), custom_call_target="tpu_custom_call" | custom-call | flops 1000 | bytes 1000 | tf_op jit(solution)/shard_map/pallas_call | solution.py:373
  38.6 2.7 %collective-permute-done.7 = f16[528,128]{1,0:T(8,128)(2,1)S(1)} collective-permute-done((f16[528,128]{1,0:T(8,128)(2,1)S(1)}, f16[528,128]{1,0:T(8,128)(2,1)S(1)}, u32[]{:S(2)}, u32[]{:S(2)}) %collective-permute-start.7) | collective-permute-done | bytes 135200 | tf_op jit(solution)/shard_map/ppermute | solution.py:286
  41.3 0.2 shard_map.67
  41.5 0.4 collective-permute-start.8
  41.9 1.1 %collective-permute-done.8 = f16[528,128]{1,0:T(8,128)(2,1)S(1)} collective-permute-done((f16[528,128]{1,0:T(8,128)(2,1)S(1)}, f16[528,128]{1,0:T(8,128)(2,1)S(1)}, u32[]{:S(2)}, u32[]{:S(2)}) %collective-permute-start.8) | collective-permute-done | bytes 135200 | tf_op jit(solution)/shard_map/ppermute | solution.py:286
  43.0 1.1 %shard_map.68 = f32[4,512,64]{2,1,0:T(8,128)} custom-call(s32[1]{0:T(128)} %bitcast.core_ref.bits_ref, f32[528,128]{1,0:T(8,128)S(1)} %get-tuple-element.68.mine_ref, f32[528,128]{1,0:T(8,128)S(1)} %convert_element_type.55.other_ref), custom_call_target="tpu_custom_call" | custom-call | flops 1000 | bytes 1000 | tf_op jit(solution)/shard_map/pallas_call | solution.py:380
  (24 shorter events, 0.4 us)
Async XLA Ops:
  0.6 10.4 %collective-permute-start = (bf16[512,512]{1,0:T(8,128)(2,1)}, bf16[512,512]{1,0:T(8,128)(2,1)S(1)}, u32[]{:S(2)}, u32[]{:S(2)}) collective-permute-start(bf16[512,512]{1,0:T(8,128)(2,1)} %bitcast.15), channel_id=1, source_target_pairs={{0,1},{1,0},{2,3},{3,2},{4,5},{5,4},{6,7},{7,6},{8,9},{9,8},{10,11... | collective-permute-start | bytes 1572872 | tf_op jit(solution)/shard_map/ppermute | solution.py:286
  1.1 15.0 %collective-permute-start.1 = (bf16[512,512]{1,0:T(8,128)(2,1)}, bf16[512,512]{1,0:T(8,128)(2,1)S(1)}, u32[]{:S(2)}, u32[]{:S(2)}) collective-permute-start(bf16[512,512]{1,0:T(8,128)(2,1)} %bitcast.16), channel_id=1, source_target_pairs={{0,15},{1,2},{2,1},{3,4},{4,3},{5,6},{6,5},{7,8},{8,7},{9,10},{10,... | collective-permute-start | bytes 1572872 | tf_op jit(solution)/shard_map/ppermute | solution.py:289
  6.8 4.2 %copy-start = (bf16[32,2,16,1024]{3,2,1,0:T(8,128)(2,1)S(1)}, bf16[32,2,16,1024]{3,2,1,0:T(8,128)(2,1)}, u32[]{:S(2)}) copy-start(bf16[32,2,16,1024]{3,2,1,0:T(8,128)(2,1)} %cot_ref.3) | copy-start | bytes 6291460
  6.8 4.2 %copy-start.2 = (bf16[64,1,8,512]{3,2,1,0:T(8,128)(2,1)S(1)}, bf16[64,1,8,512]{3,2,1,0:T(8,128)(2,1)}, u32[]{:S(2)}) copy-start(bf16[64,1,8,512]{3,2,1,0:T(8,128)(2,1)} %param.3) | copy-start | bytes 1572868
  10.9 3.4 %copy-start.1 = (bf16[4,4,4,64,32]{3,4,2,1,0:T(8,128)(2,1)S(1)}, bf16[4,4,4,64,32]{3,4,2,1,0:T(8,128)(2,1)}, u32[]{:S(2)}) copy-start(bf16[4,4,4,64,32]{3,4,2,1,0:T(8,128)(2,1)} %param.4) | copy-start | bytes 786436
  14.1 11.7 %collective-permute-start.4 = (f16[528,512]{1,0:T(8,128)(2,1)S(1)}, f16[528,512]{1,0:T(8,128)(2,1)S(1)}, u32[]{:S(2)}, u32[]{:S(2)}) collective-permute-start(f16[528,512]{1,0:T(8,128)(2,1)S(1)} %convert_element_type.42), channel_id=1, source_target_pairs={{0,15},{1,2},{2,1},{3,4},{4,3},{5,6},{6,5},{7,8},{8,7},{9,10},{10,... | collective-permute-start | bytes 1622024 | tf_op jit(solution)/shard_map/ppermute | solution.py:289
  14.2 2.0 %collective-permute-start.2 = (f32[512,128]{1,0:T(8,128)S(1)}, f32[512,128]{1,0:T(8,128)S(1)}, u32[]{:S(2)}, u32[]{:S(2)}) collective-permute-start(f32[512,128]{1,0:T(8,128)S(1)} %get-tuple-element.44), channel_id=1, source_target_pairs={{0,1},{1,0},{2,3},{3,2},{4,5},{5,4},{6,7},{7,6},{8,9},{9,8},{10,11... | collective-permute-start | bytes 786440 | tf_op jit(solution)/shard_map/ppermute | solution.py:286
  15.6 17.2 %collective-permute-start.6 = (f32[512,512]{1,0:T(8,128)S(1)}, f32[512,512]{1,0:T(8,128)S(1)}, u32[]{:S(2)}, u32[]{:S(2)}) collective-permute-start(f32[512,512]{1,0:T(8,128)S(1)} %get-tuple-element.58), channel_id=1, source_target_pairs={{0,1},{1,0},{2,3},{3,2},{4,5},{5,4},{6,7},{7,6},{8,9},{9,8},{10,11... | collective-permute-start | bytes 3145736 | tf_op jit(solution)/shard_map/ppermute | solution.py:286
  17.6 5.1 %collective-permute-start.3 = (f16[528,128]{1,0:T(8,128)(2,1)S(1)}, f16[528,128]{1,0:T(8,128)(2,1)S(1)}, u32[]{:S(2)}, u32[]{:S(2)}) collective-permute-start(f16[528,128]{1,0:T(8,128)(2,1)S(1)} %convert_element_type.43), channel_id=1, source_target_pairs={{0,4},{1,5},{2,6},{3,7},{4,0},{5,1},{6,2},{7,3},{8,12},{9,13},{10,... | collective-permute-start | bytes 405512 | tf_op jit(solution)/shard_map/ppermute | solution.py:286
  25.8 6.8 %collective-permute-start.5 = (f16[528,128]{1,0:T(8,128)(2,1)S(1)}, f16[528,128]{1,0:T(8,128)(2,1)S(1)}, u32[]{:S(2)}, u32[]{:S(2)}) collective-permute-start(f16[528,128]{1,0:T(8,128)(2,1)S(1)} %convert_element_type.46), channel_id=1, source_target_pairs={{0,8},{1,9},{2,10},{3,11},{4,12},{5,13},{6,14},{7,15},{8,0},{9,1},... | collective-permute-start | bytes 405512 | tf_op jit(solution)/shard_map/ppermute | solution.py:286
  32.8 8.5 %collective-permute-start.7 = (f16[528,128]{1,0:T(8,128)(2,1)S(1)}, f16[528,128]{1,0:T(8,128)(2,1)S(1)}, u32[]{:S(2)}, u32[]{:S(2)}) collective-permute-start(f16[528,128]{1,0:T(8,128)(2,1)S(1)} %convert_element_type.49), channel_id=1, source_target_pairs={{0,2},{1,3},{2,0},{3,1},{4,6},{5,7},{6,4},{7,5},{8,10},{9,11},{10,... | collective-permute-start | bytes 405512 | tf_op jit(solution)/shard_map/ppermute | solution.py:286
  41.5 1.4 %collective-permute-start.8 = (f16[528,128]{1,0:T(8,128)(2,1)S(1)}, f16[528,128]{1,0:T(8,128)(2,1)S(1)}, u32[]{:S(2)}, u32[]{:S(2)}) collective-permute-start(f16[528,128]{1,0:T(8,128)(2,1)S(1)} %get-tuple-element.69), channel_id=1, source_target_pairs={{0,1},{1,0},{2,3},{3,2},{4,5},{5,4},{6,7},{7,6},{8,9},{9,8},{10,11... | collective-permute-start | bytes 405512 | tf_op jit(solution)/shard_map/ppermute | solution.py:286
